TPU v7x, 256 devices: a whole 4x4x8 slice. The times are simulated.
256 devices in a mesh: edge: 16 (over x, y), tile: 16 (over z, core).
Axes of the slice: x: 4, y: 4, z: 8, core: 2. Of those that a mesh axis runs over, the one named last changes fastest.
Arguments:
- features: bfloat16 [384, 48, 64, 128], P('edge', 'tile'), may hold values from -6 to 6
- hidden_state: bfloat16 [128, 48, 64, 128], P('edge', 'tile'), may hold values from -1 to 1
- edge_source: int32 [128], P('edge'), may hold values from 0 to 23
- edge_owner: int32 [128, 1], P('edge'), may hold values from 0 to 15; in each aligned block of 8 rows (0 to 7, 8 to 15, ...) at most 2 rows name the same one
- edge_target: int32 [128], P('edge'), may hold values from 0 to 23
- edge_counts: int32 [16], P('edge'), may hold values from 4 to 8, as said below
- corr_weight: bfloat16 [49, 128], replicated, may hold values from -0.875 to 0.875
- gate_weight: bfloat16 [3, 3, 256, 256], replicated, may hold values from -0.125 to 0.125
- candidate_weight: bfloat16 [3, 3, 256, 128], replicated, may hold values from -0.125 to 0.125
- jacobian_weight: bfloat16 [128, 24], replicated, may hold values from -0.5 to 0.5
- confidence_weight: bfloat16 [128, 2], replicated, may hold values from -3 to 3
Outputs:
- hidden_next: bfloat16 [128, 48, 64, 128], P('edge', 'tile')
- camera_hessian: float32 [2304, 2304], P('tile', 'edge')
- pose_diagonal: float32 [384, 36], P('edge')
Inputs may be any that keep to these rules, and one draw needn't show every extreme that they name: `edge_owner`: in the rows of one index of edge at most 2 edges name the same owner, a bound that some block reaches. `edge_counts`: edges past a device's count are unused; some index of edge uses all 8.
All inputs are finite; a program needn't handle non-finite values.
Results may differ from a plain program's by a relative error of at most 0.015.
Values may be sent and summed in bfloat16 or wider, within the bound.
No kernel may reach another device: no remote copies, remote signals or barrier semaphores. Data moves between devices by JAX's collectives and lax.ppermute only.
A program may use at most 128 MiB of HBM per device.

v0:
```python
import jax
import jax.numpy as jnp
from jax import lax
from jax.sharding import PartitionSpec as P

MAPH = 48
MAPW = 64
WINDOW = 7


def sent_together(arrays, axis, split_dim, concat_dim, along):
    widths = [a.shape[along] for a in arrays]
    both = jnp.concatenate(arrays, axis=along)
    filled = lax.all_to_all(both, axis, split_axis=split_dim, concat_axis=concat_dim, tiled=True)
    return tuple(jnp.split(filled, [sum(widths[:k]) for k in range(1, len(widths))], axis=along))


def padded_2(cells, sides, width):
    for axis, dim in sides:
        count = lax.axis_size(axis)
        ends = count - 1
        head = lax.slice_in_dim(cells, 0, width, axis=dim)
        tail = lax.slice_in_dim(cells, cells.shape[dim] - width, cells.shape[dim], axis=dim)
        cells = jnp.concatenate(
            [
                lax.ppermute(tail, axis, [(i, (i + 1) % count) for i in range(ends)]),
                cells,
                lax.ppermute(head, axis, [((i + 1) % count, i) for i in range(ends)]),
            ],
            axis=dim,
        )
    return cells


def total_of_pieces(shard, axis):
    parts = lax.all_gather(shard, axis)
    return parts.sum(axis=0)


def pad_columns(values):
    return jnp.pad(values, ((0, 0), (0, 0), (1, 1), (0, 0)))


def convolve(padded, weight):
    row_count = padded.shape[1] - 2
    col_count = padded.shape[2] - 2
    running = jnp.zeros((padded.shape[0], row_count, col_count, weight.shape[-1]), jnp.float32)
    for row_step in range(3):
        for col_step in range(3):
            window = padded[:, row_step : row_step + row_count, col_step : col_step + col_count]
            running = running + jnp.einsum(
                "erwc,ck->erwk",
                window,
                weight[row_step, col_step],
                preferred_element_type=jnp.float32,
            )
    return running


def per_device(
    features,
    hidden_state,
    edge_source,
    edge_owner,
    edge_target,
    edge_counts,
    corr_weight,
    gate_weight,
    candidate_weight,
    jacobian_weight,
    confidence_weight,
):
    edge_total = hidden_state.shape[0]
    frame_total = features.shape[0]
    band_rows = features.shape[1]
    map_width = features.shape[2]
    hidden_width = hidden_state.shape[3]
    owner_count = lax.axis_size("edge")
    slot_depth = max(2, (2 * edge_total + owner_count - 1) // owner_count)
    my_index = lax.axis_index("edge")
    in_use = jnp.arange(edge_total) < edge_counts[0]
    owners = edge_owner[:, 0]
    owner_hits = (owners[:, None] == jnp.arange(owner_count)[None, :]).astype(jnp.int32)
    earlier = jnp.cumsum(owner_hits, axis=0) - owner_hits
    rank_within = jnp.sum(earlier * owner_hits, axis=1)
    slot_index = owners * slot_depth + rank_within
    slot_hits = (slot_index[:, None] == jnp.arange(owner_count * slot_depth)[None, :]).astype(
        jnp.int32
    )
    source_global = my_index * frame_total + edge_source
    target_global = owners * frame_total + edge_target
    send_target = jnp.sum(slot_hits * edge_target[:, None], axis=0).reshape(owner_count, slot_depth)
    send_source = jnp.sum(slot_hits * source_global[:, None], axis=0).reshape(
        owner_count, slot_depth
    )
    got_target, got_source = sent_together((send_target, send_source), "edge", 0, 0, 1)
    asked = jnp.take(features, got_target.reshape(-1), axis=0).reshape(
        (owner_count, slot_depth) + features.shape[1:]
    )
    returned = lax.all_to_all(asked, "edge", split_axis=0, concat_axis=0, tiled=True)
    target_maps = jnp.take(
        returned.reshape((owner_count * slot_depth,) + features.shape[1:]), slot_index, axis=0
    )
    radius = WINDOW // 2
    source_maps = jnp.take(features, edge_source, axis=0)
    target_rows = padded_2(target_maps, (("tile", 1),), radius)
    target_padded = jnp.pad(target_rows, ((0, 0), (0, 0), (radius, radius), (0, 0)))
    columns = []
    for row_shift in range(WINDOW):
        for col_shift in range(WINDOW):
            moved = target_padded[
                :, row_shift : row_shift + band_rows, col_shift : col_shift + map_width
            ]
            columns.append(
                jnp.einsum("erwh,erwh->erw", source_maps, moved, preferred_element_type=jnp.float32)
            )
    corr = (jnp.stack(columns, axis=-1) * features.shape[3] ** (-0.5)).astype(jnp.bfloat16)
    motion = jax.nn.relu(
        jnp.einsum("ercd,dk->erck", corr, corr_weight, preferred_element_type=jnp.float32)
    ).astype(jnp.bfloat16)
    stacked = jnp.concatenate([hidden_state, motion], axis=-1)
    state_float = hidden_state.astype(jnp.float32)
    extended = padded_2(stacked, (("tile", 1),), 2)
    gates = jax.nn.sigmoid(convolve(pad_columns(extended), gate_weight))
    inner = extended[:, 1:-1]
    reset_state = (
        gates[..., hidden_width:] * inner[..., :hidden_width].astype(jnp.float32)
    ).astype(jnp.bfloat16)
    mixed = jnp.concatenate([reset_state, inner[..., hidden_width:]], axis=-1)
    candidate = jnp.tanh(convolve(pad_columns(mixed), candidate_weight))
    update = gates[:, 1:-1, :, :hidden_width]
    new_state = ((1.0 - update) * state_float + update * candidate).astype(jnp.bfloat16)
    hidden_next = jnp.where(in_use[:, None, None, None], new_state, hidden_state)
    pixel_total = band_rows * map_width
    jacobian = jnp.einsum(
        "erwh,hk->ekrw", new_state, jacobian_weight, preferred_element_type=jnp.float32
    ).reshape(edge_total, 2, 12, pixel_total)
    confidence = jax.nn.softplus(
        jnp.einsum(
            "erwh,hk->ekrw", new_state, confidence_weight, preferred_element_type=jnp.float32
        )
    ).reshape(edge_total, 2, 1, pixel_total)
    normal_blocks = jnp.einsum(
        "ekap,ekbp->eab", jacobian * confidence, jacobian, precision=lax.Precision.HIGHEST
    ) / (MAPH * MAPW)
    normal_blocks = total_of_pieces(normal_blocks, "tile")
    normal_blocks = normal_blocks * in_use.astype(jnp.float32)[:, None, None]
    outgoing = jnp.concatenate(
        [
            normal_blocks[:, 6:, 6:].reshape(edge_total, 36),
            normal_blocks[:, :6, 6:].reshape(edge_total, 36),
        ],
        axis=1,
    )
    slot_blocks = jnp.einsum(
        "es,eq->sq", slot_hits.astype(jnp.float32), outgoing, precision=lax.Precision.HIGHEST
    ).reshape(owner_count, slot_depth, 72)
    incoming = lax.all_to_all(slot_blocks, "edge", split_axis=0, concat_axis=0, tiled=True).reshape(
        owner_count * slot_depth, 72
    )
    flat_target = got_target.reshape(-1)
    flat_source = got_source.reshape(-1)
    row_frames = jnp.concatenate(
        [source_global, target_global, my_index * frame_total + flat_target, flat_source]
    )
    col_frames = jnp.concatenate([edge_source, edge_source, flat_target, flat_target])
    block_list = jnp.concatenate(
        [
            normal_blocks[:, :6, :6],
            normal_blocks[:, 6:, :6],
            incoming[:, :36].reshape(-1, 6, 6),
            incoming[:, 36:].reshape(-1, 6, 6),
        ],
        axis=0,
    )
    on_diagonal = (row_frames == my_index * frame_total + col_frames).astype(jnp.float32)
    col_hits = (col_frames[:, None] == jnp.arange(frame_total)[None, :]).astype(jnp.float32)
    diagonal_part = jnp.einsum(
        "if,iq->fq",
        col_hits * on_diagonal[:, None],
        block_list.reshape(-1, 36),
        precision=lax.Precision.HIGHEST,
    )
    apart_blocks = block_list * (1.0 - on_diagonal)[:, None, None]
    spread = (apart_blocks[:, :, None, :] * col_hits[:, None, :, None]).reshape(
        -1, 6, frame_total * 6
    )
    own_rows = frame_total * owner_count * 6 // lax.axis_size("tile")
    frame_span = own_rows // 6
    row_hits = (
        row_frames[:, None]
        == lax.axis_index("tile") * own_rows // 6 + jnp.arange(frame_span)[None, :]
    ).astype(jnp.float32)
    placed = jnp.einsum("ic,ixq->cxq", row_hits, spread, precision=lax.Precision.HIGHEST)
    camera_hessian = placed.reshape(own_rows, frame_total * 6)
    return (hidden_next, camera_hessian, diagonal_part)


def solution(mesh):
    placed = (
        P("edge", "tile", None, None),
        P("edge", "tile", None, None),
        P("edge"),
        P("edge", None),
        P("edge"),
        P("edge"),
        P(),
        P(),
        P(),
        P(),
        P(),
    )
    return jax.shard_map(
        per_device,
        mesh=mesh,
        in_specs=placed,
        out_specs=(P("edge", "tile", None, None), P("tile", "edge"), P("edge", None)),
        check_vma=False,
    )
```

profile of v0, /device:TPU:1, one launch (start us, length us, event | category | flops | bytes accessed | tf_op | source)
XLA Modules:
  0.0 144.9 jit_solution(6282451312611522177)
XLA Ops:
  0.6 0.8 fusion.154
  1.5 0.8 select_reduce_fusion.2
  2.3 0.7 fusion.176
  3.0 0.7 compare_select_fusion.4
  3.7 0.7 select_reduce_fusion.1
  4.9 13.8 %all_to_all.22 = s32[16,1,4]{2,1,0:T(1,128)S(1)} all-to-all(s32[16,1,4]{2,1,0:T(1,128)S(1)} %copy.224), channel_id=1, replica_groups=mesh['edge'=16,'tile'=16] {'edge'}, dimensions={0} | all-to-all | bytes 512 | tf_op jit(solution)/shard_map/all_to_all | solution.py:14
  18.7 0.6 fusion.181
  19.6 0.8 gather_fusion.1
  20.5 1.4 broadcast_select_fusion
  21.8 3.8 %all-to-all-start.1 = ((bf16[16,2,3,64,128]{4,3,2,1,0:T(8,128)(2,1)}), bf16[16,2,3,64,128]{4,3,2,1,0:T(8,128)(2,1)S(1)}, u32[]{:S(2)}, u32[]{:S(2)}) async-start(bf16[16,2,3,64,128]{4,3,2,1,0:T(8,128)(2,1)} %broadcast_select_fusion), calls=%async_computation.1 | async-start | bytes 3145728 | tf_op jit(solution)/shard_map/all_to_all | solution.py:100
  25.7 0.6 gather_fusion
  27.0 0.5 iota_compare_fusion.7
  27.5 0.5 and_bitcast_fusion
  28.1 18.0 %all-to-all-done.1 = bf16[16,2,3,64,128]{4,3,2,1,0:T(8,128)(2,1)S(1)} async-done(((bf16[16,2,3,64,128]{4,3,2,1,0:T(8,128)(2,1)}), bf16[16,2,3,64,128]{4,3,2,1,0:T(8,128)(2,1)S(1)}, u32[]{:S(2)}, u32[]{:S(2)}) %all-to-all-start.1) | async-done | bytes 1572896 | tf_op jit(solution)/shard_map/all_to_all | solution.py:100
  46.1 0.6 gather_fusion.2
  46.7 0.7 broadcast_select_fusion.1
  47.4 7.6 %collective-permute-start = (bf16[8,3,64,128]{3,2,1,0:T(8,128)(2,1)S(1)}, bf16[8,3,64,128]{3,2,1,0:T(8,128)(2,1)S(1)}, u32[]{:S(2)}, u32[]{:S(2)}) collective-permute-start(bf16[8,3,64,128]{3,2,1,0:T(8,128)(2,1)S(1)} %broadcast_select_fusion.1), channel_id=1, source_target_pairs={{0,1},{1,2},{2,3},{3,4},{4,5},{5,6},{6,7},{7,8},{8,9},{9,10},{10,1... | collective-permute-start | bytes 1179656 | tf_op jit(solution)/shard_map/ppermute | solution.py:26
  55.0 1.9 %collective-permute-start.1 = (bf16[8,3,64,128]{3,2,1,0:T(8,128)(2,1)S(1)}, bf16[8,3,64,128]{3,2,1,0:T(8,128)(2,1)S(1)}, u32[]{:S(2)}, u32[]{:S(2)}) collective-permute-start(bf16[8,3,64,128]{3,2,1,0:T(8,128)(2,1)S(1)} %broadcast_select_fusion.1), channel_id=1, source_target_pairs={{1,0},{2,1},{3,2},{4,3},{5,4},{6,5},{7,6},{8,7},{9,8},{10,9},{11,1... | collective-permute-start | bytes 1179656 | tf_op jit(solution)/shard_map/ppermute | solution.py:28
  57.0 0.7 compare_and_fusion.1
  57.6 2.1 %collective-permute-done = bf16[8,3,64,128]{3,2,1,0:T(8,128)(2,1)S(1)} collective-permute-done((bf16[8,3,64,128]{3,2,1,0:T(8,128)(2,1)S(1)}, bf16[8,3,64,128]{3,2,1,0:T(8,128)(2,1)S(1)}, u32[]{:S(2)}, u32[]{:S(2)}) %collective-permute-start) | collective-permute-done | bytes 393248 | tf_op jit(solution)/shard_map/ppermute | solution.py:26
  59.7 4.4 %collective-permute-done.1 = bf16[8,3,64,128]{3,2,1,0:T(8,128)(2,1)S(1)} collective-permute-done((bf16[8,3,64,128]{3,2,1,0:T(8,128)(2,1)S(1)}, bf16[8,3,64,128]{3,2,1,0:T(8,128)(2,1)S(1)}, u32[]{:S(2)}, u32[]{:S(2)}) %collective-permute-start.1) | collective-permute-done | bytes 393248 | tf_op jit(solution)/shard_map/ppermute | solution.py:28
  64.1 0.7 fusion.5
  64.8 3.9 %fusion.62 = (f32[8,3,64]{2,1,0:T(4,128)S(1)}, f32[8,3,64]{2,1,0:T(4,128)S(1)}, f32[8,3,64]{2,1,0:T(4,128)S(1)}, f32[8,3,64]{2,1,0:T(4,128)S(1)}, f32[8,3,64]{2,...) fusion(bf16[8,9,70,128]{3,2,1,0:T(8,128)(2,1)S(1)} %fusion.5, ...), kind=kLoop, calls=%fused_computation.143 | loop fusion | flops 10394112 | bytes 7182344
  68.8 3.9 %fusion.82 = (f32[8,3,64]{2,1,0:T(4,128)S(1)}, f32[8,3,64]{2,1,0:T(4,128)S(1)}, f32[8,3,64]{2,1,0:T(4,128)S(1)}, f32[8,3,64]{2,1,0:T(4,128)S(1)}, f32[8,3,64]{2,...) fusion(bf16[8,9,70,128]{3,2,1,0:T(8,128)(2,1)S(1)} %fusion.5, ...), kind=kLoop, calls=%fused_computation.163 | loop fusion | flops 10394112 | bytes 7182344
  72.7 2.0 %fusion.42 = (f32[8,3,64]{2,1,0:T(4,128)S(1)}, f32[8,3,64]{2,1,0:T(4,128)S(1)}, f32[8,3,64]{2,1,0:T(4,128)S(1)}, f32[8,3,64]{2,1,0:T(4,128)S(1)}, f32[8,3,64]{2,...) fusion(bf16[8,9,70,128]{3,2,1,0:T(8,128)(2,1)S(1)} %fusion.5, ...), kind=kLoop, calls=%fused_computation.123 | loop fusion | flops 5099520 | bytes 3588104
  75.6 1.7 %fusion.72 = (f32[8,3,64]{2,1,0:T(4,128)S(1)}, f32[8,3,64]{2,1,0:T(4,128)S(1)}, f32[8,3,64]{2,1,0:T(4,128)S(1)}, f32[8,3,64]{2,1,0:T(4,128)S(1)}, f32[8,3,64]{2,...) fusion(bf16[8,3,64,128]{3,2,1,0:T(8,128)(2,1)S(1)} %collective-permute-done.1, ...), kind=kLoop, calls=%fused_computation.153 | loop fusion | flops 5297664 | bytes 1615880
  77.5 0.9 stack.199
  78.8 1.1 fusion.83
  79.9 1.9 %collective-permute-start.2 = (bf16[8,2,64,256]{3,2,1,0:T(8,128)(2,1)}, bf16[8,2,64,256]{3,2,1,0:T(8,128)(2,1)}, u32[]{:S(2)}, u32[]{:S(2)}) collective-permute-start(bf16[8,2,64,256]{3,2,1,0:T(8,128)(2,1)} %get-tuple-element.60), channel_id=1, source_target_pairs={{0,1},{1,2},{2,3},{3,4},{4,5},{5,6},{6,7},{7,8},{8,9},{9,10},{10,1... | collective-permute-start | bytes 1572872 | tf_op jit(solution)/shard_map/ppermute | solution.py:26
  81.8 3.4 %collective-permute-start.3 = (bf16[8,2,64,256]{3,2,1,0:T(8,128)(2,1)}, bf16[8,2,64,256]{3,2,1,0:T(8,128)(2,1)}, u32[]{:S(2)}, u32[]{:S(2)}) collective-permute-start(bf16[8,2,64,256]{3,2,1,0:T(8,128)(2,1)} %get-tuple-element.61), channel_id=1, source_target_pairs={{1,0},{2,1},{3,2},{4,3},{5,4},{6,5},{7,6},{8,7},{9,8},{10,9},{11,1... | collective-permute-start | bytes 1572872 | tf_op jit(solution)/shard_map/ppermute | solution.py:28
  85.6 2.6 %collective-permute-done.2 = bf16[8,2,64,256]{3,2,1,0:T(8,128)(2,1)} collective-permute-done((bf16[8,2,64,256]{3,2,1,0:T(8,128)(2,1)}, bf16[8,2,64,256]{3,2,1,0:T(8,128)(2,1)}, u32[]{:S(2)}, u32[]{:S(2)}) %collective-permute-start.2) | collective-permute-done | bytes 524320 | tf_op jit(solution)/shard_map/ppermute | solution.py:26
  88.2 4.7 %collective-permute-done.3 = bf16[8,2,64,256]{3,2,1,0:T(8,128)(2,1)} collective-permute-done((bf16[8,2,64,256]{3,2,1,0:T(8,128)(2,1)}, bf16[8,2,64,256]{3,2,1,0:T(8,128)(2,1)}, u32[]{:S(2)}, u32[]{:S(2)}) %collective-permute-start.3) | collective-permute-done | bytes 524320 | tf_op jit(solution)/shard_map/ppermute | solution.py:28
  92.9 1.4 pad_maximum_fusion
  95.4 0.5 fusion.7
  96.4 0.5 fusion.9
  97.0 1.5 %fusion.96 = f32[8,5,64,256]{3,2,1,0:T(8,128)S(1)} fusion(bf16[3,3,256,256]{3,2,1,0:T(8,128)(2,1)S(1)} %copy-done.3, bf16[8,2,64,256]{3,2,1,0:T(8,128)(2,1)} %collective-permute-done.3, bf16[8,3,64,128]{3,2,1,0:T(8,128)(2,1)S(1)} %fusion.29, bf16[8,3,64,128]{3,2,1,0:T(8,128)(2,1)S(1)} %copy-done.1, bf16[8,2,64,256]{3,2,1,0:T(8,128)(2,1)} %collective-permute-done.2), kind=kOutput, calls=%fused_computation.192 | convolution fusion | flops 342884352 | bytes 4587520 | tf_op jit(solution)/shard_map/erwc,ck->erwk/dot_general | solution.py:51
  98.6 1.5 %fusion.13 = f32[8,5,64,256]{3,2,1,0:T(8,128)S(1)} fusion(bf16[8,3,64,128]{3,2,1,0:T(8,128)(2,1)S(1)} %fusion.29, bf16[8,3,64,128]{3,2,1,0:T(8,128)(2,1)S(1)} %copy-done.1, bf16[8,2,64,256]{3,2,1,0:T(8,128)(2,1)} %collective-permute-done.2, bf16[3,3,256,256]{3,2,1,0:T(8,128)(2,1)S(1)} %copy-done.3), kind=kOutput, calls=%fused_computation.77 | convolution fusion | flops 339476480 | bytes 4063232 | tf_op jit(solution)/shard_map/erwc,ck->erwk/dot_general | solution.py:51
  100.1 1.5 %fusion.19 = f32[8,5,64,256]{3,2,1,0:T(8,128)S(1)} fusion(bf16[8,2,64,256]{3,2,1,0:T(8,128)(2,1)} %collective-permute-done.3, bf16[8,3,64,128]{3,2,1,0:T(8,128)(2,1)S(1)} %fusion.29, bf16[8,3,64,128]{3,2,1,0:T(8,128)(2,1)S(1)} %copy-done.1, bf16[3,3,256,256]{3,2,1,0:T(8,128)(2,1)S(1)} %copy-done.3), kind=kOutput, calls=%fused_computation.83 | convolution fusion | flops 339476480 | bytes 4063232 | tf_op jit(solution)/shard_map/erwc,ck->erwk/dot_general | solution.py:51
  101.7 1.4 add_divide_fusion
  103.5 0.9 copy-done.2
  107.8 1.3 broadcast_select_fusion.3
  110.4 0.6 fusion.30
  111.0 20.3 %all-gather = f32[128,12,12]{2,0,1:T(8,128)S(1)} all-gather(f32[8,12,12]{2,0,1:T(8,128)S(1)} %copy.283), channel_id=2, replica_groups=mesh['edge'=16,'tile'=16] {'tile'}, dimensions={0}, use_global_device_ids=true | all-gather | bytes 78336 | tf_op jit(solution)/shard_map/all_gather | solution.py:36
  131.6 0.9 fusion.148
  132.5 3.5 %all-to-all-start.2 = ((f32[16,2,72]{2,1,0:T(2,128)}), f32[16,2,72]{2,1,0:T(2,128)S(1)}, u32[]{:S(2)}, u32[]{:S(2)}) async-start(f32[16,2,72]{2,1,0:T(2,128)} %bitcast.126), calls=%async_computation.2 | async-start | bytes 32768 | tf_op jit(solution)/shard_map/all_to_all | solution.py:158
  136.5 5.9 %all-to-all-done.2 = f32[16,2,72]{2,1,0:T(2,128)S(1)} async-done(((f32[16,2,72]{2,1,0:T(2,128)}), f32[16,2,72]{2,1,0:T(2,128)S(1)}, u32[]{:S(2)}, u32[]{:S(2)}) %all-to-all-start.2) | async-done | bytes 9248 | tf_op jit(solution)/shard_map/all_to_all | solution.py:158
  143.4 0.7 reshape.312
  144.1 0.8 fusion.129
  (149 shorter events, 10.7 us)
Async XLA Ops:
  0.6 19.0 %copy-start = (bf16[24,3,64,128]{3,2,1,0:T(8,128)(2,1)S(1)}, bf16[24,3,64,128]{3,2,1,0:T(8,128)(2,1)}, u32[]{:S(2)}) copy-start(bf16[24,3,64,128]{3,2,1,0:T(8,128)(2,1)} %param.11) | copy-start | bytes 3538948
  3.0 1.4 copy-start.10
  3.7 0.8 copy-start.7
  21.8 5.7 %copy-start.6 = (s32[8,1]{0,1:T(1,128)S(1)}, s32[8,1]{0,1:T(1,128)}, u32[]{:S(2)}) copy-start(s32[8,1]{0,1:T(1,128)} %param.14) | copy-start | bytes 100
  21.8 24.2 %all-to-all-start.1 = ((bf16[16,2,3,64,128]{4,3,2,1,0:T(8,128)(2,1)}), bf16[16,2,3,64,128]{4,3,2,1,0:T(8,128)(2,1)S(1)}, u32[]{:S(2)}, u32[]{:S(2)}) async-start(bf16[16,2,3,64,128]{4,3,2,1,0:T(8,128)(2,1)} %broadcast_select_fusion), calls=%async_computation.1 | async-start | bytes 3145728 | tf_op jit(solution)/shard_map/all_to_all | solution.py:100
  47.4 12.3 %collective-permute-start = (bf16[8,3,64,128]{3,2,1,0:T(8,128)(2,1)S(1)}, bf16[8,3,64,128]{3,2,1,0:T(8,128)(2,1)S(1)}, u32[]{:S(2)}, u32[]{:S(2)}) collective-permute-start(bf16[8,3,64,128]{3,2,1,0:T(8,128)(2,1)S(1)} %broadcast_select_fusion.1), channel_id=1, source_target_pairs={{0,1},{1,2},{2,3},{3,4},{4,5},{5,6},{6,7},{7,8},{8,9},{9,10},{10,1... | collective-permute-start | bytes 1179656 | tf_op jit(solution)/shard_map/ppermute | solution.py:26
  55.0 9.1 %collective-permute-start.1 = (bf16[8,3,64,128]{3,2,1,0:T(8,128)(2,1)S(1)}, bf16[8,3,64,128]{3,2,1,0:T(8,128)(2,1)S(1)}, u32[]{:S(2)}, u32[]{:S(2)}) collective-permute-start(bf16[8,3,64,128]{3,2,1,0:T(8,128)(2,1)S(1)} %broadcast_select_fusion.1), channel_id=1, source_target_pairs={{1,0},{2,1},{3,2},{4,3},{5,4},{6,5},{7,6},{8,7},{9,8},{10,9},{11,1... | collective-permute-start | bytes 1179656 | tf_op jit(solution)/shard_map/ppermute | solution.py:28
  75.3 3.2 %copy-start.4 = (bf16[49,128]{1,0:T(8,128)(2,1)S(1)}, bf16[49,128]{1,0:T(8,128)(2,1)}, u32[]{:S(2)}) copy-start(bf16[49,128]{1,0:T(8,128)(2,1)} %param.17) | copy-start | bytes 37636
  75.6 3.2 %copy-start.1 = (bf16[8,3,64,128]{3,2,1,0:T(8,128)(2,1)S(1)}, bf16[8,3,64,128]{3,2,1,0:T(8,128)(2,1)}, u32[]{:S(2)}) copy-start(bf16[8,3,64,128]{3,2,1,0:T(8,128)(2,1)} %param.12) | copy-start | bytes 1179652
  77.5 7.7 %copy-start.14 = (s32[8]{0:T(128)S(1)}, s32[8]{0:T(128)}, u32[]{:S(2)}) copy-start(s32[8]{0:T(128)} %param.15) | copy-start | bytes 100
  77.5 7.8 %copy-start.9 = (s32[16,2]{0,1:T(2,128)S(1)}, s32[16,2]{0,1:T(2,128)}, u32[]{:S(2)}) copy-start(s32[16,2]{0,1:T(2,128)} %get-tuple-element.68) | copy-start | bytes 388
  77.5 8.0 %copy-start.8 = (s32[8]{0:T(128)S(1)}, s32[8]{0:T(128)}, u32[]{:S(2)}) copy-start(s32[8]{0:T(128)} %copy-done.7) | copy-start | bytes 100
  77.5 8.0 %copy-start.12 = (s32[8]{0:T(128)S(1)}, s32[8]{0:T(128)}, u32[]{:S(2)}) copy-start(s32[8]{0:T(128)} %param.13) | copy-start | bytes 100
  79.9 8.3 %collective-permute-start.2 = (bf16[8,2,64,256]{3,2,1,0:T(8,128)(2,1)}, bf16[8,2,64,256]{3,2,1,0:T(8,128)(2,1)}, u32[]{:S(2)}, u32[]{:S(2)}) collective-permute-start(bf16[8,2,64,256]{3,2,1,0:T(8,128)(2,1)} %get-tuple-element.60), channel_id=1, source_target_pairs={{0,1},{1,2},{2,3},{3,4},{4,5},{5,6},{6,7},{7,8},{8,9},{9,10},{10,1... | collective-permute-start | bytes 1572872 | tf_op jit(solution)/shard_map/ppermute | solution.py:26
  81.8 11.1 %collective-permute-start.3 = (bf16[8,2,64,256]{3,2,1,0:T(8,128)(2,1)}, bf16[8,2,64,256]{3,2,1,0:T(8,128)(2,1)}, u32[]{:S(2)}, u32[]{:S(2)}) collective-permute-start(bf16[8,2,64,256]{3,2,1,0:T(8,128)(2,1)} %get-tuple-element.61), channel_id=1, source_target_pairs={{1,0},{2,1},{3,2},{4,3},{5,4},{6,5},{7,6},{8,7},{9,8},{10,9},{11,1... | collective-permute-start | bytes 1572872 | tf_op jit(solution)/shard_map/ppermute | solution.py:28
  85.6 8.7 %copy-start.3 = (bf16[3,3,256,256]{3,2,1,0:T(8,128)(2,1)S(1)}, bf16[3,3,256,256]{3,2,1,0:T(8,128)(2,1)}, u32[]{:S(2)}) copy-start(bf16[3,3,256,256]{3,2,1,0:T(8,128)(2,1)} %param.18) | copy-start | bytes 3538948
  103.3 1.1 copy-start.2
  107.1 0.7 copy-start.13
  107.8 1.3 copy-start.5
  109.0 0.8 copy-start.15
  109.8 21.8 %copy-start.11 = (s32[8]{0:T(128)S(1)}, s32[8]{0:T(128)}, u32[]{:S(2)}) copy-start(s32[8]{0:T(128)} %copy-done.10) | copy-start | bytes 100
  132.5 9.9 %all-to-all-start.2 = ((f32[16,2,72]{2,1,0:T(2,128)}), f32[16,2,72]{2,1,0:T(2,128)S(1)}, u32[]{:S(2)}, u32[]{:S(2)}) async-start(f32[16,2,72]{2,1,0:T(2,128)} %bitcast.126), calls=%async_computation.2 | async-start | bytes 32768 | tf_op jit(solution)/shard_map/all_to_all | solution.py:158
where the time goes:
time: 145 us
  waiting for transfers between devices  37.7 us (26%)
  blocking collectives  34.1 us (24%)
  other arithmetic  23.1 us (16%)
  starting transfers between devices  22.1 us (15%)
  matrix products  16.8 us (12%)
  local copies, waits for them, and re-layouts  8.84 us (6%)
  between operations  2.27 us (2%)
    all_gather x1, blocking collectives, total_of_pieces(): parts = lax.all_gather(shard, axis)  20.3 us
    all_to_all x1, waiting for transfers between devices, per_device(): lax.all_to_all(asked, 'edge', split_axis=0, concat_axis=0, tiled=True)  18 us
    all_to_all x1, blocking collectives, sent_together(): lax.all_to_all(both, axis, split_axis=split_dim, concat_axis=concat_dim,...  13.8 us
    dot_general x18, matrix products, convolve(): jnp.einsum('erwc,ck->erwk', window, weight[row_step, col_step], preferred...  12.9 us
    unnamed x4, other arithmetic  11.5 us
    ppermute x2, starting transfers between devices, padded_2(): lax.ppermute(tail, axis, [(i, (i + 1) % count) for i in range(ends)])  9.5 us
    ppermute x2, waiting for transfers between devices, padded_2(): lax.ppermute(head, axis, [((i + 1) % count, i) for i in range(ends)])  9.08 us
    all_to_all x1, waiting for transfers between devices, per_device(): lax.all_to_all(slot_blocks, 'edge', split_axis=0, concat_axis=0, tiled=True)  5.95 us
  transfers between devices with their start and end apart: 6, of which 6 were waited for; matrix products, arithmetic and copies ran while one was open for 2% of the time, Pallas kernels for 0%

commit v1 on v0

--- a/solution.py
+++ b/solution.py
@@ -18,14 +18,16 @@
 def padded_2(cells, sides, width):
     for axis, dim in sides:
         count = lax.axis_size(axis)
-        ends = count - 1
+        place = lax.axis_index(axis)
         head = lax.slice_in_dim(cells, 0, width, axis=dim)
         tail = lax.slice_in_dim(cells, cells.shape[dim] - width, cells.shape[dim], axis=dim)
+        above = lax.ppermute(tail, axis, [(i, (i + 1) % count) for i in range(count)])
+        below = lax.ppermute(head, axis, [((i + 1) % count, i) for i in range(count)])
         cells = jnp.concatenate(
             [
-                lax.ppermute(tail, axis, [(i, (i + 1) % count) for i in range(ends)]),
+                jnp.where(place == 0, jnp.zeros_like(above), above),
                 cells,
-                lax.ppermute(head, axis, [((i + 1) % count, i) for i in range(ends)]),
+                jnp.where(place == count - 1, jnp.zeros_like(below), below),
             ],
             axis=dim,
         )
@@ -33,8 +35,10 @@
 
 
 def total_of_pieces(shard, axis):
-    parts = lax.all_gather(shard, axis)
-    return parts.sum(axis=0)
+    count = lax.axis_size(axis)
+    copies = jnp.broadcast_to(shard.reshape(1, shard.shape[0], -1), (count, shard.shape[0], shard.size // shard.shape[0]))
+    parts = lax.all_to_all(copies, axis, split_axis=0, concat_axis=0, tiled=True)
+    return parts.sum(axis=0).reshape(shard.shape)
 
 
 def pad_columns(values):
@@ -94,15 +98,15 @@
         owner_count, slot_depth
     )
     got_target, got_source = sent_together((send_target, send_source), "edge", 0, 0, 1)
-    asked = jnp.take(features, got_target.reshape(-1), axis=0).reshape(
+    asked = jnp.take(features, got_target.reshape(-1), axis=0, mode="clip").reshape(
         (owner_count, slot_depth) + features.shape[1:]
     )
     returned = lax.all_to_all(asked, "edge", split_axis=0, concat_axis=0, tiled=True)
     target_maps = jnp.take(
-        returned.reshape((owner_count * slot_depth,) + features.shape[1:]), slot_index, axis=0
+        returned.reshape((owner_count * slot_depth,) + features.shape[1:]), slot_index, axis=0, mode="clip"
     )
     radius = WINDOW // 2
-    source_maps = jnp.take(features, edge_source, axis=0)
+    source_maps = jnp.take(features, edge_source, axis=0, mode="clip")
     target_rows = padded_2(target_maps, (("tile", 1),), radius)
     target_padded = jnp.pad(target_rows, ((0, 0), (0, 0), (radius, radius), (0, 0)))
     columns = []

time: 145 us -> 129 us (0.89)
  blocking collectives: 34.1 us -> 13.8 us
  waiting for transfers between devices: 37.7 us -> 45.3 us
  other arithmetic: 23.1 us -> 16.7 us
  starting transfers between devices: 22.1 us -> 26.8 us
  matrix products: 16.8 us -> 13.7 us
    all_gather x1 -> x0, blocking collectives: 20.3 us -> none  [total_of_pieces(): parts = lax.all_gather(shard, axis)]
    all_to_all x0 -> x1, starting transfers between devices: none -> 9.59 us  [total_of_pieces(): lax.all_to_all(copies, axis, split_axis=0, concat_axis=0, tiled=True)]
    all_to_all x0 -> x1, waiting for transfers between devices: none -> 8.9 us  [total_of_pieces(): lax.all_to_all(copies, axis, split_axis=0, concat_axis=0, tiled=True)]
    ppermute x4, starting transfers between devices: 14.8 us -> 9.87 us  [the longest x2 6.89 us: padded_2(): lax.ppermute(head, axis, [((i + 1) % count, i) for i in range(count)])]
    ppermute x4, waiting for transfers between devices: 13.8 us -> 10.1 us  [the longest x2 6.7 us: padded_2(): lax.ppermute(head, axis, [((i + 1) % count, i) for i in range(count)])]
    select_n x5 -> x4, other arithmetic: 3.42 us -> 0.14 us  [the longest x2 0.07 us: padded_2(): jnp.where(place == 0, jnp.zeros_like(above), above)]
    dot_general x18, matrix products: 12.9 us -> 9.84 us  [convolve(): jnp.einsum('erwc,ck->erwk', window, weight[row_step, col_step], preferred...]
    all_to_all x1, waiting for transfers between devices: 18 us -> 20.4 us  [per_device(): lax.all_to_all(asked, 'edge', split_axis=0, concat_axis=0, tiled=True)]
  transfers between devices with their start and end apart: 6 -> 7, of which waited for: 6 -> 6; matrix products, arithmetic and copies ran while one was open for 2% -> 1% of each run, Pallas kernels for 0% -> 0%
where the time goes in v1:
time: 129 us; the launch traced here: 128 us
  waiting for transfers between devices  45.3 us (35%)
  starting transfers between devices  26.8 us (21%)
  other arithmetic  16.7 us (13%)
  blocking collectives  13.8 us (11%)
  matrix products  13.7 us (11%)
  local copies, waits for them, and re-layouts  9.7 us (8%)
  between operations  2.19 us (2%)
    all_to_all x1, waiting for transfers between devices, per_device(): lax.all_to_all(asked, 'edge', split_axis=0, concat_axis=0, tiled=True)  20.4 us
    all_to_all x1, blocking collectives, sent_together(): lax.all_to_all(both, axis, split_axis=split_dim, concat_axis=concat_dim,...  13.8 us
    unnamed x3, other arithmetic  11 us
    dot_general x18, matrix products, convolve(): jnp.einsum('erwc,ck->erwk', window, weight[row_step, col_step], preferred...  9.84 us
    all_to_all x1, starting transfers between devices, total_of_pieces(): lax.all_to_all(copies, axis, split_axis=0, concat_axis=0, tiled=True)  9.59 us
    all_to_all x1, waiting for transfers between devices, total_of_pieces(): lax.all_to_all(copies, axis, split_axis=0, concat_axis=0, tiled=True)  8.9 us
    ppermute x2, starting transfers between devices, padded_2(): lax.ppermute(head, axis, [((i + 1) % count, i) for i in range(count)])  6.89 us
    ppermute x2, waiting for transfers between devices, padded_2(): lax.ppermute(head, axis, [((i + 1) % count, i) for i in range(count)])  6.7 us
  transfers between devices with their start and end apart: 7, of which 6 were waited for; matrix products, arithmetic and copies ran while one was open for 1% of the time, Pallas kernels for 0%

profile of v1, /device:TPU:1, one launch (start us, length us, event | category | flops | bytes accessed | tf_op | source)
XLA Modules:
  0.0 128.2 jit_solution(11380532590144087472)
XLA Ops:
  0.6 0.8 fusion.152
  1.5 0.8 select_reduce_fusion.2
  2.3 0.7 fusion.155
  3.0 0.7 broadcast_add_fusion.1
  3.7 0.7 select_reduce_fusion.1
  4.8 13.8 %all_to_all.27 = s32[16,1,4]{2,1,0:T(1,128)S(1)} all-to-all(s32[16,1,4]{2,1,0:T(1,128)S(1)} %copy.210), channel_id=1, replica_groups=mesh['edge'=16,'tile'=16] {'edge'}, dimensions={0} | all-to-all | bytes 512 | tf_op jit(solution)/shard_map/all_to_all | solution.py:14
  18.9 1.9 %gather_fusion.1 = bf16[32,3,64,128]{3,2,1,0:T(8,128)(2,1)} fusion(bf16[24,3,64,128]{3,2,1,0:T(8,128)(2,1)S(1)} %copy-done, s32[1024]{0:T(1024)S(1)} %pad_clamp_fusion.1), kind=kCustom, calls=%fused_computation.1 | custom fusion | bytes 3145856 | tf_op jit(solution)/shard_map/jit(_take)/gather | solution.py:101
  20.8 3.8 %all-to-all-start.1 = ((bf16[16,2,3,64,128]{4,3,2,1,0:T(8,128)(2,1)}), bf16[16,2,3,64,128]{4,3,2,1,0:T(8,128)(2,1)S(1)}, u32[]{:S(2)}, u32[]{:S(2)}) async-start(bf16[16,2,3,64,128]{4,3,2,1,0:T(8,128)(2,1)} %bitcast.6), calls=%async_computation.1 | async-start | bytes 3145728 | tf_op jit(solution)/shard_map/all_to_all | solution.py:104
  24.7 20.4 %all-to-all-done.1 = bf16[16,2,3,64,128]{4,3,2,1,0:T(8,128)(2,1)S(1)} async-done(((bf16[16,2,3,64,128]{4,3,2,1,0:T(8,128)(2,1)}), bf16[16,2,3,64,128]{4,3,2,1,0:T(8,128)(2,1)S(1)}, u32[]{:S(2)}, u32[]{:S(2)}) %all-to-all-start.1) | async-done | bytes 1572896 | tf_op jit(solution)/shard_map/all_to_all | solution.py:104
  45.1 0.6 gather_fusion.2
  45.7 4.2 %collective-permute-start.1 = (bf16[8,3,64,128]{3,2,1,0:T(8,128)(2,1)S(1)}, bf16[8,3,64,128]{3,2,1,0:T(8,128)(2,1)S(1)}, u32[]{:S(2)}, u32[]{:S(2)}) collective-permute-start(bf16[8,3,64,128]{3,2,1,0:T(8,128)(2,1)S(1)} %gather_fusion.2), channel_id=1, source_target_pairs={{1,0},{2,1},{3,2},{4,3},{5,4},{6,5},{7,6},{8,7},{9,8},{10,9},{11,1... | collective-permute-start | bytes 1179656 | tf_op jit(solution)/shard_map/ppermute | solution.py:25
  49.9 1.5 %collective-permute-start = (bf16[8,3,64,128]{3,2,1,0:T(8,128)(2,1)S(1)}, bf16[8,3,64,128]{3,2,1,0:T(8,128)(2,1)S(1)}, u32[]{:S(2)}, u32[]{:S(2)}) collective-permute-start(bf16[8,3,64,128]{3,2,1,0:T(8,128)(2,1)S(1)} %gather_fusion.2), channel_id=1, source_target_pairs={{0,1},{1,2},{2,3},{3,4},{4,5},{5,6},{6,7},{7,8},{8,9},{9,10},{10,1... | collective-permute-start | bytes 1179656 | tf_op jit(solution)/shard_map/ppermute | solution.py:24
  51.4 0.6 gather_fusion
  52.7 4.4 %collective-permute-done.1 = bf16[8,3,64,128]{3,2,1,0:T(8,128)(2,1)S(1)} collective-permute-done((bf16[8,3,64,128]{3,2,1,0:T(8,128)(2,1)S(1)}, bf16[8,3,64,128]{3,2,1,0:T(8,128)(2,1)S(1)}, u32[]{:S(2)}, u32[]{:S(2)}) %collective-permute-start.1) | collective-permute-done | bytes 393248 | tf_op jit(solution)/shard_map/ppermute | solution.py:25
  57.2 0.7 fusion.5
  57.9 2.9 %fusion.70 = (f32[8,3,64]{2,1,0:T(4,128)S(1)}, f32[8,3,64]{2,1,0:T(4,128)S(1)}, f32[8,3,64]{2,1,0:T(4,128)S(1)}, f32[8,3,64]{2,1,0:T(4,128)S(1)}, f32[8,3,64]{2,...) fusion(bf16[8,3,64,128]{3,2,1,0:T(8,128)(2,1)S(1)} %gather_fusi, ...), kind=kLoop, calls=%fused_computation.152 | loop fusion | flops 8630784 | bytes 4012032
  60.8 4.0 %fusion.79 = (f32[8,3,64]{2,1,0:T(4,128)S(1)}, f32[8,3,64]{2,1,0:T(4,128)S(1)}, f32[8,3,64]{2,1,0:T(4,128)S(1)}, f32[8,3,64]{2,1,0:T(4,128)S(1)}, f32[8,3,64]{2,...) fusion(bf16[8,3,64,128]{3,2,1,0:T(8,128)(2,1)S(1)} %gather_fusi, ...), kind=kLoop, calls=%fused_computation.161 | loop fusion | flops 10785792 | bytes 7581696
  64.8 4.1 %fusion.80 = (f32[8,3,64]{2,1,0:T(4,128)S(1)}, f32[8,3,64]{2,1,0:T(4,128)S(1)}, f32[8,3,64]{2,1,0:T(4,128)S(1)}, f32[8,3,64]{2,1,0:T(4,128)S(1)}, f32[8,3,64]{2,...) fusion(bf16[8,3,64,128]{3,2,1,0:T(8,128)(2,1)S(1)} %gather_fusi, ...), kind=kLoop, calls=%fused_computation.162 | loop fusion | flops 10785792 | bytes 7581696
  70.1 0.9 stack.199
  71.5 1.4 %collective-permute-start.2 = (bf16[8,2,64,256]{3,2,1,0:T(8,128)(2,1)S(1)}, bf16[8,2,64,256]{3,2,1,0:T(8,128)(2,1)S(1)}, u32[]{:S(2)}, u32[]{:S(2)}) collective-permute-start(bf16[8,2,64,256]{3,2,1,0:T(8,128)(2,1)S(1)} %get-tuple-element.66), channel_id=1, source_target_pairs={{0,1},{1,2},{2,3},{3,4},{4,5},{5,6},{6,7},{7,8},{8,9},{9,10},{10,1... | collective-permute-start | bytes 1572872 | tf_op jit(solution)/shard_map/ppermute | solution.py:24
  73.0 2.7 %collective-permute-start.3 = (bf16[8,2,64,256]{3,2,1,0:T(8,128)(2,1)S(1)}, bf16[8,2,64,256]{3,2,1,0:T(8,128)(2,1)S(1)}, u32[]{:S(2)}, u32[]{:S(2)}) collective-permute-start(bf16[8,2,64,256]{3,2,1,0:T(8,128)(2,1)S(1)} %get-tuple-element.67), channel_id=1, source_target_pairs={{1,0},{2,1},{3,2},{4,3},{5,4},{6,5},{7,6},{8,7},{9,8},{10,9},{11,1... | collective-permute-start | bytes 1572872 | tf_op jit(solution)/shard_map/ppermute | solution.py:25
  75.7 3.4 %collective-permute-done.2 = bf16[8,2,64,256]{3,2,1,0:T(8,128)(2,1)S(1)} collective-permute-done((bf16[8,2,64,256]{3,2,1,0:T(8,128)(2,1)S(1)}, bf16[8,2,64,256]{3,2,1,0:T(8,128)(2,1)S(1)}, u32[]{:S(2)}, u32[]{:S(2)}) %collective-permute-start.2) | collective-permute-done | bytes 524320 | tf_op jit(solution)/shard_map/ppermute | solution.py:24
  79.1 0.5 fusion.13
  79.6 2.3 %collective-permute-done.3 = bf16[8,2,64,256]{3,2,1,0:T(8,128)(2,1)S(1)} collective-permute-done((bf16[8,2,64,256]{3,2,1,0:T(8,128)(2,1)S(1)}, bf16[8,2,64,256]{3,2,1,0:T(8,128)(2,1)S(1)}, u32[]{:S(2)}, u32[]{:S(2)}) %collective-permute-start.3) | collective-permute-done | bytes 524320 | tf_op jit(solution)/shard_map/ppermute | solution.py:25
  81.9 0.5 fusion.94
  82.4 0.5 fusion.19
  83.1 0.5 fusion.10
  83.7 0.5 fusion.6
  84.2 0.5 fusion.7
  84.7 0.5 fusion.8
  85.2 0.5 fusion.9
  85.9 1.4 %add_divide_fusion = f32[8,5,64,256]{3,2,1,0:T(8,128)S(1)} fusion(f32[8,5,64,256]{3,2,1,0:T(8,128)S(1)} %fusion.19, f32[8,5,64,256]{3,2,1,0:T(8,128)S(1)} %fusion.10, f32[8,5,64,256]{3,2,1,0:T(8,128)S(1)} %fusion.9, f32[8,5,64,256]{3,2,1,0:T(8,128)S(1)} %fusion.94, f32[8,5,64,256]{3,2,1,0:T(8,128)S(1)} %fusion.8, f32[8,5,64,256]{3,2,1,0:T(8,128)S(1)} %fusion.7, ...), kind=kOutput, calls=%fused_computation.55 | convolution fusion | flops 342753280 | bytes 25559040 | tf_op jit(solution)/shard_map/erwc,ck->erwk/dot_general | solution.py:55
  87.7 0.9 copy-done.2
  89.7 0.4 convolution_add_fusion.3
  90.9 0.4 convolution_add_fusion.1
  91.7 1.3 %broadcast_select_fusion.2 = (bf16[8,3,64,128]{3,2,1,0:T(8,128)(2,1)}, bf16[8,3,64,128]{3,2,1,0:T(8,128)(2,1)S(1)}) fusion(bf16[8,3,64,128]{3,2,1,0:T(8,128)(2,1)S(1)} %copy-done.1, pred[8]{0:T(512)(128)(4,1)S(1)} %iota_compare_fusion.7, f32[8,3,64,128]{3,2,1,0:T(8,128)S(1)} %convolution_add_fusion.5, bf16[3,3,256,128]{3,2,1,0:T(8,128)(2,1)S(1)} %copy-done.2, ...), kind=kOutput, calls=%fused_computation.180 | convolution fusion | flops 102236160 | bytes 4129280 | tf_op jit(solution)/shard_map/erwc,ck->erwk/dot_general | solution.py:55
  93.0 0.4 convolution_bitcast_fusion
  93.8 0.4 compare_select_fusion
  94.3 0.6 fusion.30
  95.0 0.7 broadcast_in_dim.26
  95.7 9.6 %all-to-all-start.2 = ((f32[16,8,144]{2,1,0:T(8,128)}), f32[16,8,144]{2,1,0:T(8,128)S(1)}, u32[]{:S(2)}, u32[]{:S(2)}) async-start(f32[16,8,144]{2,1,0:T(8,128)} %broadcast_in_dim.26), calls=%async_computation.2 | async-start | bytes 262144 | tf_op jit(solution)/shard_map/all_to_all | solution.py:40
  105.5 8.9 %all-to-all-done.2 = f32[16,8,144]{2,1,0:T(8,128)S(1)} async-done(((f32[16,8,144]{2,1,0:T(8,128)}), f32[16,8,144]{2,1,0:T(8,128)S(1)}, u32[]{:S(2)}, u32[]{:S(2)}) %all-to-all-start.2) | async-done | bytes 73760 | tf_op jit(solution)/shard_map/all_to_all | solution.py:40
  114.9 0.9 fusion.146
  115.8 3.5 %all-to-all-start.3 = ((f32[16,2,72]{2,1,0:T(2,128)}), f32[16,2,72]{2,1,0:T(2,128)S(1)}, u32[]{:S(2)}, u32[]{:S(2)}) async-start(f32[16,2,72]{2,1,0:T(2,128)} %bitcast.122), calls=%async_computation.3 | async-start | bytes 32768 | tf_op jit(solution)/shard_map/all_to_all | solution.py:162
  119.7 6.0 %all-to-all-done.3 = f32[16,2,72]{2,1,0:T(2,128)S(1)} async-done(((f32[16,2,72]{2,1,0:T(2,128)}), f32[16,2,72]{2,1,0:T(2,128)S(1)}, u32[]{:S(2)}, u32[]{:S(2)}) %all-to-all-start.3) | async-done | bytes 9248 | tf_op jit(solution)/shard_map/all_to_all | solution.py:162
  126.2 0.5 fusion.82
  126.7 0.7 reshape.272
  127.4 0.8 fusion.127
  (139 shorter events, 7.2 us)
Async XLA Ops:
  0.6 18.3 %copy-start = (bf16[24,3,64,128]{3,2,1,0:T(8,128)(2,1)S(1)}, bf16[24,3,64,128]{3,2,1,0:T(8,128)(2,1)}, u32[]{:S(2)}) copy-start(bf16[24,3,64,128]{3,2,1,0:T(8,128)(2,1)} %param.11) | copy-start | bytes 3538948
  3.7 0.7 copy-start.8
  20.8 30.6 %copy-start.7 = (s32[8]{0:T(128)S(1)}, s32[8]{0:T(128)}, u32[]{:S(2)}) copy-start(s32[8]{0:T(128)} %param.13) | copy-start | bytes 100
  20.8 24.2 %all-to-all-start.1 = ((bf16[16,2,3,64,128]{4,3,2,1,0:T(8,128)(2,1)}), bf16[16,2,3,64,128]{4,3,2,1,0:T(8,128)(2,1)S(1)}, u32[]{:S(2)}, u32[]{:S(2)}) async-start(bf16[16,2,3,64,128]{4,3,2,1,0:T(8,128)(2,1)} %bitcast.6), calls=%async_computation.1 | async-start | bytes 3145728 | tf_op jit(solution)/shard_map/all_to_all | solution.py:104
  45.7 11.5 %collective-permute-start.1 = (bf16[8,3,64,128]{3,2,1,0:T(8,128)(2,1)S(1)}, bf16[8,3,64,128]{3,2,1,0:T(8,128)(2,1)S(1)}, u32[]{:S(2)}, u32[]{:S(2)}) collective-permute-start(bf16[8,3,64,128]{3,2,1,0:T(8,128)(2,1)S(1)} %gather_fusion.2), channel_id=1, source_target_pairs={{1,0},{2,1},{3,2},{4,3},{5,4},{6,5},{7,6},{8,7},{9,8},{10,9},{11,1... | collective-permute-start | bytes 1179656 | tf_op jit(solution)/shard_map/ppermute | solution.py:25
  49.9 7.3 %collective-permute-start = (bf16[8,3,64,128]{3,2,1,0:T(8,128)(2,1)S(1)}, bf16[8,3,64,128]{3,2,1,0:T(8,128)(2,1)S(1)}, u32[]{:S(2)}, u32[]{:S(2)}) collective-permute-start(bf16[8,3,64,128]{3,2,1,0:T(8,128)(2,1)S(1)} %gather_fusion.2), channel_id=1, source_target_pairs={{0,1},{1,2},{2,3},{3,4},{4,5},{5,6},{6,7},{7,8},{8,9},{9,10},{10,1... | collective-permute-start | bytes 1179656 | tf_op jit(solution)/shard_map/ppermute | solution.py:24
  69.0 2.1 %copy-start.4 = (bf16[49,128]{1,0:T(8,128)(2,1)S(1)}, bf16[49,128]{1,0:T(8,128)(2,1)}, u32[]{:S(2)}) copy-start(bf16[49,128]{1,0:T(8,128)(2,1)} %param.17) | copy-start | bytes 37636
  69.2 2.2 %copy-start.1 = (bf16[8,3,64,128]{3,2,1,0:T(8,128)(2,1)S(1)}, bf16[8,3,64,128]{3,2,1,0:T(8,128)(2,1)}, u32[]{:S(2)}) copy-start(bf16[8,3,64,128]{3,2,1,0:T(8,128)(2,1)} %param.12) | copy-start | bytes 1179652
  70.1 2.9 %copy-start.6 = (s32[8,1]{0,1:T(1,128)S(1)}, s32[8,1]{0,1:T(1,128)}, u32[]{:S(2)}) copy-start(s32[8,1]{0,1:T(1,128)} %param.14) | copy-start | bytes 100
  70.1 2.9 %copy-start.10 = (s32[8]{0:T(128)S(1)}, s32[8]{0:T(128)}, u32[]{:S(2)}) copy-start(s32[8]{0:T(128)} %param.15) | copy-start | bytes 100
  71.0 8.1 %copy-start.3 = (bf16[3,3,256,256]{3,2,1,0:T(8,128)(2,1)S(1)}, bf16[3,3,256,256]{3,2,1,0:T(8,128)(2,1)}, u32[]{:S(2)}) copy-start(bf16[3,3,256,256]{3,2,1,0:T(8,128)(2,1)} %param.18) | copy-start | bytes 3538948
  71.5 7.6 %collective-permute-start.2 = (bf16[8,2,64,256]{3,2,1,0:T(8,128)(2,1)S(1)}, bf16[8,2,64,256]{3,2,1,0:T(8,128)(2,1)S(1)}, u32[]{:S(2)}, u32[]{:S(2)}) collective-permute-start(bf16[8,2,64,256]{3,2,1,0:T(8,128)(2,1)S(1)} %get-tuple-element.66), channel_id=1, source_target_pairs={{0,1},{1,2},{2,3},{3,4},{4,5},{5,6},{6,7},{7,8},{8,9},{9,10},{10,1... | collective-permute-start | bytes 1572872 | tf_op jit(solution)/shard_map/ppermute | solution.py:24
  73.0 8.9 %collective-permute-start.3 = (bf16[8,2,64,256]{3,2,1,0:T(8,128)(2,1)S(1)}, bf16[8,2,64,256]{3,2,1,0:T(8,128)(2,1)S(1)}, u32[]{:S(2)}, u32[]{:S(2)}) collective-permute-start(bf16[8,2,64,256]{3,2,1,0:T(8,128)(2,1)S(1)} %get-tuple-element.67), channel_id=1, source_target_pairs={{1,0},{2,1},{3,2},{4,3},{5,4},{6,5},{7,6},{8,7},{9,8},{10,9},{11,1... | collective-permute-start | bytes 1572872 | tf_op jit(solution)/shard_map/ppermute | solution.py:25
  87.5 1.1 copy-start.2
  91.7 1.3 %copy-start.5 = (bf16[128,24]{0,1:T(8,128)(2,1)S(1)}, bf16[128,24]{0,1:T(8,128)(2,1)}, u32[]{:S(2)}) copy-start(bf16[128,24]{0,1:T(8,128)(2,1)} %param.20) | copy-start | bytes 18436
  93.0 0.8 copy-start.11
  93.4 12.1 %copy-start.9 = (s32[8]{0:T(128)S(1)}, s32[8]{0:T(128)}, u32[]{:S(2)}) copy-start(s32[8]{0:T(128)} %copy-done.8) | copy-start | bytes 100
  95.7 18.8 %all-to-all-start.2 = ((f32[16,8,144]{2,1,0:T(8,128)}), f32[16,8,144]{2,1,0:T(8,128)S(1)}, u32[]{:S(2)}, u32[]{:S(2)}) async-start(f32[16,8,144]{2,1,0:T(8,128)} %broadcast_in_dim.26), calls=%async_computation.2 | async-start | bytes 262144 | tf_op jit(solution)/shard_map/all_to_all | solution.py:40
  115.8 9.9 %all-to-all-start.3 = ((f32[16,2,72]{2,1,0:T(2,128)}), f32[16,2,72]{2,1,0:T(2,128)S(1)}, u32[]{:S(2)}, u32[]{:S(2)}) async-start(f32[16,2,72]{2,1,0:T(2,128)} %bitcast.122), calls=%async_computation.3 | async-start | bytes 32768 | tf_op jit(solution)/shard_map/all_to_all | solution.py:162

commit v2 on v0

v2 whole, which is shorter than its diff:
```python
import jax
import jax.numpy as jnp
import numpy as np
from jax import lax
from jax.experimental import pallas as pl
from jax.experimental.pallas import tpu as pltpu
from jax.sharding import PartitionSpec as P

MAPH = 48
MAPW = 64
WINDOW = 7
RADIUS = WINDOW // 2
BAND = 3
CHIP = 2 * BAND
POSE = 12
F32 = jnp.float32
BF16 = jnp.bfloat16

DOWN_TILES = [(-3, 0), (-2, 0), (-1, 0), (-1, 1), (0, 0), (0, 1), (1, 0), (1, 1), (1, 2)]
MID_TILES = [(2, 0), (2, 1), (2, 2), (3, 0), (3, 1), (3, 2)]
UP_TILES = [(4, 0), (4, 1), (4, 2), (5, 1), (5, 2), (6, 1), (6, 2), (7, 2), (8, 2)]


def window_selector():
    chosen = np.zeros((256, CHIP + 4, WINDOW * WINDOW), np.float32)

    def fill(base, tiles, rows, moved):
        for p, (row, pair) in enumerate(tiles):
            mine = row + moved
            if mine not in rows:
                continue
            for half in range(2):
                a = 2 * pair + half - row
                if abs(a) > RADIUS:
                    continue
                for d in range(WINDOW):
                    b = RADIUS - d
                    chosen[base + 64 * half + WINDOW * p + d, mine + 2, (a + RADIUS) * WINDOW + b + RADIUS] = 1.0

    fill(0, DOWN_TILES, range(-2, 2), 0)
    fill(0, MID_TILES, range(2, 4), 0)
    fill(0, UP_TILES, range(4, 8), 0)
    fill(128, UP_TILES, range(-2, 3), -CHIP)
    fill(128, DOWN_TILES, range(3, 8), CHIP)
    return chosen


def turned_order():
    turn = np.zeros((2 * MAPW, 2 * MAPW), np.float32)
    for half in range(2):
        for pixel in range(MAPW):
            turn[(64 * half + 63 - pixel + 68) % 128, 64 * half + pixel] = 1.0
    return turn


def spread_selector():
    spread = np.zeros((3, 128, 384), np.float32)
    for part, base in enumerate((0, 6, 22)):
        for y in range(6):
            spread[part, base + y, [c for c in range(144) if c % 6 == y]] = 1.0
            spread[part, base + y, [256 + c for c in range(36) if c % 6 == y]] = 1.0
    return spread


def request_kernel(owner_ref, target_ref, source_ref, out_ref, slot_ref):
    total = target_ref.shape[0]
    rows = lax.broadcasted_iota(jnp.int32, (16, 128), 0)
    lanes = lax.broadcasted_iota(jnp.int32, (16, 128), 1)
    table = jnp.zeros((16, 128), jnp.int32)
    owners = [owner_ref[e] for e in range(total)]
    for e in range(total):
        owner = owners[e]
        rank = jnp.int32(0)
        for f in range(e):
            rank = rank + jnp.where(owners[f] == owner, 1, 0)
        slot_ref[e] = owner * 2 + rank
        table = jnp.where((rows == owner) & (lanes == rank), target_ref[e], table)
        table = jnp.where((rows == owner) & (lanes == rank + 2), source_ref[e], table)
    out_ref[:, 0, :] = table


def run_all(copies):
    for c in copies:
        c.start()
    for c in copies:
        c.wait()


def pack_kernel(source_ref, features_ref, hidden_ref, keep_ref, send_ref, sems):
    half = keep_ref.shape[0]
    core = lax.axis_index("tile") % 2
    copies = []
    for n, (ref, first) in enumerate(((keep_ref, half * core), (send_ref, half * (1 - core)))):
        for e in range(half):
            edge = first + e
            copies.append(
                pltpu.make_async_copy(
                    features_ref.at[source_ref[edge]], ref.at[e, pl.ds(0, BAND)], sems.at[n, e, 0]
                )
            )
            copies.append(
                pltpu.make_async_copy(
                    hidden_ref.at[edge], ref.at[e, pl.ds(BAND, BAND)], sems.at[n, e, 1]
                )
            )
    run_all(copies)


def pick_kernel(slot_ref, maps_ref, keep_ref, send_ref, sems):
    half = send_ref.shape[0]
    core = lax.axis_index("tile") % 2
    copies = []
    for n, (ref, first) in enumerate(((send_ref, half * (1 - core)), (keep_ref, half * core))):
        for e in range(half):
            copies.append(
                pltpu.make_async_copy(maps_ref.at[slot_ref[first + e]], ref.at[e], sems.at[n, e])
            )
    run_all(copies)


def spread_columns(wide, pixel, row, value, base):
    at = slice(MAPW * row, MAPW * (row + 1))
    wide[at, base + 128 : base + 256] = value.astype(BF16)
    left = jnp.where(pixel == 0, 0.0, pltpu.roll(value, 1, 0))
    wide[at, base : base + 128] = left.astype(BF16)
    right = jnp.where(pixel == MAPW - 1, 0.0, pltpu.roll(value, MAPW - 1, 0))
    wide[at, base + 256 : base + 384] = right.astype(BF16)


def place_bands(bands, refs, e, rows, core):
    keep_ref, came_ref, ring_ref, cross_ref = refs
    for ref, band in (
        (keep_ref, 1 + core),
        (came_ref, 2 - core),
        (ring_ref, 3 * (1 - core)),
        (cross_ref, 3 * core),
    ):
        bands[pl.ds(band, 1)] = ref[e, rows][None]


def prepare_kernel(keep_ref, came_ref, ring_ref, cross_ref, gate_ref, state_ref, part_ref, bands, slabs):
    tile = lax.axis_index("tile")
    has_above = jnp.where(tile < 2, 0.0, 1.0).astype(F32)
    has_below = jnp.where(tile >= lax.axis_size("tile") - 2, 0.0, 1.0).astype(F32)
    pixel = lax.broadcasted_iota(jnp.int32, (MAPW, 128), 0)
    span = (CHIP + 2) * MAPW
    refs = (keep_ref, came_ref, ring_ref, cross_ref)
    for e in range(keep_ref.shape[0]):
        wide, rows = slabs.at[e], bands.at[e]
        place_bands(rows, refs, e, slice(BAND, CHIP), tile % 2)
        for row in range(CHIP + 4):
            state = rows[(row + 1) // BAND, (row + 1) % BAND].astype(F32)
            if row < 2:
                state = state * has_above
            if row >= 8:
                state = state * has_below
            state_ref[e, row] = state.astype(BF16)
            spread_columns(wide, pixel, row, state, 0)
        part_ref[e] = (
            jnp.dot(wide[0:span], gate_ref[0, 0:384], preferred_element_type=F32)
            + jnp.dot(wide[MAPW : MAPW + span], gate_ref[1, 0:384], preferred_element_type=F32)
            + jnp.dot(wide[2 * MAPW : 2 * MAPW + span], gate_ref[2, 0:384], preferred_element_type=F32)
        )


def corr_kernel(
    keep_ref,
    side_ref,
    ring_ref,
    cross_ref,
    kept_ref,
    came_ref,
    turn_ref,
    down_ref,
    mid_ref,
    up_ref,
    bands,
    tbuf,
):
    core = lax.axis_index("tile") % 2
    lane = lax.broadcasted_iota(jnp.int32, (MAPW, 128), 1) & 63
    pixel = lax.broadcasted_iota(jnp.int32, (MAPW, 128), 0)
    slot = (lane * 37) >> 8
    across = pixel + RADIUS - (lane - WINDOW * slot)
    inside = (across >= 0) & (across < MAPW) & (slot < 9)
    for e in range(keep_ref.shape[0]):
        place_bands(bands.at[e], (keep_ref, side_ref, ring_ref, cross_ref), e, slice(0, BAND), core)
        sources = bands[e].reshape(4 * BAND * MAPW, 128)
        tbuf[e, pl.ds(core, 1)] = kept_ref[e][None]
        tbuf[e, pl.ds(1 - core, 1)] = came_ref[e][None]
        rows = tbuf[e].reshape(CHIP * MAPW, 128)
        products = []
        for q in range(3):
            near = sources[2 * q * MAPW : (2 * q + 8) * MAPW]
            far = jnp.dot(
                turn_ref[...], rows[128 * q : 128 * (q + 1)], preferred_element_type=F32
            ).astype(BF16)
            products.append(
                lax.dot_general(near, far, (((1,), (1,)), ((), ())), preferred_element_type=F32)
            )
        for ref, tiles in ((down_ref, DOWN_TILES), (mid_ref, MID_TILES), (up_ref, UP_TILES)):
            held = jnp.zeros((MAPW, 128), F32)
            for p, (row, q) in enumerate(tiles):
                at = MAPW * (row + RADIUS - 2 * q)
                turned = pltpu.roll(
                    products[q][at : at + MAPW], WINDOW * p, 1, stride=1, stride_axis=0
                )
                held = jnp.where(slot == p, turned, held)
            ref[e] = jnp.where(inside, held * (128.0**-0.5), 0.0).astype(BF16)


def logistic(x):
    return 0.5 * jnp.tanh(0.5 * x) + 0.5


def update_kernel(
    counts_ref,
    down_ref,
    mid_ref,
    up_ref,
    above_ref,
    below_ref,
    state_ref,
    part_ref,
    window_ref,
    gate_ref,
    cand_ref,
    jac_ref,
    conf_ref,
    kept_ref,
    given_ref,
    sums_ref,
    slabs,
    rows_out,
):
    tile = lax.axis_index("tile")
    core = tile % 2
    half = state_ref.shape[0]
    has_above = jnp.where(tile < 2, 0.0, 1.0).astype(F32)
    has_below = jnp.where(tile >= lax.axis_size("tile") - 2, 0.0, 1.0).astype(F32)
    pixel = lax.broadcasted_iota(jnp.int32, (MAPW, 128), 0)
    total = jnp.zeros((16, 128), F32)
    for e in range(half):
        wide = slabs.at[e]
        used = half * core + e < counts_ref[0]
        above = (above_ref[e].astype(F32) * has_above).astype(BF16)
        below = (below_ref[e].astype(F32) * has_below).astype(BF16)
        down, mid, up = down_ref[e], mid_ref[e], up_ref[e]
        groups = (
            (down, above, 0, 4),
            (mid, above, 4, 1),
            (mid, below, 5, 1),
            (up, below, 6, 4),
        )
        for own, other, start, count in groups:
            lanes = jnp.concatenate([own, other], axis=1)
            motion = jnp.dot(
                lanes,
                window_ref[:, 128 * start : 128 * (start + count)],
                preferred_element_type=F32,
            )
            motion = jnp.maximum(motion, 0.0)
            for n in range(count):
                row = start + n
                part = motion[:, 128 * n : 128 * (n + 1)]
                if row < 2:
                    part = part * has_above
                if row >= 8:
                    part = part * has_below
                spread_columns(wide, pixel, row, part, 384)
        span = (CHIP + 2) * MAPW
        gates = part_ref[e]
        for tap in range(3):
            gates = gates + jnp.dot(
                wide[MAPW * tap : MAPW * tap + span, 384:768],
                gate_ref[tap, 384:768],
                preferred_element_type=F32,
            )
        gates = logistic(gates)
        for row in range(CHIP + 2):
            reset = gates[MAPW * row : MAPW * (row + 1), 128:256]
            spread_columns(wide, pixel, row + 1, reset * state_ref[e, row + 1].astype(F32), 0)
        span = CHIP * MAPW
        candidate = jnp.zeros((span, 128), F32)
        for tap in range(3):
            candidate = candidate + jnp.dot(
                wide[MAPW * (tap + 1) : MAPW * (tap + 1) + span],
                cand_ref[tap],
                preferred_element_type=F32,
            )
        candidate = jnp.tanh(candidate)
        update = gates[MAPW : MAPW + span, 0:128]
        old = state_ref[e, 2 : 2 + CHIP].reshape(span, 128).astype(F32)
        fresh = ((1.0 - update) * old + update * candidate).astype(BF16)
        chosen = jnp.full((span, 128), jnp.where(used, 1, 0)) == 1
        kept = jnp.where(chosen, fresh.astype(F32), old).astype(BF16)
        rows_out[e] = kept.reshape(2, BAND, MAPW, 128)
        kept_ref[e] = rows_out[e, pl.ds(core, 1)][0]
        given_ref[e] = rows_out[e, pl.ds(1 - core, 1)][0]
        jac = jnp.dot(fresh, jac_ref[...], preferred_element_type=F32)
        logit = jnp.dot(fresh, conf_ref[...], preferred_element_type=F32)
        conf = jnp.maximum(logit, 0.0) + jnp.log1p(jnp.exp(-jnp.abs(logit)))
        normal = lax.dot_general(
            (jac * conf).astype(BF16),
            jac.astype(BF16),
            (((0,), (0,)), ((), ())),
            preferred_element_type=F32,
        )
        block = normal[0:16] + pltpu.roll(normal[64:80], 64, 1)
        lane = lax.broadcasted_iota(jnp.int32, (16, 128), 1)
        block = jnp.where(lane < 16, block, 0.0)
        block = block * jnp.where(used, 1.0 / (MAPH * MAPW), 0.0).astype(F32)
        if e:
            block = pltpu.roll(block, 32 * e, 1)
        total = total + block
    for n in range(sums_ref.shape[0]):
        sums_ref[n] = total


def slots_kernel(slot_ref, parts_ref, own_ref, out_ref):
    halves = [parts_ref[h] for h in range(2)]
    for z in range(1, parts_ref.shape[0] // 2):
        for h in range(2):
            halves[h] = halves[h] + parts_ref[2 * z + h]
    out_ref[...] = jnp.zeros_like(out_ref)
    lane = lax.broadcasted_iota(jnp.int32, (16, 128), 1)
    for e in range(8):
        block = halves[e // 4]
        if e % 4:
            block = pltpu.roll(block, 128 - 32 * (e % 4), 1)
        block = jnp.where(lane < 16, block, 0.0)
        own_ref[e] = block
        slot = slot_ref[e]
        rank = slot & 1
        out_ref[slot >> 1] += pltpu.roll(block, 16 * rank, 1)


def split_dot(hits, values):
    upper = values.astype(BF16)
    lower = (values - upper.astype(F32)).astype(BF16)
    return jnp.dot(hits, upper, preferred_element_type=F32) + jnp.dot(
        hits, lower, preferred_element_type=F32
    )


def dot_split(values, hits):
    upper = values.astype(BF16)
    lower = (values - upper.astype(F32)).astype(BF16)
    return jnp.dot(upper, hits, preferred_element_type=F32) + jnp.dot(
        lower, hits, preferred_element_type=F32
    )


def place_kernel(own_ref, came_ref, spread_ref, rows_ref, cols_ref, frames_ref, within_ref, hess_ref, diag_ref):
    own = own_ref[...].reshape(128, 128)
    came = came_ref[...].reshape(256, 128)
    values = jnp.concatenate(
        [
            dot_split(own, spread_ref[0]),
            dot_split(came, spread_ref[1]),
            dot_split(came, spread_ref[2]),
        ],
        axis=0,
    )
    hess_ref[...] = split_dot(rows_ref[...], values[:, 0:144] * cols_ref[...])
    diag_ref[...] = split_dot(frames_ref[...], values[:, 256:292] * within_ref[...])


def per_device(
    features,
    hidden_state,
    edge_source,
    edge_owner,
    edge_target,
    edge_counts,
    corr_weight,
    gate_weight,
    candidate_weight,
    jacobian_weight,
    confidence_weight,
):
    edge_total = hidden_state.shape[0]
    half = edge_total // 2
    frame_total = features.shape[0]
    channels = features.shape[3]
    owner_count = lax.axis_size("edge")
    tile_count = lax.axis_size("tile")
    my_index = lax.axis_index("edge")
    tile = lax.axis_index("tile")
    core = tile % 2
    band_shape = features.shape[1:]
    smem = pl.BlockSpec(memory_space=pltpu.SMEM)
    vmem = pl.BlockSpec(memory_space=pltpu.VMEM)
    anywhere = pl.BlockSpec(memory_space=pltpu.HBM)
    beside = [(i, i ^ 1) for i in range(tile_count)]
    ring_pairs = [(i, (i + (2 if i % 2 else -2)) % tile_count) for i in range(tile_count)]
    cross_pairs = [(i, (i + (1 if i % 2 else -1)) % tile_count) for i in range(tile_count)]
    onward = [(i, (i + 2) % tile_count) for i in range(tile_count)]
    backward = [((i + 2) % tile_count, i) for i in range(tile_count)]

    requests, slot_index = pl.pallas_call(
        request_kernel,
        out_shape=(
            jax.ShapeDtypeStruct((owner_count, 1, 128), jnp.int32),
            jax.ShapeDtypeStruct((edge_total,), jnp.int32),
        ),
        in_specs=[smem, smem, smem],
        out_specs=(vmem, smem),
        name="requests",
    )(edge_owner.reshape(-1), edge_target, edge_source)
    requests, pack_source = lax.optimization_barrier((requests, edge_source))
    got = lax.all_to_all(requests, "edge", split_axis=0, concat_axis=0, tiled=True)
    keep, send = pl.pallas_call(
        pack_kernel,
        out_shape=(jax.ShapeDtypeStruct((half, CHIP) + band_shape[1:], BF16),) * 2,
        in_specs=[smem, anywhere, anywhere],
        out_specs=(vmem, vmem),
        scratch_shapes=[pltpu.SemaphoreType.DMA((2, half, 2))],
        name="pack",
    )(pack_source, features, hidden_state)
    got, keep, send = lax.optimization_barrier((got, keep, send))
    came = lax.ppermute(send, "tile", beside)
    ring = lax.ppermute(keep, "tile", ring_pairs)
    cross = lax.ppermute(send, "tile", cross_pairs)
    asked = jnp.take(features, got[:, 0, 0:2].reshape(-1), axis=0, mode="clip")
    returned = lax.all_to_all(
        asked.reshape((owner_count, 2) + band_shape), "edge", split_axis=0, concat_axis=0, tiled=True
    ).reshape((2 * owner_count,) + band_shape)
    corr_w, gate_w, cand_w = corr_weight, gate_weight, candidate_weight
    jac_w, conf_w = jacobian_weight, confidence_weight
    sources = edge_source
    window = jnp.einsum(
        "lrd,dc->lrc", jnp.asarray(window_selector(), BF16), corr_w, preferred_element_type=F32
    ).astype(BF16).reshape(256, (CHIP + 4) * 128)
    gate_w = jnp.concatenate(
        [gate_w[:, :, :channels].reshape(3, 384, 256), gate_w[:, :, channels:].reshape(3, 384, 256)],
        axis=1,
    )
    cand_w = jnp.concatenate(
        [cand_w[:, :, :channels].reshape(3, 384, 128), cand_w[:, :, channels:].reshape(3, 384, 128)],
        axis=1,
    )
    gap = jnp.zeros((channels, 64 - POSE), BF16)
    jac_w = jnp.concatenate([jac_w[:, :POSE], gap, jac_w[:, POSE:], gap], axis=1)
    conf_w = jnp.concatenate(
        [
            jnp.broadcast_to(conf_w[:, 0:1], (channels, POSE)),
            gap,
            jnp.broadcast_to(conf_w[:, 1:2], (channels, POSE)),
            gap,
        ],
        axis=1,
    )
    state_rows, gate_part = pl.pallas_call(
        prepare_kernel,
        out_shape=(
            jax.ShapeDtypeStruct((half, CHIP + 4, MAPW, 128), BF16),
            jax.ShapeDtypeStruct((half, (CHIP + 2) * MAPW, 256), F32),
        ),
        in_specs=[vmem] * 5,
        out_specs=(vmem,) * 2,
        scratch_shapes=[
            pltpu.VMEM((half, 4, BAND, MAPW, 128), BF16),
            pltpu.VMEM((half, (CHIP + 4) * MAPW, 384), BF16),
        ],
        compiler_params=pltpu.CompilerParams(vmem_limit_bytes=16 * 1024 * 1024),
        name="prepare",
    )(keep, came, ring, cross, gate_w)
    x = np.arange(16)
    asked_target, asked_source = got[:, 0, 0:2], got[:, 0, 2:4]
    other_group = jnp.arange(owner_count)[:, None] * frame_total + asked_source
    source_global = my_index * frame_total + sources
    target_global = edge_owner[:, 0] * frame_total + edge_target

    def by_row(upper, lower):
        return jnp.where(x[None, :] < 6, upper[:, None], lower[:, None]).reshape(-1)

    def each_row(value):
        return jnp.broadcast_to(value[:, None], (value.shape[0], 16)).reshape(-1)

    row_frame = jnp.concatenate(
        [by_row(source_global, target_global)]
        + [
            by_row(other_group[:, q], my_index * frame_total + asked_target[:, q])
            for q in range(2)
        ]
    )
    col_frame = jnp.concatenate([each_row(sources), each_row(asked_target[:, 0]), each_row(asked_target[:, 1])])
    stack = edge_total * 16 + 2 * owner_count * 16
    xs = np.tile(x, stack // 16)
    real = xs < POSE
    on_diagonal = row_frame == my_index * frame_total + col_frame
    own_rows = 6 * frame_total * owner_count // tile_count
    row_place = row_frame * 6 + xs % 6 - tile * own_rows
    row_place = jnp.where(real & ~on_diagonal, row_place, -1)
    diag_place = jnp.where(real & on_diagonal, col_frame, -1)
    row_hits = (jnp.arange(own_rows)[:, None] == row_place[None, :]).astype(BF16)
    diag_hits = (jnp.arange(frame_total)[:, None] == diag_place[None, :]).astype(BF16)
    col_hits = (col_frame[:, None] == (np.arange(6 * frame_total) // 6)[None, :]).astype(F32)
    within = jnp.asarray((xs[:, None] % 6 == np.arange(36)[None, :] // 6).astype(np.float32))

    kept_maps, sent_maps = pl.pallas_call(
        pick_kernel,
        out_shape=(jax.ShapeDtypeStruct((half,) + band_shape, BF16),) * 2,
        in_specs=[smem, anywhere],
        out_specs=(vmem, vmem),
        scratch_shapes=[pltpu.SemaphoreType.DMA((2, half))],
        name="pick",
    )(slot_index, returned)
    came_maps = lax.ppermute(sent_maps, "tile", beside)
    turn = jnp.asarray(turned_order(), BF16)
    down, mid, up = pl.pallas_call(
        corr_kernel,
        out_shape=(jax.ShapeDtypeStruct((half, MAPW, 128), BF16),) * 3,
        in_specs=[vmem] * 7,
        out_specs=(vmem,) * 3,
        scratch_shapes=[
            pltpu.VMEM((half, 4, BAND, MAPW, channels), BF16),
            pltpu.VMEM((half, 2, BAND, MAPW, channels), BF16),
        ],
        compiler_params=pltpu.CompilerParams(vmem_limit_bytes=16 * 1024 * 1024),
        name="windows",
    )(keep, came, ring, cross, kept_maps, came_maps, turn)
    up_came = lax.ppermute(up, "tile", onward)
    down_came = lax.ppermute(down, "tile", backward)
    kept, given, sums = pl.pallas_call(
        update_kernel,
        out_shape=(
            jax.ShapeDtypeStruct((half, BAND, MAPW, 128), BF16),
            jax.ShapeDtypeStruct((half, BAND, MAPW, 128), BF16),
            jax.ShapeDtypeStruct((tile_count, 16, 128), F32),
        ),
        in_specs=[smem] + [vmem] * 12,
        out_specs=(vmem,) * 3,
        scratch_shapes=[
            pltpu.VMEM((half, (CHIP + 4) * MAPW, 768), BF16),
            pltpu.VMEM((half, 2, BAND, MAPW, 128), BF16),
        ],
        compiler_params=pltpu.CompilerParams(vmem_limit_bytes=24 * 1024 * 1024),
        name="update",
    )(
        edge_counts,
        down,
        mid,
        up,
        up_came,
        down_came,
        state_rows,
        gate_part,
        window,
        gate_w,
        cand_w,
        jac_w,
        conf_w,
    )
    parts = lax.all_to_all(sums, "tile", split_axis=0, concat_axis=0, tiled=True)
    given_came = lax.ppermute(given, "tile", beside)
    hidden_next = jnp.where(
        core == 0,
        jnp.concatenate([kept, given_came], axis=0),
        jnp.concatenate([given_came, kept], axis=0),
    )
    own_blocks, outgoing = pl.pallas_call(
        slots_kernel,
        out_shape=(
            jax.ShapeDtypeStruct((edge_total, 16, 128), F32),
            jax.ShapeDtypeStruct((owner_count, 16, 128), F32),
        ),
        in_specs=[smem, vmem],
        out_specs=(vmem, vmem),
        name="slots",
    )(slot_index, parts)
    incoming = lax.all_to_all(outgoing, "edge", split_axis=0, concat_axis=0, tiled=True)
    camera_hessian, pose_diagonal = pl.pallas_call(
        place_kernel,
        out_shape=(
            jax.ShapeDtypeStruct((own_rows, 6 * frame_total), F32),
            jax.ShapeDtypeStruct((frame_total, 36), F32),
        ),
        in_specs=[vmem] * 7,
        out_specs=(vmem, vmem),
        name="place",
    )(own_blocks, incoming, jnp.asarray(spread_selector(), BF16), row_hits, col_hits, diag_hits, within)
    return (hidden_next, camera_hessian, pose_diagonal)


def solution(mesh):
    placed = (
        P("edge", "tile", None, None),
        P("edge", "tile", None, None),
        P("edge"),
        P("edge", None),
        P("edge"),
        P("edge"),
        P(),
        P(),
        P(),
        P(),
        P(),
    )
    return jax.shard_map(
        per_device,
        mesh=mesh,
        in_specs=placed,
        out_specs=(P("edge", "tile", None, None), P("tile", "edge"), P("edge", None)),
        check_vma=False,
    )
```

time: 145 us -> 109 us (0.75)
  blocking collectives: 34.1 us -> 0 us
  Pallas kernels: 0 us -> 27.7 us
  other arithmetic: 23.1 us -> 4.19 us
  starting transfers between devices: 22.1 us -> 39 us
  matrix products: 16.8 us -> 0.38 us
  waiting for transfers between devices: 37.7 us -> 27.4 us
    pallas_call x0 -> x8, Pallas kernels: none -> 27.7 us  [the longest x1 10.4 us: per_device(): pl.pallas_call(update_kernel, out_shape=(jax.ShapeDtypeStruct((half, BAND...]
    all_gather x1 -> x0, blocking collectives: 20.3 us -> none  [total_of_pieces(): parts = lax.all_gather(shard, axis)]
    dot_general x25 -> x1, matrix products: 16.8 us -> 0.38 us  [per_device(): jnp.einsum('lrd,dc->lrc', jnp.asarray(window_selector(), BF16), corr_w, p...]
    all_to_all x2 -> x4, starting transfers between devices: 7.33 us -> 23.7 us  [the longest x1 7.6 us: per_device(): lax.all_to_all(requests, 'edge', split_axis=0, concat_axis=0, tiled=True)]
    all_to_all x1 -> x0, blocking collectives: 13.8 us -> none  [sent_together(): lax.all_to_all(both, axis, split_axis=split_dim, concat_axis=concat_dim,...]
    ppermute x4 -> x7, waiting for transfers between devices: 13.8 us -> 1.25 us  [the longest x1 1.24 us: per_device(): came_maps = lax.ppermute(sent_maps, 'tile', beside)]
    unnamed x4 -> x2, other arithmetic: 11.5 us -> 0.01 us
    concatenate x4 -> x3, other arithmetic: 3.36 us -> 0.23 us  [the longest x1 0.11 us: per_device(): jnp.concatenate([jnp.broadcast_to(conf_w[:, 0:1], (channels, POSE)), gap,...]
  transfers between devices with their start and end apart: 6 -> 11, of which waited for: 6 -> 5; matrix products, arithmetic and copies ran while one was open for 2% -> 7% of each run, Pallas kernels for 0% -> 9%
where the time goes in v2:
time: 109 us; the launch traced here: 108 us
  starting transfers between devices  39 us (36%)
  Pallas kernels  27.7 us (25%)
  waiting for transfers between devices  27.4 us (25%)
  local copies, waits for them, and re-layouts  8.11 us (7%)
  other arithmetic  4.19 us (4%)
  between operations  1.73 us (2%)
    all_to_all x1, waiting for transfers between devices, per_device(): lax.all_to_all(asked.reshape((owner_count, 2) + band_shape), 'edge', spli...  12.8 us
    pallas_call x1, Pallas kernels, per_device(): pl.pallas_call(update_kernel, out_shape=(jax.ShapeDtypeStruct((half, BAND...  10.4 us
    all_to_all x1, starting transfers between devices, per_device(): lax.all_to_all(requests, 'edge', split_axis=0, concat_axis=0, tiled=True)  7.6 us
    all_to_all x1, waiting for transfers between devices, per_device(): lax.all_to_all(sums, 'tile', split_axis=0, concat_axis=0, tiled=True)  7.36 us
    all_to_all x1, starting transfers between devices, per_device(): lax.all_to_all(asked.reshape((owner_count, 2) + band_shape), 'edge', spli...  6.38 us
    all_to_all x1, starting transfers between devices, per_device(): lax.all_to_all(sums, 'tile', split_axis=0, concat_axis=0, tiled=True)  6.23 us
    all_to_all x1, waiting for transfers between devices, per_device(): lax.all_to_all(outgoing, 'edge', split_axis=0, concat_axis=0, tiled=True)  5.74 us
    ppermute x1, starting transfers between devices, per_device(): came_maps = lax.ppermute(sent_maps, 'tile', beside)  4.37 us
  transfers between devices with their start and end apart: 11, of which 5 were waited for; matrix products, arithmetic and copies ran while one was open for 7% of the time, Pallas kernels for 9%

profile of v2, /device:TPU:1, one launch (start us, length us, event | category | flops | bytes accessed | tf_op | source)
XLA Modules:
  0.0 108.5 jit_solution(1159947602862349056)
XLA Ops:
  0.7 1.5 %requests.1 = (s32[16,1,128]{2,1,0:T(1,128)}, s32[8]{0:T(128)}) custom-call(s32[8]{0:T(128)} %bitcast.38, s32[8]{0:T(128)} %target_ref.1, s32[8]{0:T(128)} %source_ref.2), custom_call_target="tpu_custom_call" | custom-call | tf_op jit(solution)/shard_map/requests/pallas_call | solution.py:401
  2.2 7.6 %all-to-all-start = ((s32[16,1,128]{2,1,0:T(1,128)}), s32[16,1,128]{2,1,0:T(1,128)S(1)}, u32[]{:S(2)}, u32[]{:S(2)}) async-start(s32[16,1,128]{2,1,0:T(1,128)} %get-tuple-element.27), calls=%async_computation | async-start | bytes 16384 | tf_op jit(solution)/shard_map/all_to_all | solution.py:412
  9.8 0.7 multiply_add_fusion
  10.5 1.1 %fusion.6 = (bf16[3,3,128,128]{3,2,1,0:T(8,128)(2,1)S(1)}, bf16[3,3,128,128]{3,2,1,0:T(8,128)(2,1)S(1)}) fusion(bf16[3,3,256,128]{3,2,1,0:T(8,128)(2,1)} %param.29), kind=kLoop, calls=%fused_computation.44 | loop fusion | bytes 1179648 | tf_op jit(solution)/shard_map/slice | solution.py:440
  11.6 0.1 copy.30
  11.8 0.1 copy.29
  12.0 0.1 reshape.74
  12.1 0.4 convolution_convert_fusion
  12.6 0.1 broadcast_in_dim.138
  12.6 0.1 broadcast_in_dim.136
  12.7 0.1 pad_maximum_fusion.2
  13.0 2.8 %pack.1 = (bf16[4,6,64,128]{3,2,1,0:T(8,128)(2,1)}, bf16[4,6,64,128]{3,2,1,0:T(8,128)(2,1)}) custom-call(s32[8]{0:T(128)} %source_ref.2, bf16[24,3,64,128]{3,2,1,0:T(8,128)(2,1)} %features_ref.1, bf16[8,3,64,128]{3,2,1,0:T(8,128)(2,1)} %hidden_ref.1), custom_call_target="tpu_custom_call" | custom-call | tf_op jit(solution)/shard_map/pack/pallas_call | solution.py:413
  15.8 0.3 all-to-all-done
  16.1 0.1 fusion.7
  16.2 0.1 reshape.79
  16.3 1.9 %gather_fusion = bf16[32,3,64,128]{3,2,1,0:T(8,128)(2,1)} fusion(bf16[24,3,64,128]{3,2,1,0:T(8,128)(2,1)S(1)} %copy-done.4, s32[1024]{0:T(1024)S(1)} %pad_clamp_fusion), kind=kCustom, calls=%fused_computation | custom fusion | bytes 3145856 | tf_op jit(solution)/shard_map/jit(_take)/gather | solution.py:425
  18.2 6.4 %all-to-all-start.1 = ((bf16[16,2,3,64,128]{4,3,2,1,0:T(8,128)(2,1)}), bf16[16,2,3,64,128]{4,3,2,1,0:T(8,128)(2,1)}, u32[]{:S(2)}, u32[]{:S(2)}) async-start(bf16[16,2,3,64,128]{4,3,2,1,0:T(8,128)(2,1)} %bitcast.1), calls=%async_computation.1 | async-start | bytes 3145728 | tf_op jit(solution)/shard_map/all_to_all | solution.py:426
  25.3 0.2 copy.31.window_ref
  25.6 0.9 copy-done.5
  26.8 1.6 %collective-permute-start = (bf16[4,6,64,128]{3,2,1,0:T(8,128)(2,1)}, bf16[4,6,64,128]{3,2,1,0:T(8,128)(2,1)S(1)}, u32[]{:S(2)}, u32[]{:S(2)}) collective-permute-start(bf16[4,6,64,128]{3,2,1,0:T(8,128)(2,1)} %get-tuple-element.32), channel_id=1, source_target_pairs={{0,1},{1,0},{2,3},{3,2},{4,5},{5,4},{6,7},{7,6},{8,9},{9,8},{10,11... | collective-permute-start | bytes 1179656 | tf_op jit(solution)/shard_map/ppermute | solution.py:422
  28.4 1.6 %collective-permute-start.2 = (bf16[4,6,64,128]{3,2,1,0:T(8,128)(2,1)}, bf16[4,6,64,128]{3,2,1,0:T(8,128)(2,1)}, u32[]{:S(2)}, u32[]{:S(2)}) collective-permute-start(bf16[4,6,64,128]{3,2,1,0:T(8,128)(2,1)} %get-tuple-element.32), channel_id=1, source_target_pairs={{0,15},{1,2},{2,1},{3,4},{4,3},{5,6},{6,5},{7,8},{8,7},{9,10},{10,... | collective-permute-start | bytes 1179656 | tf_op jit(solution)/shard_map/ppermute | solution.py:424
  30.0 1.6 %collective-permute-start.1 = (bf16[4,6,64,128]{3,2,1,0:T(8,128)(2,1)S(1)}, bf16[4,6,64,128]{3,2,1,0:T(8,128)(2,1)}, u32[]{:S(2)}, u32[]{:S(2)}) collective-permute-start(bf16[4,6,64,128]{3,2,1,0:T(8,128)(2,1)S(1)} %copy-done.1), channel_id=1, source_target_pairs={{0,14},{1,3},{2,0},{3,5},{4,2},{5,7},{6,4},{7,9},{8,6},{9,11},{10,... | collective-permute-start | bytes 1179656 | tf_op jit(solution)/shard_map/ppermute | solution.py:423
  31.9 0.1 reshape.75
  32.0 0.1 reshape.76
  32.2 0.1 select_n.51
  32.4 12.8 %all-to-all-done.1 = bf16[16,2,3,64,128]{4,3,2,1,0:T(8,128)(2,1)} async-done(((bf16[16,2,3,64,128]{4,3,2,1,0:T(8,128)(2,1)}), bf16[16,2,3,64,128]{4,3,2,1,0:T(8,128)(2,1)}, u32[]{:S(2)}, u32[]{:S(2)}) %all-to-all-start.1) | async-done | bytes 1572896 | tf_op jit(solution)/shard_map/all_to_all | solution.py:426
  45.1 2.4 %pick.1 = (bf16[4,3,64,128]{3,2,1,0:T(8,128)(2,1)}, bf16[4,3,64,128]{3,2,1,0:T(8,128)(2,1)}) custom-call(s32[8]{0:T(128)} %get-tuple-element.33.slot_ref, bf16[32,3,64,128]{3,2,1,0:T(8,128)(2,1)} %bitcast.2.maps_ref), custom_call_target="tpu_custom_call" | custom-call | tf_op jit(solution)/shard_map/pick/pallas_call | solution.py:502
  47.6 4.4 %collective-permute-start.3 = (bf16[4,3,64,128]{3,2,1,0:T(8,128)(2,1)}, bf16[4,3,64,128]{3,2,1,0:T(8,128)(2,1)S(1)}, u32[]{:S(2)}, u32[]{:S(2)}) collective-permute-start(bf16[4,3,64,128]{3,2,1,0:T(8,128)(2,1)} %get-tuple-element.36), channel_id=1, source_target_pairs={{0,1},{1,0},{2,3},{3,2},{4,5},{5,4},{6,7},{7,6},{8,9},{9,8},{10,11... | collective-permute-start | bytes 589832 | tf_op jit(solution)/shard_map/ppermute | solution.py:510
  52.0 1.2 %collective-permute-done.3.came_ref = bf16[4,3,64,128]{3,2,1,0:T(8,128)(2,1)S(1)} collective-permute-done((bf16[4,3,64,128]{3,2,1,0:T(8,128)(2,1)}, bf16[4,3,64,128]{3,2,1,0:T(8,128)(2,1)S(1)}, u32[]{:S(2)}, u32[]{:S(2)}) %collective-permute-start.3) | collective-permute-done | bytes 196640 | tf_op jit(solution)/shard_map/ppermute | solution.py:510
  53.3 0.9 copy-done.2
  54.2 2.8 %windows.1 = (bf16[4,64,128]{2,1,0:T(8,128)(2,1)S(1)}, bf16[4,64,128]{2,1,0:T(8,128)(2,1)S(1)}, bf16[4,64,128]{2,1,0:T(8,128)(2,1)S(1)}) custom-call(bf16[4,6,64,128]{3,2,1,0:T(8,128)(2,1)S(1)} %copy-done.1, bf16[4,6,64,128]{3,2,1,0:T(8,128)(2,1)S(1)} %collective-permute-done.side_ref.came_ref, bf16[4,6,64,128]{3,2,1,0:T(8,128)(2,1)} %collective-permute-done.1.ring_ref, ...), custom_call_target="tpu_custom_call" | custom-call | tf_op jit(solution)/shard_map/windows/pallas_call | solution.py:512
  57.0 1.7 %collective-permute-start.4 = (bf16[4,64,128]{2,1,0:T(8,128)(2,1)S(1)}, bf16[4,64,128]{2,1,0:T(8,128)(2,1)S(1)}, u32[]{:S(2)}, u32[]{:S(2)}) collective-permute-start(bf16[4,64,128]{2,1,0:T(8,128)(2,1)S(1)} %get-tuple-element.39.up_ref), channel_id=1, source_target_pairs={{0,2},{1,3},{2,4},{3,5},{4,6},{5,7},{6,8},{7,9},{8,10},{9,11},{10,... | collective-permute-start | bytes 196616 | tf_op jit(solution)/shard_map/ppermute | solution.py:524
  58.8 4.2 %collective-permute-start.5 = (bf16[4,64,128]{2,1,0:T(8,128)(2,1)S(1)}, bf16[4,64,128]{2,1,0:T(8,128)(2,1)S(1)}, u32[]{:S(2)}, u32[]{:S(2)}) collective-permute-start(bf16[4,64,128]{2,1,0:T(8,128)(2,1)S(1)} %get-tuple-element.37.down_ref), channel_id=1, source_target_pairs={{2,0},{3,1},{4,2},{5,3},{6,4},{7,5},{8,6},{9,7},{10,8},{11,9},{12,... | collective-permute-start | bytes 196616 | tf_op jit(solution)/shard_map/ppermute | solution.py:525
  63.0 3.1 %prepare.1 = (bf16[4,10,64,128]{3,2,1,0:T(8,128)(2,1)S(1)}, f32[4,512,256]{2,1,0:T(8,128)S(1)}) custom-call(bf16[4,6,64,128]{3,2,1,0:T(8,128)(2,1)S(1)} %copy-done.1, bf16[4,6,64,128]{3,2,1,0:T(8,128)(2,1)S(1)} %collective-permute-done.side_ref.came_ref, bf16[4,6,64,128]{3,2,1,0:T(8,128)(2,1)} %collective-permute-done.1.ring_ref, ...), custom_call_target="tpu_custom_call" | custom-call | tf_op jit(solution)/shard_map/prepare/pallas_call | solution.py:454
  66.1 10.4 %update.1 = (bf16[4,3,64,128]{3,2,1,0:T(8,128)(2,1)S(1)}, bf16[4,3,64,128]{3,2,1,0:T(8,128)(2,1)S(1)}, f32[16,16,128]{2,1,0:T(8,128)}) custom-call(s32[1]{0:T(128)S(6)} %copy.40.counts_ref, bf16[4,64,128]{2,1,0:T(8,128)(2,1)S(1)} %get-tuple-element.37.down_ref, bf16[4,64,128]{2,1,0:T(8,128)(2,1)S(1)} %get-tuple-element.38.mid_ref, ...), custom_call_target="tpu_custom_call" | custom-call | tf_op jit(solution)/shard_map/update/pallas_call | solution.py:526
  76.5 6.2 %all-to-all-start.2 = ((f32[16,16,128]{2,1,0:T(8,128)}), f32[16,16,128]{2,1,0:T(8,128)S(1)}, u32[]{:S(2)}, u32[]{:S(2)}) async-start(f32[16,16,128]{2,1,0:T(8,128)} %get-tuple-element.44), calls=%async_computation.2 | async-start | bytes 262144 | tf_op jit(solution)/shard_map/all_to_all | solution.py:556
  82.7 0.7 fusion.rows_ref
  83.4 1.0 compare_convert_fusion.cols_ref
  84.4 0.1 collective-permute-start.6
  84.5 7.4 %all-to-all-done.2.parts_ref = f32[16,16,128]{2,1,0:T(8,128)S(1)} async-done(((f32[16,16,128]{2,1,0:T(8,128)}), f32[16,16,128]{2,1,0:T(8,128)S(1)}, u32[]{:S(2)}, u32[]{:S(2)}) %all-to-all-start.2) | async-done | bytes 131104 | tf_op jit(solution)/shard_map/all_to_all | solution.py:556
  91.9 0.7 copy-done.7
  92.5 1.7 %slots.1 = (f32[8,16,128]{2,1,0:T(8,128)}, f32[16,16,128]{2,1,0:T(8,128)}) custom-call(s32[8]{0:T(128)} %get-tuple-element.33.slot_ref, f32[16,16,128]{2,1,0:T(8,128)} %copy-done.7), custom_call_target="tpu_custom_call" | custom-call | tf_op jit(solution)/shard_map/slots/pallas_call | solution.py:563
  94.3 3.5 %all-to-all-start.3 = ((f32[16,16,128]{2,1,0:T(8,128)}), f32[16,16,128]{2,1,0:T(8,128)S(1)}, u32[]{:S(2)}, u32[]{:S(2)}) async-start(f32[16,16,128]{2,1,0:T(8,128)} %get-tuple-element.46), calls=%async_computation.3 | async-start | bytes 262144 | tf_op jit(solution)/shard_map/all_to_all | solution.py:573
  97.8 0.6 fusion.1.frames_ref
  98.4 0.8 maximum_select_fusion
  99.2 5.7 %all-to-all-done.3.came_ref = f32[16,16,128]{2,1,0:T(8,128)S(1)} async-done(((f32[16,16,128]{2,1,0:T(8,128)}), f32[16,16,128]{2,1,0:T(8,128)S(1)}, u32[]{:S(2)}, u32[]{:S(2)}) %all-to-all-start.3) | async-done | bytes 131104 | tf_op jit(solution)/shard_map/all_to_all | solution.py:573
  104.9 0.6 copy-done.6
  105.6 2.9 %place.1 = (f32[144,144]{1,0:T(8,128)}, f32[24,36]{1,0:T(8,128)}) custom-call(f32[8,16,128]{2,1,0:T(8,128)} %get-tuple-element.45.own_ref, f32[16,16,128]{2,1,0:T(8,128)} %copy-done.6, bf16[3,128,384]{2,1,0:T(8,128)(2,1)} %constant.56.clone.spread_ref, bf16[144,640]{1,0:T(8,128)(2,1)} %fusion.rows_ref, f32[640,144]{1,0:T(8,128)} %compare_convert_fusion.cols_ref, ...), custom_call_target="tpu_custom_call" | custom-call | tf_op jit(solution)/shard_map/place/pallas_call | solution.py:574
  (63 shorter events, 1.1 us)
Async XLA Ops:
  0.6 11.4 %copy-start = (bf16[49,128]{1,0:T(8,128)(2,1)S(1)}, bf16[49,128]{1,0:T(8,128)(2,1)}, u32[]{:S(2)}) copy-start(bf16[49,128]{1,0:T(8,128)(2,1)} %param.27) | copy-start | bytes 37636
  0.6 11.4 %copy-start.8 = (bf16[256,10,49]{0,2,1:T(8,128)(2,1)S(1)}, bf16[256,10,49]{0,2,1:T(8,128)(2,1)}, u32[]{:S(2)}) copy-start(bf16[256,10,49]{0,2,1:T(8,128)(2,1)} %constant.49.clone) | copy-start | bytes 752644
  0.7 11.8 %copy-start.13 = (pred[16]{0:T(512)(128)(4,1)S(1)}, pred[16]{0:T(512)(128)(4,1)}, u32[]{:S(2)}) copy-start(pred[16]{0:T(512)(128)(4,1)} %constant.63) | copy-start | bytes 52
  0.7 11.2 %copy-start.11 = (s32[8]{0:T(128)S(1)}, s32[8]{0:T(128)}, u32[]{:S(2)}) copy-start(s32[8]{0:T(128)} %source_ref.2) | copy-start | bytes 100
  0.7 10.9 %copy-start.12 = (bf16[128,2]{0,1:T(2,128)(2,1)S(1)}, bf16[128,2]{0,1:T(2,128)(2,1)}, u32[]{:S(2)}) copy-start(bf16[128,2]{0,1:T(2,128)(2,1)} %param.31) | copy-start | bytes 1540
  0.7 10.9 %copy-start.9 = (bf16[128,24]{0,1:T(8,128)(2,1)S(1)}, bf16[128,24]{0,1:T(8,128)(2,1)}, u32[]{:S(2)}) copy-start(bf16[128,24]{0,1:T(8,128)(2,1)} %param.30) | copy-start | bytes 18436
  2.2 13.9 %all-to-all-start = ((s32[16,1,128]{2,1,0:T(1,128)}), s32[16,1,128]{2,1,0:T(1,128)S(1)}, u32[]{:S(2)}, u32[]{:S(2)}) async-start(s32[16,1,128]{2,1,0:T(1,128)} %get-tuple-element.27), calls=%async_computation | async-start | bytes 16384 | tf_op jit(solution)/shard_map/all_to_all | solution.py:412
  12.5 3.8 %copy-start.4 = (bf16[24,3,64,128]{3,2,1,0:T(8,128)(2,1)S(1)}, bf16[24,3,64,128]{3,2,1,0:T(8,128)(2,1)}, u32[]{:S(2)}) copy-start(bf16[24,3,64,128]{3,2,1,0:T(8,128)(2,1)} %features_ref.1) | copy-start | bytes 3538948
  18.2 26.9 %all-to-all-start.1 = ((bf16[16,2,3,64,128]{4,3,2,1,0:T(8,128)(2,1)}), bf16[16,2,3,64,128]{4,3,2,1,0:T(8,128)(2,1)}, u32[]{:S(2)}, u32[]{:S(2)}) async-start(bf16[16,2,3,64,128]{4,3,2,1,0:T(8,128)(2,1)} %bitcast.1), calls=%async_computation.1 | async-start | bytes 3145728 | tf_op jit(solution)/shard_map/all_to_all | solution.py:426
  25.3 1.3 %copy-start.5 = (bf16[3,3,256,256]{3,2,1,0:T(8,128)(2,1)S(1)}, bf16[3,3,256,256]{3,2,1,0:T(8,128)(2,1)}, u32[]{:S(2)}) copy-start(bf16[3,3,256,256]{3,2,1,0:T(8,128)(2,1)} %param.28) | copy-start | bytes 3538948
  26.7 3.3 %copy-start.1 = (bf16[4,6,64,128]{3,2,1,0:T(8,128)(2,1)S(1)}, bf16[4,6,64,128]{3,2,1,0:T(8,128)(2,1)}, u32[]{:S(2)}) copy-start(bf16[4,6,64,128]{3,2,1,0:T(8,128)(2,1)} %get-tuple-element.31.keep_ref) | copy-start | bytes 1179652
  26.7 26.5 %copy-start.3 = (bf16[128,128]{1,0:T(8,128)(2,1)S(1)}, bf16[128,128]{1,0:T(8,128)(2,1)}, u32[]{:S(2)}) copy-start(bf16[128,128]{1,0:T(8,128)(2,1)} %constant.55.clone.turn_ref) | copy-start | bytes 98308
  26.8 25.2 %collective-permute-start = (bf16[4,6,64,128]{3,2,1,0:T(8,128)(2,1)}, bf16[4,6,64,128]{3,2,1,0:T(8,128)(2,1)S(1)}, u32[]{:S(2)}, u32[]{:S(2)}) collective-permute-start(bf16[4,6,64,128]{3,2,1,0:T(8,128)(2,1)} %get-tuple-element.32), channel_id=1, source_target_pairs={{0,1},{1,0},{2,3},{3,2},{4,5},{5,4},{6,7},{7,6},{8,9},{9,8},{10,11... | collective-permute-start | bytes 1179656 | tf_op jit(solution)/shard_map/ppermute | solution.py:422
  28.4 23.7 %collective-permute-start.2 = (bf16[4,6,64,128]{3,2,1,0:T(8,128)(2,1)}, bf16[4,6,64,128]{3,2,1,0:T(8,128)(2,1)}, u32[]{:S(2)}, u32[]{:S(2)}) collective-permute-start(bf16[4,6,64,128]{3,2,1,0:T(8,128)(2,1)} %get-tuple-element.32), channel_id=1, source_target_pairs={{0,15},{1,2},{2,1},{3,4},{4,3},{5,6},{6,5},{7,8},{8,7},{9,10},{10,... | collective-permute-start | bytes 1179656 | tf_op jit(solution)/shard_map/ppermute | solution.py:424
  30.0 22.0 %collective-permute-start.1 = (bf16[4,6,64,128]{3,2,1,0:T(8,128)(2,1)S(1)}, bf16[4,6,64,128]{3,2,1,0:T(8,128)(2,1)}, u32[]{:S(2)}, u32[]{:S(2)}) collective-permute-start(bf16[4,6,64,128]{3,2,1,0:T(8,128)(2,1)S(1)} %copy-done.1), channel_id=1, source_target_pairs={{0,14},{1,3},{2,0},{3,5},{4,2},{5,7},{6,4},{7,9},{8,6},{9,11},{10,... | collective-permute-start | bytes 1179656 | tf_op jit(solution)/shard_map/ppermute | solution.py:423
  47.6 15.4 %copy-start.10 = (s32[640]{0:T(1024)S(1)}, s32[640]{0:T(1024)}, u32[]{:S(2)}) copy-start(s32[640]{0:T(1024)} %constant.51.clone) | copy-start | bytes 7684
  47.6 15.4 %copy-start.15 = (pred[640]{0:T(1024)(128)(4,1)S(1)}, pred[640]{0:T(1024)(128)(4,1)}, u32[]{:S(2)}) copy-start(pred[640]{0:T(1024)(128)(4,1)} %constant.52.clone) | copy-start | bytes 1924
  47.6 5.7 %collective-permute-start.3 = (bf16[4,3,64,128]{3,2,1,0:T(8,128)(2,1)}, bf16[4,3,64,128]{3,2,1,0:T(8,128)(2,1)S(1)}, u32[]{:S(2)}, u32[]{:S(2)}) collective-permute-start(bf16[4,3,64,128]{3,2,1,0:T(8,128)(2,1)} %get-tuple-element.36), channel_id=1, source_target_pairs={{0,1},{1,0},{2,3},{3,2},{4,5},{5,4},{6,7},{7,6},{8,9},{9,8},{10,11... | collective-permute-start | bytes 589832 | tf_op jit(solution)/shard_map/ppermute | solution.py:510
  53.3 0.9 copy-start.2
  57.0 9.1 %collective-permute-start.4 = (bf16[4,64,128]{2,1,0:T(8,128)(2,1)S(1)}, bf16[4,64,128]{2,1,0:T(8,128)(2,1)S(1)}, u32[]{:S(2)}, u32[]{:S(2)}) collective-permute-start(bf16[4,64,128]{2,1,0:T(8,128)(2,1)S(1)} %get-tuple-element.39.up_ref), channel_id=1, source_target_pairs={{0,2},{1,3},{2,4},{3,5},{4,6},{5,7},{6,8},{7,9},{8,10},{9,11},{10,... | collective-permute-start | bytes 196616 | tf_op jit(solution)/shard_map/ppermute | solution.py:524
  58.8 7.4 %collective-permute-start.5 = (bf16[4,64,128]{2,1,0:T(8,128)(2,1)S(1)}, bf16[4,64,128]{2,1,0:T(8,128)(2,1)S(1)}, u32[]{:S(2)}, u32[]{:S(2)}) collective-permute-start(bf16[4,64,128]{2,1,0:T(8,128)(2,1)S(1)} %get-tuple-element.37.down_ref), channel_id=1, source_target_pairs={{2,0},{3,1},{4,2},{5,3},{6,4},{7,5},{8,6},{9,7},{10,8},{11,9},{12,... | collective-permute-start | bytes 196616 | tf_op jit(solution)/shard_map/ppermute | solution.py:525
  66.1 17.3 %copy-start.14 = (s32[144]{0:T(256)S(1)}, s32[144]{0:T(256)}, u32[]{:S(2)}) copy-start(s32[144]{0:T(256)} %constant.64) | copy-start | bytes 1732
  76.5 15.4 %all-to-all-start.2 = ((f32[16,16,128]{2,1,0:T(8,128)}), f32[16,16,128]{2,1,0:T(8,128)S(1)}, u32[]{:S(2)}, u32[]{:S(2)}) async-start(f32[16,16,128]{2,1,0:T(8,128)} %get-tuple-element.44), calls=%async_computation.2 | async-start | bytes 262144 | tf_op jit(solution)/shard_map/all_to_all | solution.py:556
  84.4 14.0 %collective-permute-start.6 = (bf16[4,3,64,128]{3,2,1,0:T(8,128)(2,1)S(1)}, bf16[4,3,64,128]{3,2,1,0:T(8,128)(2,1)S(1)}, u32[]{:S(2)}, u32[]{:S(2)}) collective-permute-start(bf16[4,3,64,128]{3,2,1,0:T(8,128)(2,1)S(1)} %get-tuple-element.43), channel_id=1, source_target_pairs={{0,1},{1,0},{2,3},{3,2},{4,5},{5,4},{6,7},{7,6},{8,9},{9,8},{10,11... | collective-permute-start | bytes 589832 | tf_op jit(solution)/shard_map/ppermute | solution.py:557
  91.9 0.7 copy-start.7
  94.3 10.7 %all-to-all-start.3 = ((f32[16,16,128]{2,1,0:T(8,128)}), f32[16,16,128]{2,1,0:T(8,128)S(1)}, u32[]{:S(2)}, u32[]{:S(2)}) async-start(f32[16,16,128]{2,1,0:T(8,128)} %get-tuple-element.46), calls=%async_computation.3 | async-start | bytes 262144 | tf_op jit(solution)/shard_map/all_to_all | solution.py:573
  104.9 0.7 copy-start.6

commit v3 on v2

--- a/solution.py
+++ b/solution.py
@@ -51,15 +51,6 @@
         for pixel in range(MAPW):
             turn[(64 * half + 63 - pixel + 68) % 128, 64 * half + pixel] = 1.0
     return turn
-
-
-def spread_selector():
-    spread = np.zeros((3, 128, 384), np.float32)
-    for part, base in enumerate((0, 6, 22)):
-        for y in range(6):
-            spread[part, base + y, [c for c in range(144) if c % 6 == y]] = 1.0
-            spread[part, base + y, [256 + c for c in range(36) if c % 6 == y]] = 1.0
-    return spread
 
 
 def request_kernel(owner_ref, target_ref, source_ref, out_ref, slot_ref):
@@ -183,7 +174,7 @@
     slot = (lane * 37) >> 8
     across = pixel + RADIUS - (lane - WINDOW * slot)
     inside = (across >= 0) & (across < MAPW) & (slot < 9)
-    for e in range(keep_ref.shape[0]):
+    for e in range(kept_ref.shape[0]):
         place_bands(bands.at[e], (keep_ref, side_ref, ring_ref, cross_ref), e, slice(0, BAND), core)
         sources = bands[e].reshape(4 * BAND * MAPW, 128)
         tbuf[e, pl.ds(core, 1)] = kept_ref[e][None]
@@ -224,6 +215,7 @@
     part_ref,
     window_ref,
     gate_ref,
+    pair_ref,
     cand_ref,
     jac_ref,
     conf_ref,
@@ -231,6 +223,7 @@
     given_ref,
     sums_ref,
     slabs,
+    gates_ref,
     rows_out,
 ):
     tile = lax.axis_index("tile")
@@ -239,10 +232,11 @@
     has_above = jnp.where(tile < 2, 0.0, 1.0).astype(F32)
     has_below = jnp.where(tile >= lax.axis_size("tile") - 2, 0.0, 1.0).astype(F32)
     pixel = lax.broadcasted_iota(jnp.int32, (MAPW, 128), 0)
-    total = jnp.zeros((16, 128), F32)
-    for e in range(half):
-        wide = slabs.at[e]
-        used = half * core + e < counts_ref[0]
+    wider = (CHIP + 2) * MAPW
+    span = CHIP * MAPW
+    blocks = []
+
+    def motion_rows(e):
         above = (above_ref[e].astype(F32) * has_above).astype(BF16)
         below = (below_ref[e].astype(F32) * has_below).astype(BF16)
         down, mid, up = down_ref[e], mid_ref[e], up_ref[e]
@@ -267,29 +261,35 @@
                     part = part * has_above
                 if row >= 8:
                     part = part * has_below
-                spread_columns(wide, pixel, row, part, 384)
-        span = (CHIP + 2) * MAPW
+                spread_columns(slabs.at[e], pixel, row, part, 384)
+
+    def gate_rows(e):
         gates = part_ref[e]
         for tap in range(3):
             gates = gates + jnp.dot(
-                wide[MAPW * tap : MAPW * tap + span, 384:768],
+                slabs[e, MAPW * tap : MAPW * tap + wider, 384:768],
                 gate_ref[tap, 384:768],
                 preferred_element_type=F32,
             )
-        gates = logistic(gates)
+        gates_ref[e] = gates
+
+    def reset_rows(e):
         for row in range(CHIP + 2):
-            reset = gates[MAPW * row : MAPW * (row + 1), 128:256]
-            spread_columns(wide, pixel, row + 1, reset * state_ref[e, row + 1].astype(F32), 0)
-        span = CHIP * MAPW
-        candidate = jnp.zeros((span, 128), F32)
-        for tap in range(3):
-            candidate = candidate + jnp.dot(
-                wide[MAPW * (tap + 1) : MAPW * (tap + 1) + span],
-                cand_ref[tap],
-                preferred_element_type=F32,
+            reset = logistic(gates_ref[e, MAPW * row : MAPW * (row + 1), 128:256])
+            spread_columns(
+                slabs.at[e], pixel, row + 1, reset * state_ref[e, row + 1].astype(F32), 0
             )
-        candidate = jnp.tanh(candidate)
-        update = gates[MAPW : MAPW + span, 0:128]
+
+    def candidate_rows(e):
+        two = jnp.dot(
+            slabs[e, MAPW : 2 * MAPW + span], pair_ref[...], preferred_element_type=F32
+        )
+        third = jnp.dot(
+            slabs[e, 3 * MAPW : 3 * MAPW + span], cand_ref[...], preferred_element_type=F32
+        )
+        candidate = jnp.tanh(two[0:span, 0:128] + two[MAPW : MAPW + span, 128:256] + third)
+        used = half * core + e < counts_ref[0]
+        update = logistic(gates_ref[e, MAPW : MAPW + span, 0:128])
         old = state_ref[e, 2 : 2 + CHIP].reshape(span, 128).astype(F32)
         fresh = ((1.0 - update) * old + update * candidate).astype(BF16)
         chosen = jnp.full((span, 128), jnp.where(used, 1, 0)) == 1
@@ -312,7 +312,14 @@
         block = block * jnp.where(used, 1.0 / (MAPH * MAPW), 0.0).astype(F32)
         if e:
             block = pltpu.roll(block, 32 * e, 1)
-        total = total + block
+        blocks.append(block)
+
+    stages = (motion_rows, gate_rows, reset_rows, candidate_rows)
+    for step in range(half + len(stages) - 1):
+        for n, stage in enumerate(stages):
+            if 0 <= step - n < half:
+                stage(step - n)
+    total = sum(blocks[1:], blocks[0])
     for n in range(sums_ref.shape[0]):
         sums_ref[n] = total
 
@@ -335,6 +342,43 @@
         out_ref[slot >> 1] += pltpu.roll(block, 16 * rank, 1)
 
 
+def tables_kernel(source_ref, owner_ref, target_ref, got_ref, rows_ref, cols_ref, frames_ref):
+    me = lax.axis_index("edge")
+    frames = frames_ref.shape[0]
+    before = lax.axis_index("tile") * rows_ref.shape[0]
+    stack = cols_ref.shape[0]
+    edges = source_ref.shape[0]
+    groups = got_ref.shape[0]
+    lane = lax.broadcasted_iota(jnp.int32, (16, stack), 1)
+    block, x = lane >> 4, lane & 15
+    line = lax.broadcasted_iota(jnp.int32, (16, stack), 0)
+    column = (lax.broadcasted_iota(jnp.int32, (16, cols_ref.shape[1]), 1) * 683) >> 12
+    row_place = jnp.full((16, stack), -1, jnp.int32)
+    diag_place = jnp.full((16, stack), -1, jnp.int32)
+    for b in range(stack // 16):
+        if b < edges:
+            col = source_ref[b]
+            upper = me * frames + col
+            lower = owner_ref[b] * frames + target_ref[b]
+        else:
+            q, g = divmod(b - edges, groups)
+            col = got_ref[g, 0, q]
+            upper = g * frames + got_ref[g, 0, q + 2]
+            lower = me * frames + col
+        mine = me * frames + col
+        for frame, start in ((upper, 0), (lower, 6)):
+            here = (block == b) & (x >= start) & (x < start + 6)
+            at = jnp.where(frame == mine, -stack, 6 * frame - before - start)
+            row_place = jnp.where(here, x + at, row_place)
+            diag_place = jnp.where(here, jnp.where(frame == mine, col, -1), diag_place)
+        cols_ref[16 * b : 16 * (b + 1)] = jnp.where(column == col, 1.0, 0.0).astype(BF16)
+    for n in range(rows_ref.shape[0] // 16):
+        hit = jnp.where(line + 16 * n == row_place, 1.0, 0.0)
+        rows_ref[16 * n : 16 * (n + 1)] = hit.astype(BF16)
+    hits = [jnp.where(line + 16 * n == diag_place, 1.0, 0.0) for n in range(2)]
+    frames_ref[...] = jnp.concatenate(hits, axis=0)[0:frames].astype(BF16)
+
+
 def split_dot(hits, values):
     upper = values.astype(BF16)
     lower = (values - upper.astype(F32)).astype(BF16)
@@ -351,18 +395,19 @@
     )
 
 
-def place_kernel(own_ref, came_ref, spread_ref, rows_ref, cols_ref, frames_ref, within_ref, hess_ref, diag_ref):
+def place_kernel(own_ref, came_ref, rows_ref, cols_ref, frames_ref, within_ref, hess_ref, diag_ref):
     own = own_ref[...].reshape(128, 128)
     came = came_ref[...].reshape(256, 128)
+    lane = lax.broadcasted_iota(jnp.int32, (128, 384), 0)
+    place = lax.broadcasted_iota(jnp.int32, (128, 384), 1)
+    place = jnp.where(place < 256, place, place - 256)
+    place = place - 6 * ((place * 683) >> 12)
+    spread = [jnp.where(lane == place + base, 1.0, 0.0).astype(BF16) for base in (0, 6, 22)]
     values = jnp.concatenate(
-        [
-            dot_split(own, spread_ref[0]),
-            dot_split(came, spread_ref[1]),
-            dot_split(came, spread_ref[2]),
-        ],
+        [dot_split(own, spread[0]), dot_split(came, spread[1]), dot_split(came, spread[2])],
         axis=0,
     )
-    hess_ref[...] = split_dot(rows_ref[...], values[:, 0:144] * cols_ref[...])
+    hess_ref[...] = split_dot(rows_ref[...], values[:, 0:144] * cols_ref[...].astype(F32))
     diag_ref[...] = split_dot(frames_ref[...], values[:, 256:292] * within_ref[...])
 
 
@@ -419,16 +464,15 @@
         name="pack",
     )(pack_source, features, hidden_state)
     got, keep, send = lax.optimization_barrier((got, keep, send))
+    asked = jnp.take(features, got[:, 0, 0:2].reshape(-1), axis=0, mode="clip")
     came = lax.ppermute(send, "tile", beside)
     ring = lax.ppermute(keep, "tile", ring_pairs)
     cross = lax.ppermute(send, "tile", cross_pairs)
-    asked = jnp.take(features, got[:, 0, 0:2].reshape(-1), axis=0, mode="clip")
+    corr_w, gate_w, cand_w = corr_weight, gate_weight, candidate_weight
+    jac_w, conf_w = jacobian_weight, confidence_weight
     returned = lax.all_to_all(
         asked.reshape((owner_count, 2) + band_shape), "edge", split_axis=0, concat_axis=0, tiled=True
     ).reshape((2 * owner_count,) + band_shape)
-    corr_w, gate_w, cand_w = corr_weight, gate_weight, candidate_weight
-    jac_w, conf_w = jacobian_weight, confidence_weight
-    sources = edge_source
     window = jnp.einsum(
         "lrd,dc->lrc", jnp.asarray(window_selector(), BF16), corr_w, preferred_element_type=F32
     ).astype(BF16).reshape(256, (CHIP + 4) * 128)
@@ -440,6 +484,8 @@
         [cand_w[:, :, :channels].reshape(3, 384, 128), cand_w[:, :, channels:].reshape(3, 384, 128)],
         axis=1,
     )
+    cand_pair = jnp.concatenate([cand_w[0], cand_w[1]], axis=1)
+    cand_w = cand_w[2]
     gap = jnp.zeros((channels, 64 - POSE), BF16)
     jac_w = jnp.concatenate([jac_w[:, :POSE], gap, jac_w[:, POSE:], gap], axis=1)
     conf_w = jnp.concatenate(
@@ -451,6 +497,31 @@
         ],
         axis=1,
     )
+    own_rows = 6 * frame_total * owner_count // tile_count
+    stack = 16 * (edge_total + 2 * owner_count)
+    row_hits, col_hits, diag_hits = pl.pallas_call(
+        tables_kernel,
+        out_shape=(
+            jax.ShapeDtypeStruct((own_rows, stack), BF16),
+            jax.ShapeDtypeStruct((stack, 6 * frame_total), BF16),
+            jax.ShapeDtypeStruct((frame_total, stack), BF16),
+        ),
+        in_specs=[smem] * 4,
+        out_specs=(vmem,) * 3,
+        name="tables",
+    )(edge_source, edge_owner.reshape(-1), edge_target, got)
+    within = jnp.asarray(
+        (np.arange(stack)[:, None] % 16 % 6 == np.arange(36)[None, :] // 6).astype(np.float32)
+    )
+    kept_maps, sent_maps = pl.pallas_call(
+        pick_kernel,
+        out_shape=(jax.ShapeDtypeStruct((half,) + band_shape, BF16),) * 2,
+        in_specs=[smem, anywhere],
+        out_specs=(vmem, vmem),
+        scratch_shapes=[pltpu.SemaphoreType.DMA((2, half))],
+        name="pick",
+    )(slot_index, returned)
+    kept_maps, keep_later = lax.optimization_barrier((kept_maps, keep))
     state_rows, gate_part = pl.pallas_call(
         prepare_kernel,
         out_shape=(
@@ -465,48 +536,7 @@
         ],
         compiler_params=pltpu.CompilerParams(vmem_limit_bytes=16 * 1024 * 1024),
         name="prepare",
-    )(keep, came, ring, cross, gate_w)
-    x = np.arange(16)
-    asked_target, asked_source = got[:, 0, 0:2], got[:, 0, 2:4]
-    other_group = jnp.arange(owner_count)[:, None] * frame_total + asked_source
-    source_global = my_index * frame_total + sources
-    target_global = edge_owner[:, 0] * frame_total + edge_target
-
-    def by_row(upper, lower):
-        return jnp.where(x[None, :] < 6, upper[:, None], lower[:, None]).reshape(-1)
-
-    def each_row(value):
-        return jnp.broadcast_to(value[:, None], (value.shape[0], 16)).reshape(-1)
-
-    row_frame = jnp.concatenate(
-        [by_row(source_global, target_global)]
-        + [
-            by_row(other_group[:, q], my_index * frame_total + asked_target[:, q])
-            for q in range(2)
-        ]
-    )
-    col_frame = jnp.concatenate([each_row(sources), each_row(asked_target[:, 0]), each_row(asked_target[:, 1])])
-    stack = edge_total * 16 + 2 * owner_count * 16
-    xs = np.tile(x, stack // 16)
-    real = xs < POSE
-    on_diagonal = row_frame == my_index * frame_total + col_frame
-    own_rows = 6 * frame_total * owner_count // tile_count
-    row_place = row_frame * 6 + xs % 6 - tile * own_rows
-    row_place = jnp.where(real & ~on_diagonal, row_place, -1)
-    diag_place = jnp.where(real & on_diagonal, col_frame, -1)
-    row_hits = (jnp.arange(own_rows)[:, None] == row_place[None, :]).astype(BF16)
-    diag_hits = (jnp.arange(frame_total)[:, None] == diag_place[None, :]).astype(BF16)
-    col_hits = (col_frame[:, None] == (np.arange(6 * frame_total) // 6)[None, :]).astype(F32)
-    within = jnp.asarray((xs[:, None] % 6 == np.arange(36)[None, :] // 6).astype(np.float32))
-
-    kept_maps, sent_maps = pl.pallas_call(
-        pick_kernel,
-        out_shape=(jax.ShapeDtypeStruct((half,) + band_shape, BF16),) * 2,
-        in_specs=[smem, anywhere],
-        out_specs=(vmem, vmem),
-        scratch_shapes=[pltpu.SemaphoreType.DMA((2, half))],
-        name="pick",
-    )(slot_index, returned)
+    )(keep_later, came, ring, cross, gate_w)
     came_maps = lax.ppermute(sent_maps, "tile", beside)
     turn = jnp.asarray(turned_order(), BF16)
     down, mid, up = pl.pallas_call(
@@ -530,10 +560,11 @@
             jax.ShapeDtypeStruct((half, BAND, MAPW, 128), BF16),
             jax.ShapeDtypeStruct((tile_count, 16, 128), F32),
         ),
-        in_specs=[smem] + [vmem] * 12,
+        in_specs=[smem] + [vmem] * 13,
         out_specs=(vmem,) * 3,
         scratch_shapes=[
             pltpu.VMEM((half, (CHIP + 4) * MAPW, 768), BF16),
+            pltpu.VMEM((half, (CHIP + 2) * MAPW, 256), F32),
             pltpu.VMEM((half, 2, BAND, MAPW, 128), BF16),
         ],
         compiler_params=pltpu.CompilerParams(vmem_limit_bytes=24 * 1024 * 1024),
@@ -549,6 +580,7 @@
         gate_part,
         window,
         gate_w,
+        cand_pair,
         cand_w,
         jac_w,
         conf_w,
@@ -577,10 +609,10 @@
             jax.ShapeDtypeStruct((own_rows, 6 * frame_total), F32),
             jax.ShapeDtypeStruct((frame_total, 36), F32),
         ),
-        in_specs=[vmem] * 7,
+        in_specs=[vmem] * 6,
         out_specs=(vmem, vmem),
         name="place",
-    )(own_blocks, incoming, jnp.asarray(spread_selector(), BF16), row_hits, col_hits, diag_hits, within)
+    )(own_blocks, incoming, row_hits, col_hits, diag_hits, within)
     return (hidden_next, camera_hessian, pose_diagonal)
 
 

time: 109 us -> 103 us (0.945)
  Pallas kernels: 27.7 us -> 24.7 us
  local copies, waits for them, and re-layouts: 8.11 us -> 6.38 us
  starting transfers between devices: 39 us -> 37.5 us
  other arithmetic: 4.19 us -> 3.02 us
    pallas_call x1, Pallas kernels: 10.4 us -> 5.94 us  [per_device(): pl.pallas_call(update_kernel, out_shape=(jax.ShapeDtypeStruct((half, BAND...]
    all_to_all x1, waiting for transfers between devices: 0.32 us -> 3.52 us  [per_device(): lax.all_to_all(requests, 'edge', split_axis=0, concat_axis=0, tiled=True)]
    all_to_all x1, waiting for transfers between devices: 12.8 us -> 10 us  [per_device(): lax.all_to_all(asked.reshape((owner_count, 2) + band_shape), 'edge', spli...]
    convert_element_type x3 -> x0, other arithmetic: 2.31 us -> none  [the longest x1 0.98 us: per_device(): (col_frame[:, None] == (np.arange(6 * frame_total) // 6)[None, :]).astype...]
    pallas_call x0 -> x1, Pallas kernels: none -> 1.88 us  [per_device(): pl.pallas_call(tables_kernel, out_shape=(jax.ShapeDtypeStruct((own_rows,...]
    all_to_all x1, starting transfers between devices: 6.38 us -> 4.52 us  [per_device(): lax.all_to_all(asked.reshape((owner_count, 2) + band_shape), 'edge', spli...]
    all_to_all x1, waiting for transfers between devices: 7.36 us -> 8.98 us  [per_device(): lax.all_to_all(sums, 'tile', split_axis=0, concat_axis=0, tiled=True)]
    all_to_all x1, waiting for transfers between devices: 5.74 us -> 4.46 us  [per_device(): lax.all_to_all(outgoing, 'edge', split_axis=0, concat_axis=0, tiled=True)]
  transfers between devices with their start and end apart: 11 -> 11, of which waited for: 5 -> 5; matrix products, arithmetic and copies ran while one was open for 7% -> 5% of each run, Pallas kernels for 9% -> 12%
where the time goes in v3:
time: 103 us; the launch traced here: 102 us
  starting transfers between devices  37.5 us (36%)
  waiting for transfers between devices  28.3 us (27%)
  Pallas kernels  24.7 us (24%)
  local copies, waits for them, and re-layouts  6.38 us (6%)
  other arithmetic  3.02 us (3%)
  between operations  1.56 us (2%)
    all_to_all x1, waiting for transfers between devices, per_device(): lax.all_to_all(asked.reshape((owner_count, 2) + band_shape), 'edge', spli...  10 us
    all_to_all x1, waiting for transfers between devices, per_device(): lax.all_to_all(sums, 'tile', split_axis=0, concat_axis=0, tiled=True)  8.98 us
    all_to_all x1, starting transfers between devices, per_device(): lax.all_to_all(requests, 'edge', split_axis=0, concat_axis=0, tiled=True)  7.6 us
    all_to_all x1, starting transfers between devices, per_device(): lax.all_to_all(sums, 'tile', split_axis=0, concat_axis=0, tiled=True)  6.23 us
    pallas_call x1, Pallas kernels, per_device(): pl.pallas_call(update_kernel, out_shape=(jax.ShapeDtypeStruct((half, BAND...  5.94 us
    all_to_all x1, starting transfers between devices, per_device(): lax.all_to_all(asked.reshape((owner_count, 2) + band_shape), 'edge', spli...  4.52 us
    all_to_all x1, waiting for transfers between devices, per_device(): lax.all_to_all(outgoing, 'edge', split_axis=0, concat_axis=0, tiled=True)  4.46 us
    ppermute x1, starting transfers between devices, per_device(): came_maps = lax.ppermute(sent_maps, 'tile', beside)  4.25 us
  transfers between devices with their start and end apart: 11, of which 5 were waited for; matrix products, arithmetic and copies ran while one was open for 5% of the time, Pallas kernels for 12%

profile of v3, /device:TPU:1, one launch (start us, length us, event | category | flops | bytes accessed | tf_op | source)
XLA Modules:
  0.0 101.7 jit_solution(13217600004491136906)
XLA Ops:
  0.6 0.0 copy-start
  0.6 0.0 copy-start.5
  0.7 1.5 %requests.1 = (s32[16,1,128]{2,1,0:T(1,128)}, s32[8]{0:T(128)}) custom-call(s32[8]{0:T(128)} %bitcast.27, s32[8]{0:T(128)} %target_ref.3, s32[8]{0:T(128)} %source_ref.4), custom_call_target="tpu_custom_call" | custom-call | tf_op jit(solution)/shard_map/requests/pallas_call | solution.py:446
  2.1 7.6 %all-to-all-start = ((s32[16,1,128]{2,1,0:T(1,128)}), s32[16,1,128]{2,1,0:T(1,128)S(1)}, u32[]{:S(2)}, u32[]{:S(2)}) async-start(s32[16,1,128]{2,1,0:T(1,128)} %get-tuple-element.32), calls=%async_computation | async-start | bytes 16384 | tf_op jit(solution)/shard_map/all_to_all | solution.py:457
  9.7 2.8 %pack.1 = (bf16[4,6,64,128]{3,2,1,0:T(8,128)(2,1)}, bf16[4,6,64,128]{3,2,1,0:T(8,128)(2,1)}) custom-call(s32[8]{0:T(128)} %source_ref.4, bf16[24,3,64,128]{3,2,1,0:T(8,128)(2,1)} %features_ref.1, bf16[8,3,64,128]{3,2,1,0:T(8,128)(2,1)} %hidden_ref.1), custom_call_target="tpu_custom_call" | custom-call | tf_op jit(solution)/shard_map/pack/pallas_call | solution.py:458
  12.6 3.5 %all-to-all-done.got_ref = s32[16,1,128]{2,1,0:T(1,128)S(1)} async-done(((s32[16,1,128]{2,1,0:T(1,128)}), s32[16,1,128]{2,1,0:T(1,128)S(1)}, u32[]{:S(2)}, u32[]{:S(2)}) %all-to-all-start) | async-done | bytes 8224 | tf_op jit(solution)/shard_map/all_to_all | solution.py:457
  16.1 0.1 reshape.42
  16.2 1.9 %gather_fusion = bf16[32,3,64,128]{3,2,1,0:T(8,128)(2,1)} fusion(bf16[24,3,64,128]{3,2,1,0:T(8,128)(2,1)S(1)} %copy-done.5, s32[1024]{0:T(1024)S(1)} %pad_clamp_fusion), kind=kCustom, calls=%fused_computation | custom fusion | bytes 3145856 | tf_op jit(solution)/shard_map/jit(_take)/gather | solution.py:467
  18.1 4.5 %all-to-all-start.1 = ((bf16[16,2,3,64,128]{4,3,2,1,0:T(8,128)(2,1)}), bf16[16,2,3,64,128]{4,3,2,1,0:T(8,128)(2,1)}, u32[]{:S(2)}, u32[]{:S(2)}) async-start(bf16[16,2,3,64,128]{4,3,2,1,0:T(8,128)(2,1)} %bitcast.1), calls=%async_computation.1 | async-start | bytes 3145728 | tf_op jit(solution)/shard_map/all_to_all | solution.py:473
  22.7 0.0 copy-start.12
  22.7 0.0 copy-start.10
  22.7 0.7 fusion.4
  23.5 0.1 copy-done.10
  23.6 0.4 convolution_convert_fusion
  24.0 0.1 copy-done.6
  24.1 1.1 %fusion.8 = (bf16[3,3,128,256]{3,2,1,0:T(8,128)(2,1)}, bf16[3,3,128,256]{3,2,1,0:T(8,128)(2,1)}) fusion(bf16[3,3,256,256]{3,2,1,0:T(8,128)(2,1)S(1)} %copy-done.6), kind=kLoop, calls=%fused_computation.26 | loop fusion | bytes 2359296 | tf_op jit(solution)/shard_map/slice | solution.py:480
  25.2 2.1 %collective-permute-start = (bf16[4,6,64,128]{3,2,1,0:T(8,128)(2,1)}, bf16[4,6,64,128]{3,2,1,0:T(8,128)(2,1)S(1)}, u32[]{:S(2)}, u32[]{:S(2)}) collective-permute-start(bf16[4,6,64,128]{3,2,1,0:T(8,128)(2,1)} %get-tuple-element.37), channel_id=1, source_target_pairs={{0,1},{1,0},{2,3},{3,2},{4,5},{5,4},{6,7},{7,6},{8,9},{9,8},{10,11... | collective-permute-start | bytes 1179656 | tf_op jit(solution)/shard_map/ppermute | solution.py:468
  27.3 1.5 %collective-permute-start.2 = (bf16[4,6,64,128]{3,2,1,0:T(8,128)(2,1)}, bf16[4,6,64,128]{3,2,1,0:T(8,128)(2,1)S(1)}, u32[]{:S(2)}, u32[]{:S(2)}) collective-permute-start(bf16[4,6,64,128]{3,2,1,0:T(8,128)(2,1)} %get-tuple-element.37), channel_id=1, source_target_pairs={{0,15},{1,2},{2,1},{3,4},{4,3},{5,6},{6,5},{7,8},{8,7},{9,10},{10,... | collective-permute-start | bytes 1179656 | tf_op jit(solution)/shard_map/ppermute | solution.py:470
  28.9 1.6 %collective-permute-start.1 = (bf16[4,6,64,128]{3,2,1,0:T(8,128)(2,1)S(1)}, bf16[4,6,64,128]{3,2,1,0:T(8,128)(2,1)}, u32[]{:S(2)}, u32[]{:S(2)}) collective-permute-start(bf16[4,6,64,128]{3,2,1,0:T(8,128)(2,1)S(1)} %copy-done.1), channel_id=1, source_target_pairs={{0,14},{1,3},{2,0},{3,5},{4,2},{5,7},{6,4},{7,9},{8,6},{9,11},{10,... | collective-permute-start | bytes 1179656 | tf_op jit(solution)/shard_map/ppermute | solution.py:469
  31.2 0.2 copy.22.window_ref
  31.4 0.1 copy.21
  31.6 0.1 copy.20
  31.7 0.0 copy-start.4
  31.7 1.3 %pad_maximum_fusion.gate_ref = bf16[3,768,256]{2,1,0:T(8,128)(2,1)S(1)} fusion(bf16[3,384,256]{2,1,0:T(8,128)(2,1)} %bitcast.24, bf16[3,384,256]{2,1,0:T(8,128)(2,1)} %bitcast.23), kind=kLoop, calls=%fused_computation.2 | loop fusion | flops 2359296 | bytes 2359296 | tf_op jit(solution)/shard_map/concatenate | solution.py:479
  33.1 10.0 %all-to-all-done.1 = bf16[16,2,3,64,128]{4,3,2,1,0:T(8,128)(2,1)} async-done(((bf16[16,2,3,64,128]{4,3,2,1,0:T(8,128)(2,1)}), bf16[16,2,3,64,128]{4,3,2,1,0:T(8,128)(2,1)}, u32[]{:S(2)}, u32[]{:S(2)}) %all-to-all-start.1) | async-done | bytes 1572896 | tf_op jit(solution)/shard_map/all_to_all | solution.py:473
  43.1 2.4 %pick.1 = (bf16[4,3,64,128]{3,2,1,0:T(8,128)(2,1)}, bf16[4,3,64,128]{3,2,1,0:T(8,128)(2,1)}) custom-call(s32[8]{0:T(128)} %get-tuple-element.38.slot_ref, bf16[32,3,64,128]{3,2,1,0:T(8,128)(2,1)} %bitcast.2.maps_ref), custom_call_target="tpu_custom_call" | custom-call | tf_op jit(solution)/shard_map/pick/pallas_call | solution.py:516
  45.5 4.2 %collective-permute-start.3 = (bf16[4,3,64,128]{3,2,1,0:T(8,128)(2,1)}, bf16[4,3,64,128]{3,2,1,0:T(8,128)(2,1)S(1)}, u32[]{:S(2)}, u32[]{:S(2)}) collective-permute-start(bf16[4,3,64,128]{3,2,1,0:T(8,128)(2,1)} %get-tuple-element.42), channel_id=1, source_target_pairs={{0,1},{1,0},{2,3},{3,2},{4,5},{5,4},{6,7},{7,6},{8,9},{9,8},{10,11... | collective-permute-start | bytes 589832 | tf_op jit(solution)/shard_map/ppermute | solution.py:540
  49.8 1.2 %collective-permute-done.3.came_ref = bf16[4,3,64,128]{3,2,1,0:T(8,128)(2,1)S(1)} collective-permute-done((bf16[4,3,64,128]{3,2,1,0:T(8,128)(2,1)}, bf16[4,3,64,128]{3,2,1,0:T(8,128)(2,1)S(1)}, u32[]{:S(2)}, u32[]{:S(2)}) %collective-permute-start.3) | collective-permute-done | bytes 196640 | tf_op jit(solution)/shard_map/ppermute | solution.py:540
  51.1 0.9 copy-done.3
  52.0 2.7 %windows.1 = (bf16[4,64,128]{2,1,0:T(8,128)(2,1)S(1)}, bf16[4,64,128]{2,1,0:T(8,128)(2,1)S(1)}, bf16[4,64,128]{2,1,0:T(8,128)(2,1)S(1)}) custom-call(bf16[4,6,64,128]{3,2,1,0:T(8,128)(2,1)S(1)} %copy-done.1, bf16[4,6,64,128]{3,2,1,0:T(8,128)(2,1)S(1)} %collective-permute-done.side_ref.came_ref, bf16[4,6,64,128]{3,2,1,0:T(8,128)(2,1)} %collective-permute-done.1.ring_ref, ...), custom_call_target="tpu_custom_call" | custom-call | tf_op jit(solution)/shard_map/windows/pallas_call | solution.py:542
  54.7 1.7 %collective-permute-start.4 = (bf16[4,64,128]{2,1,0:T(8,128)(2,1)S(1)}, bf16[4,64,128]{2,1,0:T(8,128)(2,1)S(1)}, u32[]{:S(2)}, u32[]{:S(2)}) collective-permute-start(bf16[4,64,128]{2,1,0:T(8,128)(2,1)S(1)} %get-tuple-element.45.up_ref), channel_id=1, source_target_pairs={{0,2},{1,3},{2,4},{3,5},{4,6},{5,7},{6,8},{7,9},{8,10},{9,11},{10,... | collective-permute-start | bytes 196616 | tf_op jit(solution)/shard_map/ppermute | solution.py:554
  56.4 4.2 %collective-permute-start.5 = (bf16[4,64,128]{2,1,0:T(8,128)(2,1)S(1)}, bf16[4,64,128]{2,1,0:T(8,128)(2,1)S(1)}, u32[]{:S(2)}, u32[]{:S(2)}) collective-permute-start(bf16[4,64,128]{2,1,0:T(8,128)(2,1)S(1)} %get-tuple-element.43.down_ref), channel_id=1, source_target_pairs={{2,0},{3,1},{4,2},{5,3},{6,4},{7,5},{8,6},{9,7},{10,8},{11,9},{12,... | collective-permute-start | bytes 196616 | tf_op jit(solution)/shard_map/ppermute | solution.py:555
  60.7 0.1 broadcast_in_dim.26
  60.7 0.1 broadcast_in_dim.24
  60.8 0.1 pad_maximum_fusion.3
  61.0 3.0 %prepare.1 = (bf16[4,10,64,128]{3,2,1,0:T(8,128)(2,1)S(1)}, f32[4,512,256]{2,1,0:T(8,128)S(1)}) custom-call(bf16[4,6,64,128]{3,2,1,0:T(8,128)(2,1)S(1)} %copy-done.1, bf16[4,6,64,128]{3,2,1,0:T(8,128)(2,1)S(1)} %collective-permute-done.side_ref.came_ref, bf16[4,6,64,128]{3,2,1,0:T(8,128)(2,1)} %collective-permute-done.1.ring_ref, ...), custom_call_target="tpu_custom_call" | custom-call | tf_op jit(solution)/shard_map/prepare/pallas_call | solution.py:525
  64.0 5.9 %update.1 = (bf16[4,3,64,128]{3,2,1,0:T(8,128)(2,1)S(1)}, bf16[4,3,64,128]{3,2,1,0:T(8,128)(2,1)S(1)}, f32[16,16,128]{2,1,0:T(8,128)}) custom-call(s32[1]{0:T(128)S(6)} %copy.23.counts_ref, bf16[4,64,128]{2,1,0:T(8,128)(2,1)S(1)} %get-tuple-element.43.down_ref, bf16[4,64,128]{2,1,0:T(8,128)(2,1)S(1)} %get-tuple-element.44.mid_ref, ...), custom_call_target="tpu_custom_call" | custom-call | tf_op jit(solution)/shard_map/update/pallas_call | solution.py:556
  69.9 6.2 %all-to-all-start.2 = ((f32[16,16,128]{2,1,0:T(8,128)}), f32[16,16,128]{2,1,0:T(8,128)S(1)}, u32[]{:S(2)}, u32[]{:S(2)}) async-start(f32[16,16,128]{2,1,0:T(8,128)} %get-tuple-element.51), calls=%async_computation.2 | async-start | bytes 262144 | tf_op jit(solution)/shard_map/all_to_all | solution.py:588
  76.2 0.2 collective-permute-start.6
  76.4 9.0 %all-to-all-done.2.parts_ref = f32[16,16,128]{2,1,0:T(8,128)S(1)} async-done(((f32[16,16,128]{2,1,0:T(8,128)}), f32[16,16,128]{2,1,0:T(8,128)S(1)}, u32[]{:S(2)}, u32[]{:S(2)}) %all-to-all-start.2) | async-done | bytes 131104 | tf_op jit(solution)/shard_map/all_to_all | solution.py:588
  85.3 0.7 copy-done.8
  86.0 1.7 %slots.1 = (f32[8,16,128]{2,1,0:T(8,128)}, f32[16,16,128]{2,1,0:T(8,128)}) custom-call(s32[8]{0:T(128)} %get-tuple-element.38.slot_ref, f32[16,16,128]{2,1,0:T(8,128)} %copy-done.8), custom_call_target="tpu_custom_call" | custom-call | tf_op jit(solution)/shard_map/slots/pallas_call | solution.py:595
  87.7 3.5 %all-to-all-start.3 = ((f32[16,16,128]{2,1,0:T(8,128)}), f32[16,16,128]{2,1,0:T(8,128)S(1)}, u32[]{:S(2)}, u32[]{:S(2)}) async-start(f32[16,16,128]{2,1,0:T(8,128)} %get-tuple-element.53), calls=%async_computation.3 | async-start | bytes 262144 | tf_op jit(solution)/shard_map/all_to_all | solution.py:605
  91.3 1.9 %tables.1 = (bf16[144,640]{1,0:T(8,128)(2,1)}, bf16[640,144]{1,0:T(8,128)(2,1)}, bf16[24,640]{1,0:T(8,128)(2,1)}) custom-call(s32[8]{0:T(128)} %source_ref.4, s32[8]{0:T(128)} %bitcast.28, s32[8]{0:T(128)} %target_ref.3, s32[16,1,128]{2,1,0:T(1,128)} %copy-done.11), custom_call_target="tpu_custom_call" | custom-call | tf_op jit(solution)/shard_map/tables/pallas_call | solution.py:502
  93.1 0.8 maximum_select_fusion
  93.9 4.5 %all-to-all-done.3.came_ref = f32[16,16,128]{2,1,0:T(8,128)S(1)} async-done(((f32[16,16,128]{2,1,0:T(8,128)}), f32[16,16,128]{2,1,0:T(8,128)S(1)}, u32[]{:S(2)}, u32[]{:S(2)}) %all-to-all-start.3) | async-done | bytes 131104 | tf_op jit(solution)/shard_map/all_to_all | solution.py:605
  98.4 0.7 copy-done.9
  99.1 2.7 %place.1 = (f32[144,144]{1,0:T(8,128)}, f32[24,36]{1,0:T(8,128)}) custom-call(f32[8,16,128]{2,1,0:T(8,128)} %get-tuple-element.52.own_ref, f32[16,16,128]{2,1,0:T(8,128)} %copy-done.9, bf16[144,640]{1,0:T(8,128)(2,1)} %get-tuple-element.54.rows_ref, bf16[640,144]{1,0:T(8,128)(2,1)} %get-tuple-element.55.cols_ref, ...), custom_call_target="tpu_custom_call" | custom-call | tf_op jit(solution)/shard_map/place/pallas_call | solution.py:606
  (31 shorter events, 0.2 us)
Async XLA Ops:
  0.6 22.9 %copy-start = (bf16[49,128]{1,0:T(8,128)(2,1)S(1)}, bf16[49,128]{1,0:T(8,128)(2,1)}, u32[]{:S(2)}) copy-start(bf16[49,128]{1,0:T(8,128)(2,1)} %param.20) | copy-start | bytes 37636
  0.6 15.6 %copy-start.5 = (bf16[24,3,64,128]{3,2,1,0:T(8,128)(2,1)S(1)}, bf16[24,3,64,128]{3,2,1,0:T(8,128)(2,1)}, u32[]{:S(2)}) copy-start(bf16[24,3,64,128]{3,2,1,0:T(8,128)(2,1)} %features_ref.1) | copy-start | bytes 3538948
  2.1 13.9 %all-to-all-start = ((s32[16,1,128]{2,1,0:T(1,128)}), s32[16,1,128]{2,1,0:T(1,128)S(1)}, u32[]{:S(2)}, u32[]{:S(2)}) async-start(s32[16,1,128]{2,1,0:T(1,128)} %get-tuple-element.32), calls=%async_computation | async-start | bytes 16384 | tf_op jit(solution)/shard_map/all_to_all | solution.py:457
  16.1 2.0 %copy-start.11 = (s32[16,1,128]{2,1,0:T(1,128)}, s32[16,1,128]{2,1,0:T(1,128)S(1)}, u32[]{:S(2)}) copy-start(s32[16,1,128]{2,1,0:T(1,128)S(1)} %all-to-all-done.got_ref) | copy-start | bytes 24580
  18.1 4.5 %copy-start.7 = (bf16[3,3,256,128]{3,2,1,0:T(8,128)(2,1)S(1)}, bf16[3,3,256,128]{3,2,1,0:T(8,128)(2,1)}, u32[]{:S(2)}) copy-start(bf16[3,3,256,128]{3,2,1,0:T(8,128)(2,1)} %param.22) | copy-start | bytes 1769476
  18.1 25.0 %all-to-all-start.1 = ((bf16[16,2,3,64,128]{4,3,2,1,0:T(8,128)(2,1)}), bf16[16,2,3,64,128]{4,3,2,1,0:T(8,128)(2,1)}, u32[]{:S(2)}, u32[]{:S(2)}) async-start(bf16[16,2,3,64,128]{4,3,2,1,0:T(8,128)(2,1)} %bitcast.1), calls=%async_computation.1 | async-start | bytes 3145728 | tf_op jit(solution)/shard_map/all_to_all | solution.py:473
  22.7 0.8 copy-start.12
  22.7 1.0 copy-start.10
  22.7 1.4 %copy-start.6 = (bf16[3,3,256,256]{3,2,1,0:T(8,128)(2,1)S(1)}, bf16[3,3,256,256]{3,2,1,0:T(8,128)(2,1)}, u32[]{:S(2)}) copy-start(bf16[3,3,256,256]{3,2,1,0:T(8,128)(2,1)} %param.21) | copy-start | bytes 3538948
  23.6 5.2 %copy-start.1 = (bf16[4,6,64,128]{3,2,1,0:T(8,128)(2,1)S(1)}, bf16[4,6,64,128]{3,2,1,0:T(8,128)(2,1)}, u32[]{:S(2)}) copy-start(bf16[4,6,64,128]{3,2,1,0:T(8,128)(2,1)} %get-tuple-element.46.keep_ref) | copy-start | bytes 1179652
  25.2 24.6 %collective-permute-start = (bf16[4,6,64,128]{3,2,1,0:T(8,128)(2,1)}, bf16[4,6,64,128]{3,2,1,0:T(8,128)(2,1)S(1)}, u32[]{:S(2)}, u32[]{:S(2)}) collective-permute-start(bf16[4,6,64,128]{3,2,1,0:T(8,128)(2,1)} %get-tuple-element.37), channel_id=1, source_target_pairs={{0,1},{1,0},{2,3},{3,2},{4,5},{5,4},{6,7},{7,6},{8,9},{9,8},{10,11... | collective-permute-start | bytes 1179656 | tf_op jit(solution)/shard_map/ppermute | solution.py:468
  27.3 22.5 %collective-permute-start.2 = (bf16[4,6,64,128]{3,2,1,0:T(8,128)(2,1)}, bf16[4,6,64,128]{3,2,1,0:T(8,128)(2,1)S(1)}, u32[]{:S(2)}, u32[]{:S(2)}) collective-permute-start(bf16[4,6,64,128]{3,2,1,0:T(8,128)(2,1)} %get-tuple-element.37), channel_id=1, source_target_pairs={{0,15},{1,2},{2,1},{3,4},{4,3},{5,6},{6,5},{7,8},{8,7},{9,10},{10,... | collective-permute-start | bytes 1179656 | tf_op jit(solution)/shard_map/ppermute | solution.py:470
  28.9 20.9 %collective-permute-start.1 = (bf16[4,6,64,128]{3,2,1,0:T(8,128)(2,1)S(1)}, bf16[4,6,64,128]{3,2,1,0:T(8,128)(2,1)}, u32[]{:S(2)}, u32[]{:S(2)}) collective-permute-start(bf16[4,6,64,128]{3,2,1,0:T(8,128)(2,1)S(1)} %copy-done.1), channel_id=1, source_target_pairs={{0,14},{1,3},{2,0},{3,5},{4,2},{5,7},{6,4},{7,9},{8,6},{9,11},{10,... | collective-permute-start | bytes 1179656 | tf_op jit(solution)/shard_map/ppermute | solution.py:469
  31.7 18.1 %copy-start.13 = (bf16[128,2]{0,1:T(2,128)(2,1)S(1)}, bf16[128,2]{0,1:T(2,128)(2,1)}, u32[]{:S(2)}) copy-start(bf16[128,2]{0,1:T(2,128)(2,1)} %param.24) | copy-start | bytes 1540
  31.7 19.4 %copy-start.4 = (bf16[128,128]{1,0:T(8,128)(2,1)S(1)}, bf16[128,128]{1,0:T(8,128)(2,1)}, u32[]{:S(2)}) copy-start(bf16[128,128]{1,0:T(8,128)(2,1)} %constant.28.clone.turn_ref) | copy-start | bytes 98308
  45.5 5.5 %collective-permute-start.3 = (bf16[4,3,64,128]{3,2,1,0:T(8,128)(2,1)}, bf16[4,3,64,128]{3,2,1,0:T(8,128)(2,1)S(1)}, u32[]{:S(2)}, u32[]{:S(2)}) collective-permute-start(bf16[4,3,64,128]{3,2,1,0:T(8,128)(2,1)} %get-tuple-element.42), channel_id=1, source_target_pairs={{0,1},{1,0},{2,3},{3,2},{4,5},{5,4},{6,7},{7,6},{8,9},{9,8},{10,11... | collective-permute-start | bytes 589832 | tf_op jit(solution)/shard_map/ppermute | solution.py:540
  51.1 0.9 copy-start.3
  54.7 9.3 %copy-start.2 = (bf16[768,128]{1,0:T(8,128)(2,1)S(1)}, bf16[768,128]{1,0:T(8,128)(2,1)}, u32[]{:S(2)}) copy-start(bf16[768,128]{1,0:T(8,128)(2,1)} %get-tuple-element.61.cand_ref) | copy-start | bytes 589828
  54.7 9.2 %collective-permute-start.4 = (bf16[4,64,128]{2,1,0:T(8,128)(2,1)S(1)}, bf16[4,64,128]{2,1,0:T(8,128)(2,1)S(1)}, u32[]{:S(2)}, u32[]{:S(2)}) collective-permute-start(bf16[4,64,128]{2,1,0:T(8,128)(2,1)S(1)} %get-tuple-element.45.up_ref), channel_id=1, source_target_pairs={{0,2},{1,3},{2,4},{3,5},{4,6},{5,7},{6,8},{7,9},{8,10},{9,11},{10,... | collective-permute-start | bytes 196616 | tf_op jit(solution)/shard_map/ppermute | solution.py:554
  56.4 7.5 %collective-permute-start.5 = (bf16[4,64,128]{2,1,0:T(8,128)(2,1)S(1)}, bf16[4,64,128]{2,1,0:T(8,128)(2,1)S(1)}, u32[]{:S(2)}, u32[]{:S(2)}) collective-permute-start(bf16[4,64,128]{2,1,0:T(8,128)(2,1)S(1)} %get-tuple-element.43.down_ref), channel_id=1, source_target_pairs={{2,0},{3,1},{4,2},{5,3},{6,4},{7,5},{8,6},{9,7},{10,8},{11,9},{12,... | collective-permute-start | bytes 196616 | tf_op jit(solution)/shard_map/ppermute | solution.py:555
  69.9 15.4 %all-to-all-start.2 = ((f32[16,16,128]{2,1,0:T(8,128)}), f32[16,16,128]{2,1,0:T(8,128)S(1)}, u32[]{:S(2)}, u32[]{:S(2)}) async-start(f32[16,16,128]{2,1,0:T(8,128)} %get-tuple-element.51), calls=%async_computation.2 | async-start | bytes 262144 | tf_op jit(solution)/shard_map/all_to_all | solution.py:588
  76.2 17.0 %collective-permute-start.6 = (bf16[4,3,64,128]{3,2,1,0:T(8,128)(2,1)S(1)}, bf16[4,3,64,128]{3,2,1,0:T(8,128)(2,1)S(1)}, u32[]{:S(2)}, u32[]{:S(2)}) collective-permute-start(bf16[4,3,64,128]{3,2,1,0:T(8,128)(2,1)S(1)} %get-tuple-element.50), channel_id=1, source_target_pairs={{0,1},{1,0},{2,3},{3,2},{4,5},{5,4},{6,7},{7,6},{8,9},{9,8},{10,11... | collective-permute-start | bytes 589832 | tf_op jit(solution)/shard_map/ppermute | solution.py:589
  85.3 0.7 copy-start.8
  87.7 10.7 %all-to-all-start.3 = ((f32[16,16,128]{2,1,0:T(8,128)}), f32[16,16,128]{2,1,0:T(8,128)S(1)}, u32[]{:S(2)}, u32[]{:S(2)}) async-start(f32[16,16,128]{2,1,0:T(8,128)} %get-tuple-element.53), calls=%async_computation.3 | async-start | bytes 262144 | tf_op jit(solution)/shard_map/all_to_all | solution.py:605
  98.4 0.7 copy-start.9

commit v4 on v3

--- a/solution.py
+++ b/solution.py
@@ -118,7 +118,7 @@
     wide[at, base + 256 : base + 384] = right.astype(BF16)
 
 
-def place_bands(bands, refs, e, rows, core):
+def place_bands(bands, refs, e, core):
     keep_ref, came_ref, ring_ref, cross_ref = refs
     for ref, band in (
         (keep_ref, 1 + core),
@@ -126,7 +126,7 @@
         (ring_ref, 3 * (1 - core)),
         (cross_ref, 3 * core),
     ):
-        bands[pl.ds(band, 1)] = ref[e, rows][None]
+        bands[pl.ds(band, 1)] = ref[e][None]
 
 
 def prepare_kernel(keep_ref, came_ref, ring_ref, cross_ref, gate_ref, state_ref, part_ref, bands, slabs):
@@ -138,7 +138,7 @@
     refs = (keep_ref, came_ref, ring_ref, cross_ref)
     for e in range(keep_ref.shape[0]):
         wide, rows = slabs.at[e], bands.at[e]
-        place_bands(rows, refs, e, slice(BAND, CHIP), tile % 2)
+        place_bands(rows, refs, e, tile % 2)
         for row in range(CHIP + 4):
             state = rows[(row + 1) // BAND, (row + 1) % BAND].astype(F32)
             if row < 2:
@@ -175,7 +175,7 @@
     across = pixel + RADIUS - (lane - WINDOW * slot)
     inside = (across >= 0) & (across < MAPW) & (slot < 9)
     for e in range(kept_ref.shape[0]):
-        place_bands(bands.at[e], (keep_ref, side_ref, ring_ref, cross_ref), e, slice(0, BAND), core)
+        place_bands(bands.at[e], (keep_ref, side_ref, ring_ref, cross_ref), e, core)
         sources = bands[e].reshape(4 * BAND * MAPW, 128)
         tbuf[e, pl.ds(core, 1)] = kept_ref[e][None]
         tbuf[e, pl.ds(1 - core, 1)] = came_ref[e][None]
@@ -515,7 +515,7 @@
     )
     kept_maps, sent_maps = pl.pallas_call(
         pick_kernel,
-        out_shape=(jax.ShapeDtypeStruct((half,) + band_shape, BF16),) * 2,
+        out_shape=(pltpu.VMEM((half,) + band_shape, BF16),) * 2,
         in_specs=[smem, anywhere],
         out_specs=(vmem, vmem),
         scratch_shapes=[pltpu.SemaphoreType.DMA((2, half))],
@@ -528,7 +528,9 @@
             jax.ShapeDtypeStruct((half, CHIP + 4, MAPW, 128), BF16),
             jax.ShapeDtypeStruct((half, (CHIP + 2) * MAPW, 256), F32),
         ),
-        in_specs=[vmem] * 5,
+        grid=(1,),
+        in_specs=[pl.BlockSpec((half, BAND, MAPW, channels), lambda i: (0, 1, 0, 0))] * 4
+        + [vmem],
         out_specs=(vmem,) * 2,
         scratch_shapes=[
             pltpu.VMEM((half, 4, BAND, MAPW, 128), BF16),
@@ -542,7 +544,9 @@
     down, mid, up = pl.pallas_call(
         corr_kernel,
         out_shape=(jax.ShapeDtypeStruct((half, MAPW, 128), BF16),) * 3,
-        in_specs=[vmem] * 7,
+        grid=(1,),
+        in_specs=[pl.BlockSpec((half, BAND, MAPW, channels), lambda i: (0, 0, 0, 0))] * 4
+        + [vmem] * 3,
         out_specs=(vmem,) * 3,
         scratch_shapes=[
             pltpu.VMEM((half, 4, BAND, MAPW, channels), BF16),
@@ -595,7 +599,7 @@
     own_blocks, outgoing = pl.pallas_call(
         slots_kernel,
         out_shape=(
-            jax.ShapeDtypeStruct((edge_total, 16, 128), F32),
+            pltpu.VMEM((edge_total, 16, 128), F32),
             jax.ShapeDtypeStruct((owner_count, 16, 128), F32),
         ),
         in_specs=[smem, vmem],

time: 103 us -> 101 us (0.981)
  transfers between devices with their start and end apart: 11 -> 11, of which waited for: 5 -> 5; matrix products, arithmetic and copies ran while one was open for 5% -> 5% of each run, Pallas kernels for 12% -> 11%
where the time goes in v4:
time: 101 us; the launch traced here: 100 us
  starting transfers between devices  37.5 us (37%)
  waiting for transfers between devices  28 us (28%)
  Pallas kernels  24 us (24%)
  local copies, waits for them, and re-layouts  5.48 us (5%)
  other arithmetic  2.99 us (3%)
  between operations  1.56 us (2%)
    all_to_all x1, waiting for transfers between devices, per_device(): lax.all_to_all(asked.reshape((owner_count, 2) + band_shape), 'edge', spli...  10 us
    all_to_all x1, waiting for transfers between devices, per_device(): lax.all_to_all(sums, 'tile', split_axis=0, concat_axis=0, tiled=True)  8.98 us
    all_to_all x1, starting transfers between devices, per_device(): lax.all_to_all(requests, 'edge', split_axis=0, concat_axis=0, tiled=True)  7.6 us
    all_to_all x1, starting transfers between devices, per_device(): lax.all_to_all(sums, 'tile', split_axis=0, concat_axis=0, tiled=True)  6.23 us
    pallas_call x1, Pallas kernels, per_device(): pl.pallas_call(update_kernel, out_shape=(jax.ShapeDtypeStruct((half, BAND...  5.94 us
    all_to_all x1, starting transfers between devices, per_device(): lax.all_to_all(asked.reshape((owner_count, 2) + band_shape), 'edge', spli...  4.52 us
    all_to_all x1, waiting for transfers between devices, per_device(): lax.all_to_all(outgoing, 'edge', split_axis=0, concat_axis=0, tiled=True)  4.46 us
    ppermute x1, starting transfers between devices, per_device(): came_maps = lax.ppermute(sent_maps, 'tile', beside)  4.25 us
  transfers between devices with their start and end apart: 11, of which 5 were waited for; matrix products, arithmetic and copies ran while one was open for 5% of the time, Pallas kernels for 11%

profile of v4, /device:TPU:1, one launch (start us, length us, event | category | flops | bytes accessed | tf_op | source)
XLA Modules:
  0.0 100.0 jit_solution(16174694299740963787)
XLA Ops:
  0.6 0.0 copy-start
  0.6 0.0 copy-start.5
  0.7 1.5 %requests.1 = (s32[16,1,128]{2,1,0:T(1,128)}, s32[8]{0:T(128)}) custom-call(s32[8]{0:T(128)} %bitcast.27, s32[8]{0:T(128)} %target_ref.3, s32[8]{0:T(128)} %source_ref.4), custom_call_target="tpu_custom_call" | custom-call | tf_op jit(solution)/shard_map/requests/pallas_call | solution.py:446
  2.1 7.6 %all-to-all-start = ((s32[16,1,128]{2,1,0:T(1,128)}), s32[16,1,128]{2,1,0:T(1,128)S(1)}, u32[]{:S(2)}, u32[]{:S(2)}) async-start(s32[16,1,128]{2,1,0:T(1,128)} %get-tuple-element.32), calls=%async_computation | async-start | bytes 16384 | tf_op jit(solution)/shard_map/all_to_all | solution.py:457
  9.7 2.8 %pack.1 = (bf16[4,6,64,128]{3,2,1,0:T(8,128)(2,1)}, bf16[4,6,64,128]{3,2,1,0:T(8,128)(2,1)}) custom-call(s32[8]{0:T(128)} %source_ref.4, bf16[24,3,64,128]{3,2,1,0:T(8,128)(2,1)} %features_ref.1, bf16[8,3,64,128]{3,2,1,0:T(8,128)(2,1)} %hidden_ref.1), custom_call_target="tpu_custom_call" | custom-call | tf_op jit(solution)/shard_map/pack/pallas_call | solution.py:458
  12.6 3.5 %all-to-all-done.got_ref = s32[16,1,128]{2,1,0:T(1,128)S(1)} async-done(((s32[16,1,128]{2,1,0:T(1,128)}), s32[16,1,128]{2,1,0:T(1,128)S(1)}, u32[]{:S(2)}, u32[]{:S(2)}) %all-to-all-start) | async-done | bytes 8224 | tf_op jit(solution)/shard_map/all_to_all | solution.py:457
  16.1 0.1 reshape.42
  16.2 1.9 %gather_fusion = bf16[32,3,64,128]{3,2,1,0:T(8,128)(2,1)} fusion(bf16[24,3,64,128]{3,2,1,0:T(8,128)(2,1)S(1)} %copy-done.5, s32[1024]{0:T(1024)S(1)} %pad_clamp_fusion), kind=kCustom, calls=%fused_computation | custom fusion | bytes 3145856 | tf_op jit(solution)/shard_map/jit(_take)/gather | solution.py:467
  18.1 4.5 %all-to-all-start.1 = ((bf16[16,2,3,64,128]{4,3,2,1,0:T(8,128)(2,1)}), bf16[16,2,3,64,128]{4,3,2,1,0:T(8,128)(2,1)}, u32[]{:S(2)}, u32[]{:S(2)}) async-start(bf16[16,2,3,64,128]{4,3,2,1,0:T(8,128)(2,1)} %bitcast.1), calls=%async_computation.1 | async-start | bytes 3145728 | tf_op jit(solution)/shard_map/all_to_all | solution.py:473
  22.7 0.0 copy-start.12
  22.7 0.0 copy-start.10
  22.7 0.0 copy-start.6
  22.7 0.7 fusion.4
  23.5 0.2 copy-done.10
  23.6 0.4 convolution_convert_fusion
  24.0 0.1 copy-done.6
  24.1 1.1 %fusion.8 = (bf16[3,3,128,256]{3,2,1,0:T(8,128)(2,1)}, bf16[3,3,128,256]{3,2,1,0:T(8,128)(2,1)}) fusion(bf16[3,3,256,256]{3,2,1,0:T(8,128)(2,1)S(1)} %copy-done.6), kind=kLoop, calls=%fused_computation.26 | loop fusion | bytes 2359296 | tf_op jit(solution)/shard_map/slice | solution.py:480
  25.2 2.1 %collective-permute-start = (bf16[4,6,64,128]{3,2,1,0:T(8,128)(2,1)}, bf16[4,6,64,128]{3,2,1,0:T(8,128)(2,1)S(1)}, u32[]{:S(2)}, u32[]{:S(2)}) collective-permute-start(bf16[4,6,64,128]{3,2,1,0:T(8,128)(2,1)} %get-tuple-element.37), channel_id=1, source_target_pairs={{0,1},{1,0},{2,3},{3,2},{4,5},{5,4},{6,7},{7,6},{8,9},{9,8},{10,11... | collective-permute-start | bytes 1179656 | tf_op jit(solution)/shard_map/ppermute | solution.py:468
  27.3 1.5 %collective-permute-start.2 = (bf16[4,6,64,128]{3,2,1,0:T(8,128)(2,1)}, bf16[4,6,64,128]{3,2,1,0:T(8,128)(2,1)}, u32[]{:S(2)}, u32[]{:S(2)}) collective-permute-start(bf16[4,6,64,128]{3,2,1,0:T(8,128)(2,1)} %get-tuple-element.37), channel_id=1, source_target_pairs={{0,15},{1,2},{2,1},{3,4},{4,3},{5,6},{6,5},{7,8},{8,7},{9,10},{10,... | collective-permute-start | bytes 1179656 | tf_op jit(solution)/shard_map/ppermute | solution.py:470
  28.9 1.6 %collective-permute-start.1 = (bf16[4,6,64,128]{3,2,1,0:T(8,128)(2,1)S(1)}, bf16[4,6,64,128]{3,2,1,0:T(8,128)(2,1)}, u32[]{:S(2)}, u32[]{:S(2)}) collective-permute-start(bf16[4,6,64,128]{3,2,1,0:T(8,128)(2,1)S(1)} %copy-done.1), channel_id=1, source_target_pairs={{0,14},{1,3},{2,0},{3,5},{4,2},{5,7},{6,4},{7,9},{8,6},{9,11},{10,... | collective-permute-start | bytes 1179656 | tf_op jit(solution)/shard_map/ppermute | solution.py:469
  31.2 0.2 copy.22.window_ref
  31.4 0.1 copy.21
  31.6 0.1 copy.20
  31.7 0.0 copy-start.4
  31.7 1.3 %pad_maximum_fusion.gate_ref = bf16[3,768,256]{2,1,0:T(8,128)(2,1)S(1)} fusion(bf16[3,384,256]{2,1,0:T(8,128)(2,1)} %bitcast.24, bf16[3,384,256]{2,1,0:T(8,128)(2,1)} %bitcast.23), kind=kLoop, calls=%fused_computation.2 | loop fusion | flops 2359296 | bytes 2359296 | tf_op jit(solution)/shard_map/concatenate | solution.py:479
  33.1 10.0 %all-to-all-done.1 = bf16[16,2,3,64,128]{4,3,2,1,0:T(8,128)(2,1)} async-done(((bf16[16,2,3,64,128]{4,3,2,1,0:T(8,128)(2,1)}), bf16[16,2,3,64,128]{4,3,2,1,0:T(8,128)(2,1)}, u32[]{:S(2)}, u32[]{:S(2)}) %all-to-all-start.1) | async-done | bytes 1572896 | tf_op jit(solution)/shard_map/all_to_all | solution.py:473
  43.1 1.7 %pick.1 = (bf16[4,3,64,128]{3,2,1,0:T(8,128)(2,1)S(1)}, bf16[4,3,64,128]{3,2,1,0:T(8,128)(2,1)S(1)}) custom-call(s32[8]{0:T(128)} %get-tuple-element.38.slot_ref, bf16[32,3,64,128]{3,2,1,0:T(8,128)(2,1)} %bitcast.2.maps_ref), custom_call_target="tpu_custom_call" | custom-call | tf_op jit(solution)/shard_map/pick/pallas_call | solution.py:516
  44.8 4.2 %collective-permute-start.3 = (bf16[4,3,64,128]{3,2,1,0:T(8,128)(2,1)S(1)}, bf16[4,3,64,128]{3,2,1,0:T(8,128)(2,1)S(1)}, u32[]{:S(2)}, u32[]{:S(2)}) collective-permute-start(bf16[4,3,64,128]{3,2,1,0:T(8,128)(2,1)S(1)} %get-tuple-element.42), channel_id=1, source_target_pairs={{0,1},{1,0},{2,3},{3,2},{4,5},{5,4},{6,7},{7,6},{8,9},{9,8},{10,11... | collective-permute-start | bytes 589832 | tf_op jit(solution)/shard_map/ppermute | solution.py:542
  49.1 1.0 %collective-permute-done.3.came_ref = bf16[4,3,64,128]{3,2,1,0:T(8,128)(2,1)S(1)} collective-permute-done((bf16[4,3,64,128]{3,2,1,0:T(8,128)(2,1)S(1)}, bf16[4,3,64,128]{3,2,1,0:T(8,128)(2,1)S(1)}, u32[]{:S(2)}, u32[]{:S(2)}) %collective-permute-start.3) | collective-permute-done | bytes 196640 | tf_op jit(solution)/shard_map/ppermute | solution.py:542
  50.1 2.8 %windows.1 = (bf16[4,64,128]{2,1,0:T(8,128)(2,1)S(1)}, bf16[4,64,128]{2,1,0:T(8,128)(2,1)S(1)}, bf16[4,64,128]{2,1,0:T(8,128)(2,1)S(1)}) custom-call(bf16[4,6,64,128]{3,2,1,0:T(8,128)(2,1)S(1)} %copy-done.1, bf16[4,6,64,128]{3,2,1,0:T(8,128)(2,1)S(1)} %collective-permute-done.side_ref.came_ref, bf16[4,6,64,128]{3,2,1,0:T(8,128)(2,1)} %collective-permute-done.1.ring_ref, ...), custom_call_target="tpu_custom_call" | custom-call | tf_op jit(solution)/shard_map/windows/pallas_call | solution.py:544
  52.9 1.7 %collective-permute-start.4 = (bf16[4,64,128]{2,1,0:T(8,128)(2,1)S(1)}, bf16[4,64,128]{2,1,0:T(8,128)(2,1)S(1)}, u32[]{:S(2)}, u32[]{:S(2)}) collective-permute-start(bf16[4,64,128]{2,1,0:T(8,128)(2,1)S(1)} %get-tuple-element.45.up_ref), channel_id=1, source_target_pairs={{0,2},{1,3},{2,4},{3,5},{4,6},{5,7},{6,8},{7,9},{8,10},{9,11},{10,... | collective-permute-start | bytes 196616 | tf_op jit(solution)/shard_map/ppermute | solution.py:558
  54.6 4.2 %collective-permute-start.5 = (bf16[4,64,128]{2,1,0:T(8,128)(2,1)S(1)}, bf16[4,64,128]{2,1,0:T(8,128)(2,1)S(1)}, u32[]{:S(2)}, u32[]{:S(2)}) collective-permute-start(bf16[4,64,128]{2,1,0:T(8,128)(2,1)S(1)} %get-tuple-element.43.down_ref), channel_id=1, source_target_pairs={{2,0},{3,1},{4,2},{5,3},{6,4},{7,5},{8,6},{9,7},{10,8},{11,9},{12,... | collective-permute-start | bytes 196616 | tf_op jit(solution)/shard_map/ppermute | solution.py:559
  58.8 0.1 broadcast_in_dim.26
  58.9 0.1 broadcast_in_dim.24
  59.0 0.1 pad_maximum_fusion.3
  59.1 3.1 %prepare.1 = (bf16[4,10,64,128]{3,2,1,0:T(8,128)(2,1)S(1)}, f32[4,512,256]{2,1,0:T(8,128)S(1)}) custom-call(bf16[4,6,64,128]{3,2,1,0:T(8,128)(2,1)S(1)} %copy-done.1, bf16[4,6,64,128]{3,2,1,0:T(8,128)(2,1)S(1)} %collective-permute-done.side_ref.came_ref, bf16[4,6,64,128]{3,2,1,0:T(8,128)(2,1)} %collective-permute-done.1.ring_ref, ...), custom_call_target="tpu_custom_call" | custom-call | tf_op jit(solution)/shard_map/prepare/pallas_call | solution.py:525
  62.2 5.9 %update.1 = (bf16[4,3,64,128]{3,2,1,0:T(8,128)(2,1)S(1)}, bf16[4,3,64,128]{3,2,1,0:T(8,128)(2,1)S(1)}, f32[16,16,128]{2,1,0:T(8,128)}) custom-call(s32[1]{0:T(128)S(6)} %copy.23.counts_ref, bf16[4,64,128]{2,1,0:T(8,128)(2,1)S(1)} %get-tuple-element.43.down_ref, bf16[4,64,128]{2,1,0:T(8,128)(2,1)S(1)} %get-tuple-element.44.mid_ref, ...), custom_call_target="tpu_custom_call" | custom-call | tf_op jit(solution)/shard_map/update/pallas_call | solution.py:560
  68.2 6.2 %all-to-all-start.2 = ((f32[16,16,128]{2,1,0:T(8,128)}), f32[16,16,128]{2,1,0:T(8,128)S(1)}, u32[]{:S(2)}, u32[]{:S(2)}) async-start(f32[16,16,128]{2,1,0:T(8,128)} %get-tuple-element.51), calls=%async_computation.2 | async-start | bytes 262144 | tf_op jit(solution)/shard_map/all_to_all | solution.py:592
  74.4 0.2 collective-permute-start.6
  74.6 9.0 %all-to-all-done.2.parts_ref = f32[16,16,128]{2,1,0:T(8,128)S(1)} async-done(((f32[16,16,128]{2,1,0:T(8,128)}), f32[16,16,128]{2,1,0:T(8,128)S(1)}, u32[]{:S(2)}, u32[]{:S(2)}) %all-to-all-start.2) | async-done | bytes 131104 | tf_op jit(solution)/shard_map/all_to_all | solution.py:592
  83.6 0.7 copy-done.8
  84.2 1.7 %slots.1 = (f32[8,16,128]{2,1,0:T(8,128)S(1)}, f32[16,16,128]{2,1,0:T(8,128)}) custom-call(s32[8]{0:T(128)} %get-tuple-element.38.slot_ref, f32[16,16,128]{2,1,0:T(8,128)} %copy-done.8), custom_call_target="tpu_custom_call" | custom-call | tf_op jit(solution)/shard_map/slots/pallas_call | solution.py:599
  86.0 3.5 %all-to-all-start.3 = ((f32[16,16,128]{2,1,0:T(8,128)}), f32[16,16,128]{2,1,0:T(8,128)S(1)}, u32[]{:S(2)}, u32[]{:S(2)}) async-start(f32[16,16,128]{2,1,0:T(8,128)} %get-tuple-element.53), calls=%async_computation.3 | async-start | bytes 262144 | tf_op jit(solution)/shard_map/all_to_all | solution.py:609
  89.5 1.9 %tables.1 = (bf16[144,640]{1,0:T(8,128)(2,1)}, bf16[640,144]{1,0:T(8,128)(2,1)}, bf16[24,640]{1,0:T(8,128)(2,1)}) custom-call(s32[8]{0:T(128)} %source_ref.4, s32[8]{0:T(128)} %bitcast.28, s32[8]{0:T(128)} %target_ref.3, s32[16,1,128]{2,1,0:T(1,128)} %copy-done.11), custom_call_target="tpu_custom_call" | custom-call | tf_op jit(solution)/shard_map/tables/pallas_call | solution.py:502
  91.4 0.8 maximum_select_fusion
  92.2 4.5 %all-to-all-done.3.came_ref = f32[16,16,128]{2,1,0:T(8,128)S(1)} async-done(((f32[16,16,128]{2,1,0:T(8,128)}), f32[16,16,128]{2,1,0:T(8,128)S(1)}, u32[]{:S(2)}, u32[]{:S(2)}) %all-to-all-start.3) | async-done | bytes 131104 | tf_op jit(solution)/shard_map/all_to_all | solution.py:609
  96.6 0.7 copy-done.9
  97.3 2.7 %place.1 = (f32[144,144]{1,0:T(8,128)}, f32[24,36]{1,0:T(8,128)}) custom-call(f32[8,16,128]{2,1,0:T(8,128)} %copy-done.3, f32[16,16,128]{2,1,0:T(8,128)} %copy-done.9, bf16[144,640]{1,0:T(8,128)(2,1)} %get-tuple-element.54.rows_ref, bf16[640,144]{1,0:T(8,128)(2,1)} %get-tuple-element.55.cols_ref, bf16[24,640]{1,0:T(8,128)(2,1)} %get-tuple-element.56.frames_ref, ...), custom_call_target="tpu_custom_call" | custom-call | tf_op jit(solution)/shard_map/place/pallas_call | solution.py:610
  (31 shorter events, 0.2 us)
Async XLA Ops:
  0.6 22.8 %copy-start = (bf16[49,128]{1,0:T(8,128)(2,1)S(1)}, bf16[49,128]{1,0:T(8,128)(2,1)}, u32[]{:S(2)}) copy-start(bf16[49,128]{1,0:T(8,128)(2,1)} %param.20) | copy-start | bytes 37636
  0.6 15.6 %copy-start.5 = (bf16[24,3,64,128]{3,2,1,0:T(8,128)(2,1)S(1)}, bf16[24,3,64,128]{3,2,1,0:T(8,128)(2,1)}, u32[]{:S(2)}) copy-start(bf16[24,3,64,128]{3,2,1,0:T(8,128)(2,1)} %features_ref.1) | copy-start | bytes 3538948
  2.1 13.9 %all-to-all-start = ((s32[16,1,128]{2,1,0:T(1,128)}), s32[16,1,128]{2,1,0:T(1,128)S(1)}, u32[]{:S(2)}, u32[]{:S(2)}) async-start(s32[16,1,128]{2,1,0:T(1,128)} %get-tuple-element.32), calls=%async_computation | async-start | bytes 16384 | tf_op jit(solution)/shard_map/all_to_all | solution.py:457
  16.1 2.0 %copy-start.11 = (s32[16,1,128]{2,1,0:T(1,128)}, s32[16,1,128]{2,1,0:T(1,128)S(1)}, u32[]{:S(2)}) copy-start(s32[16,1,128]{2,1,0:T(1,128)S(1)} %all-to-all-done.got_ref) | copy-start | bytes 24580
  18.1 4.5 %copy-start.7 = (bf16[3,3,256,128]{3,2,1,0:T(8,128)(2,1)S(1)}, bf16[3,3,256,128]{3,2,1,0:T(8,128)(2,1)}, u32[]{:S(2)}) copy-start(bf16[3,3,256,128]{3,2,1,0:T(8,128)(2,1)} %param.22) | copy-start | bytes 1769476
  18.1 25.0 %all-to-all-start.1 = ((bf16[16,2,3,64,128]{4,3,2,1,0:T(8,128)(2,1)}), bf16[16,2,3,64,128]{4,3,2,1,0:T(8,128)(2,1)}, u32[]{:S(2)}, u32[]{:S(2)}) async-start(bf16[16,2,3,64,128]{4,3,2,1,0:T(8,128)(2,1)} %bitcast.1), calls=%async_computation.1 | async-start | bytes 3145728 | tf_op jit(solution)/shard_map/all_to_all | solution.py:473
  22.7 0.8 copy-start.12
  22.7 1.0 copy-start.10
  22.7 1.4 %copy-start.6 = (bf16[3,3,256,256]{3,2,1,0:T(8,128)(2,1)S(1)}, bf16[3,3,256,256]{3,2,1,0:T(8,128)(2,1)}, u32[]{:S(2)}) copy-start(bf16[3,3,256,256]{3,2,1,0:T(8,128)(2,1)} %param.21) | copy-start | bytes 3538948
  23.6 5.2 %copy-start.1 = (bf16[4,6,64,128]{3,2,1,0:T(8,128)(2,1)S(1)}, bf16[4,6,64,128]{3,2,1,0:T(8,128)(2,1)}, u32[]{:S(2)}) copy-start(bf16[4,6,64,128]{3,2,1,0:T(8,128)(2,1)} %get-tuple-element.46.keep_ref) | copy-start | bytes 1179652
  25.2 23.8 %collective-permute-start = (bf16[4,6,64,128]{3,2,1,0:T(8,128)(2,1)}, bf16[4,6,64,128]{3,2,1,0:T(8,128)(2,1)S(1)}, u32[]{:S(2)}, u32[]{:S(2)}) collective-permute-start(bf16[4,6,64,128]{3,2,1,0:T(8,128)(2,1)} %get-tuple-element.37), channel_id=1, source_target_pairs={{0,1},{1,0},{2,3},{3,2},{4,5},{5,4},{6,7},{7,6},{8,9},{9,8},{10,11... | collective-permute-start | bytes 1179656 | tf_op jit(solution)/shard_map/ppermute | solution.py:468
  27.3 21.8 %collective-permute-start.2 = (bf16[4,6,64,128]{3,2,1,0:T(8,128)(2,1)}, bf16[4,6,64,128]{3,2,1,0:T(8,128)(2,1)}, u32[]{:S(2)}, u32[]{:S(2)}) collective-permute-start(bf16[4,6,64,128]{3,2,1,0:T(8,128)(2,1)} %get-tuple-element.37), channel_id=1, source_target_pairs={{0,15},{1,2},{2,1},{3,4},{4,3},{5,6},{6,5},{7,8},{8,7},{9,10},{10,... | collective-permute-start | bytes 1179656 | tf_op jit(solution)/shard_map/ppermute | solution.py:470
  28.9 20.2 %collective-permute-start.1 = (bf16[4,6,64,128]{3,2,1,0:T(8,128)(2,1)S(1)}, bf16[4,6,64,128]{3,2,1,0:T(8,128)(2,1)}, u32[]{:S(2)}, u32[]{:S(2)}) collective-permute-start(bf16[4,6,64,128]{3,2,1,0:T(8,128)(2,1)S(1)} %copy-done.1), channel_id=1, source_target_pairs={{0,14},{1,3},{2,0},{3,5},{4,2},{5,7},{6,4},{7,9},{8,6},{9,11},{10,... | collective-permute-start | bytes 1179656 | tf_op jit(solution)/shard_map/ppermute | solution.py:469
  31.7 17.4 %copy-start.13 = (bf16[128,2]{0,1:T(2,128)(2,1)S(1)}, bf16[128,2]{0,1:T(2,128)(2,1)}, u32[]{:S(2)}) copy-start(bf16[128,2]{0,1:T(2,128)(2,1)} %param.24) | copy-start | bytes 1540
  31.7 18.4 %copy-start.4 = (bf16[128,128]{1,0:T(8,128)(2,1)S(1)}, bf16[128,128]{1,0:T(8,128)(2,1)}, u32[]{:S(2)}) copy-start(bf16[128,128]{1,0:T(8,128)(2,1)} %constant.28.clone.turn_ref) | copy-start | bytes 98308
  44.8 5.3 %collective-permute-start.3 = (bf16[4,3,64,128]{3,2,1,0:T(8,128)(2,1)S(1)}, bf16[4,3,64,128]{3,2,1,0:T(8,128)(2,1)S(1)}, u32[]{:S(2)}, u32[]{:S(2)}) collective-permute-start(bf16[4,3,64,128]{3,2,1,0:T(8,128)(2,1)S(1)} %get-tuple-element.42), channel_id=1, source_target_pairs={{0,1},{1,0},{2,3},{3,2},{4,5},{5,4},{6,7},{7,6},{8,9},{9,8},{10,11... | collective-permute-start | bytes 589832 | tf_op jit(solution)/shard_map/ppermute | solution.py:542
  52.9 9.3 %copy-start.2 = (bf16[768,128]{1,0:T(8,128)(2,1)S(1)}, bf16[768,128]{1,0:T(8,128)(2,1)}, u32[]{:S(2)}) copy-start(bf16[768,128]{1,0:T(8,128)(2,1)} %get-tuple-element.61.cand_ref) | copy-start | bytes 589828
  52.9 9.3 %collective-permute-start.4 = (bf16[4,64,128]{2,1,0:T(8,128)(2,1)S(1)}, bf16[4,64,128]{2,1,0:T(8,128)(2,1)S(1)}, u32[]{:S(2)}, u32[]{:S(2)}) collective-permute-start(bf16[4,64,128]{2,1,0:T(8,128)(2,1)S(1)} %get-tuple-element.45.up_ref), channel_id=1, source_target_pairs={{0,2},{1,3},{2,4},{3,5},{4,6},{5,7},{6,8},{7,9},{8,10},{9,11},{10,... | collective-permute-start | bytes 196616 | tf_op jit(solution)/shard_map/ppermute | solution.py:558
  54.6 7.6 %collective-permute-start.5 = (bf16[4,64,128]{2,1,0:T(8,128)(2,1)S(1)}, bf16[4,64,128]{2,1,0:T(8,128)(2,1)S(1)}, u32[]{:S(2)}, u32[]{:S(2)}) collective-permute-start(bf16[4,64,128]{2,1,0:T(8,128)(2,1)S(1)} %get-tuple-element.43.down_ref), channel_id=1, source_target_pairs={{2,0},{3,1},{4,2},{5,3},{6,4},{7,5},{8,6},{9,7},{10,8},{11,9},{12,... | collective-permute-start | bytes 196616 | tf_op jit(solution)/shard_map/ppermute | solution.py:559
  68.2 15.4 %all-to-all-start.2 = ((f32[16,16,128]{2,1,0:T(8,128)}), f32[16,16,128]{2,1,0:T(8,128)S(1)}, u32[]{:S(2)}, u32[]{:S(2)}) async-start(f32[16,16,128]{2,1,0:T(8,128)} %get-tuple-element.51), calls=%async_computation.2 | async-start | bytes 262144 | tf_op jit(solution)/shard_map/all_to_all | solution.py:592
  74.4 17.0 %collective-permute-start.6 = (bf16[4,3,64,128]{3,2,1,0:T(8,128)(2,1)S(1)}, bf16[4,3,64,128]{3,2,1,0:T(8,128)(2,1)S(1)}, u32[]{:S(2)}, u32[]{:S(2)}) collective-permute-start(bf16[4,3,64,128]{3,2,1,0:T(8,128)(2,1)S(1)} %get-tuple-element.50), channel_id=1, source_target_pairs={{0,1},{1,0},{2,3},{3,2},{4,5},{5,4},{6,7},{7,6},{8,9},{9,8},{10,11... | collective-permute-start | bytes 589832 | tf_op jit(solution)/shard_map/ppermute | solution.py:593
  83.6 0.7 copy-start.8
  86.0 10.7 %copy-start.3 = (f32[8,16,128]{2,1,0:T(8,128)}, f32[8,16,128]{2,1,0:T(8,128)S(1)}, u32[]{:S(2)}) copy-start(f32[8,16,128]{2,1,0:T(8,128)S(1)} %get-tuple-element.52.own_ref) | copy-start | bytes 196612
  86.0 10.7 %all-to-all-start.3 = ((f32[16,16,128]{2,1,0:T(8,128)}), f32[16,16,128]{2,1,0:T(8,128)S(1)}, u32[]{:S(2)}, u32[]{:S(2)}) async-start(f32[16,16,128]{2,1,0:T(8,128)} %get-tuple-element.53), calls=%async_computation.3 | async-start | bytes 262144 | tf_op jit(solution)/shard_map/all_to_all | solution.py:609
  96.6 0.7 copy-start.9

commit v5 on v4

--- a/solution.py
+++ b/solution.py
@@ -218,7 +218,7 @@
     pair_ref,
     cand_ref,
     jac_ref,
-    conf_ref,
+    head_ref,
     kept_ref,
     given_ref,
     sums_ref,
@@ -298,15 +298,15 @@
         kept_ref[e] = rows_out[e, pl.ds(core, 1)][0]
         given_ref[e] = rows_out[e, pl.ds(1 - core, 1)][0]
         jac = jnp.dot(fresh, jac_ref[...], preferred_element_type=F32)
-        logit = jnp.dot(fresh, conf_ref[...], preferred_element_type=F32)
+        turned = lax.dot_general(
+            head_ref[...], fresh, (((1,), (1,)), ((), ())), preferred_element_type=F32
+        )
+        logit = turned[32:64]
         conf = jnp.maximum(logit, 0.0) + jnp.log1p(jnp.exp(-jnp.abs(logit)))
-        normal = lax.dot_general(
-            (jac * conf).astype(BF16),
-            jac.astype(BF16),
-            (((0,), (0,)), ((), ())),
-            preferred_element_type=F32,
+        normal = jnp.dot(
+            (turned[0:32] * conf).astype(BF16), jac.astype(BF16), preferred_element_type=F32
         )
-        block = normal[0:16] + pltpu.roll(normal[64:80], 64, 1)
+        block = normal[0:16] + pltpu.roll(normal[16:32], 64, 1)
         lane = lax.broadcasted_iota(jnp.int32, (16, 128), 1)
         block = jnp.where(lane < 16, block, 0.0)
         block = block * jnp.where(used, 1.0 / (MAPH * MAPW), 0.0).astype(F32)
@@ -487,16 +487,19 @@
     cand_pair = jnp.concatenate([cand_w[0], cand_w[1]], axis=1)
     cand_w = cand_w[2]
     gap = jnp.zeros((channels, 64 - POSE), BF16)
-    jac_w = jnp.concatenate([jac_w[:, :POSE], gap, jac_w[:, POSE:], gap], axis=1)
-    conf_w = jnp.concatenate(
+    short = jnp.zeros((channels, 16 - POSE), BF16)
+    head_w = jnp.concatenate(
         [
-            jnp.broadcast_to(conf_w[:, 0:1], (channels, POSE)),
-            gap,
-            jnp.broadcast_to(conf_w[:, 1:2], (channels, POSE)),
-            gap,
+            jac_w[:, :POSE],
+            short,
+            jac_w[:, POSE:],
+            short,
+            jnp.broadcast_to(conf_w[:, 0:1], (channels, 16)),
+            jnp.broadcast_to(conf_w[:, 1:2], (channels, 16)),
         ],
         axis=1,
-    )
+    ).T
+    jac_w = jnp.concatenate([jac_w[:, :POSE], gap, jac_w[:, POSE:], gap], axis=1)
     own_rows = 6 * frame_total * owner_count // tile_count
     stack = 16 * (edge_total + 2 * owner_count)
     row_hits, col_hits, diag_hits = pl.pallas_call(
@@ -587,7 +590,7 @@
         cand_pair,
         cand_w,
         jac_w,
-        conf_w,
+        head_w,
     )
     parts = lax.all_to_all(sums, "tile", split_axis=0, concat_axis=0, tiled=True)
     given_came = lax.ppermute(given, "tile", beside)

time: 101 us -> 103 us (1.020)
  local copies, waits for them, and re-layouts: 5.48 us -> 8.14 us
  Pallas kernels: 24 us -> 21.7 us
  waiting for transfers between devices: 28 us -> 29.6 us
    all_to_all x1, waiting for transfers between devices: 10 us -> 12.7 us  [per_device(): lax.all_to_all(asked.reshape((owner_count, 2) + band_shape), 'edge', spli...]
    concatenate x0 -> x1, local copies, waits for them, and re-layouts: none -> 1.45 us  [per_device(): jnp.concatenate([jac_w[:, :POSE], short, jac_w[:, POSE:], short, jnp.broa...]
    reshape x1, local copies, waits for them, and re-layouts: 0.24 us -> 1.33 us  [per_device(): window = jnp.einsum('lrd,dc->lrc', jnp.asarray(window_selector(), BF16),...]
    ppermute x1, waiting for transfers between devices: 1.04 us -> 0.01 us  [per_device(): came_maps = lax.ppermute(sent_maps, 'tile', beside)]
  transfers between devices with their start and end apart: 11 -> 11, of which waited for: 5 -> 4; matrix products, arithmetic and copies ran while one was open for 5% -> 8% of each run, Pallas kernels for 11% -> 10%
where the time goes in v5:
time: 103 us; the launch traced here: 102 us
  starting transfers between devices  37.7 us (37%)
  waiting for transfers between devices  29.6 us (29%)
  Pallas kernels  21.7 us (21%)
  local copies, waits for them, and re-layouts  8.14 us (8%)
  other arithmetic  2.29 us (2%)
  between operations  1.57 us (2%)
  matrix products  1.21 us (1%)
    all_to_all x1, waiting for transfers between devices, per_device(): lax.all_to_all(asked.reshape((owner_count, 2) + band_shape), 'edge', spli...  12.7 us
    all_to_all x1, waiting for transfers between devices, per_device(): lax.all_to_all(sums, 'tile', split_axis=0, concat_axis=0, tiled=True)  8.98 us
    all_to_all x1, starting transfers between devices, per_device(): lax.all_to_all(requests, 'edge', split_axis=0, concat_axis=0, tiled=True)  7.6 us
    all_to_all x1, starting transfers between devices, per_device(): lax.all_to_all(sums, 'tile', split_axis=0, concat_axis=0, tiled=True)  6.44 us
    pallas_call x1, Pallas kernels, per_device(): pl.pallas_call(update_kernel, out_shape=(jax.ShapeDtypeStruct((half, BAND...  5.54 us
    all_to_all x1, starting transfers between devices, per_device(): lax.all_to_all(asked.reshape((owner_count, 2) + band_shape), 'edge', spli...  4.55 us
    all_to_all x1, waiting for transfers between devices, per_device(): lax.all_to_all(outgoing, 'edge', split_axis=0, concat_axis=0, tiled=True)  4.46 us
    ppermute x1, starting transfers between devices, per_device(): came_maps = lax.ppermute(sent_maps, 'tile', beside)  4.25 us
  transfers between devices with their start and end apart: 11, of which 4 were waited for; matrix products, arithmetic and copies ran while one was open for 8% of the time, Pallas kernels for 10%

profile of v5, /device:TPU:1, one launch (start us, length us, event | category | flops | bytes accessed | tf_op | source)
XLA Modules:
  0.0 102.2 jit_solution(14356338367163191000)
XLA Ops:
  0.6 0.0 copy-start
  0.6 0.0 copy-start.4
  0.7 1.5 %requests.1 = (s32[16,1,128]{2,1,0:T(1,128)}, s32[8]{0:T(128)}) custom-call(s32[8]{0:T(128)} %bitcast.29, s32[8]{0:T(128)} %target_ref.3, s32[8]{0:T(128)} %source_ref.4), custom_call_target="tpu_custom_call" | custom-call | tf_op jit(solution)/shard_map/requests/pallas_call | solution.py:446
  2.1 7.6 %all-to-all-start = ((s32[16,1,128]{2,1,0:T(1,128)}), s32[16,1,128]{2,1,0:T(1,128)S(1)}, u32[]{:S(2)}, u32[]{:S(2)}) async-start(s32[16,1,128]{2,1,0:T(1,128)} %get-tuple-element.32), calls=%async_computation | async-start | bytes 16384 | tf_op jit(solution)/shard_map/all_to_all | solution.py:457
  9.7 2.8 %pack.1 = (bf16[4,6,64,128]{3,2,1,0:T(8,128)(2,1)}, bf16[4,6,64,128]{3,2,1,0:T(8,128)(2,1)}) custom-call(s32[8]{0:T(128)} %source_ref.4, bf16[24,3,64,128]{3,2,1,0:T(8,128)(2,1)} %features_ref.1, bf16[8,3,64,128]{3,2,1,0:T(8,128)(2,1)} %hidden_ref.1), custom_call_target="tpu_custom_call" | custom-call | tf_op jit(solution)/shard_map/pack/pallas_call | solution.py:458
  12.6 3.5 %all-to-all-done.got_ref = s32[16,1,128]{2,1,0:T(1,128)S(1)} async-done(((s32[16,1,128]{2,1,0:T(1,128)}), s32[16,1,128]{2,1,0:T(1,128)S(1)}, u32[]{:S(2)}, u32[]{:S(2)}) %all-to-all-start) | async-done | bytes 8224 | tf_op jit(solution)/shard_map/all_to_all | solution.py:457
  16.1 0.1 reshape.42
  16.2 1.9 %gather_fusion = bf16[32,3,64,128]{3,2,1,0:T(8,128)(2,1)} fusion(bf16[24,3,64,128]{3,2,1,0:T(8,128)(2,1)S(1)} %copy-done.4, s32[1024]{0:T(1024)S(1)} %pad_clamp_fusion), kind=kCustom, calls=%fused_computation | custom fusion | bytes 3145856 | tf_op jit(solution)/shard_map/jit(_take)/gather | solution.py:467
  18.1 4.5 %all-to-all-start.1 = ((bf16[16,2,3,64,128]{4,3,2,1,0:T(8,128)(2,1)}), bf16[16,2,3,64,128]{4,3,2,1,0:T(8,128)(2,1)}, u32[]{:S(2)}, u32[]{:S(2)}) async-start(bf16[16,2,3,64,128]{4,3,2,1,0:T(8,128)(2,1)} %bitcast.1), calls=%async_computation.1 | async-start | bytes 3145728 | tf_op jit(solution)/shard_map/all_to_all | solution.py:473
  22.7 0.0 copy-start.5
  22.8 0.0 copy-start.1
  22.8 0.0 copy-start.12
  22.8 1.2 %convolution_convert_fusion = bf16[256,10,128]{0,2,1:T(8,128)(2,1)} fusion(bf16[256,10,49]{0,2,1:T(8,128)(2,1)S(1)} %copy-done.9, bf16[49,128]{1,0:T(8,128)(2,1)S(1)} %copy-done), kind=kOutput, calls=%fused_computation.1 | convolution fusion | flops 32440320 | bytes 918784 | tf_op jit(solution)/shard_map/lrd,dc->lrc/dot_general | solution.py:476
  24.0 1.1 %fusion.6 = (bf16[3,3,128,256]{3,2,1,0:T(8,128)(2,1)}, bf16[3,3,128,256]{3,2,1,0:T(8,128)(2,1)}) fusion(bf16[3,3,256,256]{3,2,1,0:T(8,128)(2,1)S(1)} %copy-done.5), kind=kLoop, calls=%fused_computation.21 | loop fusion | bytes 2359296 | tf_op jit(solution)/shard_map/slice | solution.py:480
  25.1 2.1 %collective-permute-start = (bf16[4,6,64,128]{3,2,1,0:T(8,128)(2,1)}, bf16[4,6,64,128]{3,2,1,0:T(8,128)(2,1)S(1)}, u32[]{:S(2)}, u32[]{:S(2)}) collective-permute-start(bf16[4,6,64,128]{3,2,1,0:T(8,128)(2,1)} %get-tuple-element.37), channel_id=1, source_target_pairs={{0,1},{1,0},{2,3},{3,2},{4,5},{5,4},{6,7},{7,6},{8,9},{9,8},{10,11... | collective-permute-start | bytes 1179656 | tf_op jit(solution)/shard_map/ppermute | solution.py:468
  27.2 1.5 %collective-permute-start.2 = (bf16[4,6,64,128]{3,2,1,0:T(8,128)(2,1)}, bf16[4,6,64,128]{3,2,1,0:T(8,128)(2,1)S(1)}, u32[]{:S(2)}, u32[]{:S(2)}) collective-permute-start(bf16[4,6,64,128]{3,2,1,0:T(8,128)(2,1)} %get-tuple-element.37), channel_id=1, source_target_pairs={{0,15},{1,2},{2,1},{3,4},{4,3},{5,6},{6,5},{7,8},{8,7},{9,10},{10,... | collective-permute-start | bytes 1179656 | tf_op jit(solution)/shard_map/ppermute | solution.py:470
  28.8 1.6 %collective-permute-start.1 = (bf16[4,6,64,128]{3,2,1,0:T(8,128)(2,1)S(1)}, bf16[4,6,64,128]{3,2,1,0:T(8,128)(2,1)S(1)}, u32[]{:S(2)}, u32[]{:S(2)}) collective-permute-start(bf16[4,6,64,128]{3,2,1,0:T(8,128)(2,1)S(1)} %copy-done.1), channel_id=1, source_target_pairs={{0,14},{1,3},{2,0},{3,5},{4,2},{5,7},{6,4},{7,9},{8,6},{9,11},{10,... | collective-permute-start | bytes 1179656 | tf_op jit(solution)/shard_map/ppermute | solution.py:469
  30.5 12.7 %all-to-all-done.1 = bf16[16,2,3,64,128]{4,3,2,1,0:T(8,128)(2,1)} async-done(((bf16[16,2,3,64,128]{4,3,2,1,0:T(8,128)(2,1)}), bf16[16,2,3,64,128]{4,3,2,1,0:T(8,128)(2,1)}, u32[]{:S(2)}, u32[]{:S(2)}) %all-to-all-start.1) | async-done | bytes 1572896 | tf_op jit(solution)/shard_map/all_to_all | solution.py:473
  43.1 1.7 %pick.1 = (bf16[4,3,64,128]{3,2,1,0:T(8,128)(2,1)S(1)}, bf16[4,3,64,128]{3,2,1,0:T(8,128)(2,1)S(1)}) custom-call(s32[8]{0:T(128)} %get-tuple-element.38.slot_ref, bf16[32,3,64,128]{3,2,1,0:T(8,128)(2,1)} %bitcast.2.maps_ref), custom_call_target="tpu_custom_call" | custom-call | tf_op jit(solution)/shard_map/pick/pallas_call | solution.py:519
  44.8 4.2 %collective-permute-start.3 = (bf16[4,3,64,128]{3,2,1,0:T(8,128)(2,1)S(1)}, bf16[4,3,64,128]{3,2,1,0:T(8,128)(2,1)S(1)}, u32[]{:S(2)}, u32[]{:S(2)}) collective-permute-start(bf16[4,3,64,128]{3,2,1,0:T(8,128)(2,1)S(1)} %get-tuple-element.42), channel_id=1, source_target_pairs={{0,1},{1,0},{2,3},{3,2},{4,5},{5,4},{6,7},{7,6},{8,9},{9,8},{10,11... | collective-permute-start | bytes 589832 | tf_op jit(solution)/shard_map/ppermute | solution.py:545
  49.8 1.3 %copy.22.window_ref = bf16[256,1280]{1,0:T(8,128)(2,1)S(1)} copy(bf16[256,1280]{0,1:T(8,128)(2,1)} %bitcast.24) | data formatting | bytes 1310720 | tf_op jit(solution)/shard_map/reshape | solution.py:478
  51.1 0.0 copy-start.3
  51.1 0.1 copy.21
  51.3 0.1 copy.20
  51.4 0.6 broadcast_in_dim.26
  52.0 1.4 %concatenate.25 = bf16[128,64]{0,1:T(8,128)(2,1)S(1)} concatenate(bf16[128,12]{0,1:T(8,128)(2,1)S(1)} %get-tuple-element.66, bf16[128,4]{0,1:T(4,128)(2,1)} %broadcast_in_dim.26, bf16[128,12]{0,1:T(8,128)(2,1)S(1)} %get-tuple-element.67, bf16[128,4]{0,1:T(4,128)(2,1)} %broadcast_in_dim.26, bf16[128,16]{0,1:T(8,128)(2,1)S(1)} %broadcast_in_dim.28, ...), dimensions={1} | concatenate | bytes 32768 | tf_op jit(solution)/shard_map/concatenate | solution.py:491
  53.4 1.3 %pad_maximum_fusion.gate_ref = bf16[3,768,256]{2,1,0:T(8,128)(2,1)S(1)} fusion(bf16[3,384,256]{2,1,0:T(8,128)(2,1)} %bitcast.26, bf16[3,384,256]{2,1,0:T(8,128)(2,1)} %bitcast.25), kind=kLoop, calls=%fused_computation.2 | loop fusion | flops 2359296 | bytes 2359296 | tf_op jit(solution)/shard_map/concatenate | solution.py:479
  54.7 0.0 collective-permute-done.side_ref.came_ref
  54.7 0.0 collective-permute-done.1.ring_ref
  54.8 0.0 collective-permute-done.2.cross_ref
  54.8 1.8 %windows.1 = (bf16[4,64,128]{2,1,0:T(8,128)(2,1)S(1)}, bf16[4,64,128]{2,1,0:T(8,128)(2,1)S(1)}, bf16[4,64,128]{2,1,0:T(8,128)(2,1)S(1)}) custom-call(bf16[4,6,64,128]{3,2,1,0:T(8,128)(2,1)S(1)} %copy-done.1, bf16[4,6,64,128]{3,2,1,0:T(8,128)(2,1)S(1)} %collective-permute-done.side_ref.came_ref, bf16[4,6,64,128]{3,2,1,0:T(8,128)(2,1)S(1)} %collective-permute-done.1.ring_ref, ...), custom_call_target="tpu_custom_call" | custom-call | tf_op jit(solution)/shard_map/windows/pallas_call | solution.py:547
  56.6 1.7 %collective-permute-start.4 = (bf16[4,64,128]{2,1,0:T(8,128)(2,1)S(1)}, bf16[4,64,128]{2,1,0:T(8,128)(2,1)S(1)}, u32[]{:S(2)}, u32[]{:S(2)}) collective-permute-start(bf16[4,64,128]{2,1,0:T(8,128)(2,1)S(1)} %get-tuple-element.45.up_ref), channel_id=1, source_target_pairs={{0,2},{1,3},{2,4},{3,5},{4,6},{5,7},{6,8},{7,9},{8,10},{9,11},{10,... | collective-permute-start | bytes 196616 | tf_op jit(solution)/shard_map/ppermute | solution.py:561
  58.3 4.2 %collective-permute-start.5 = (bf16[4,64,128]{2,1,0:T(8,128)(2,1)S(1)}, bf16[4,64,128]{2,1,0:T(8,128)(2,1)S(1)}, u32[]{:S(2)}, u32[]{:S(2)}) collective-permute-start(bf16[4,64,128]{2,1,0:T(8,128)(2,1)S(1)} %get-tuple-element.43.down_ref), channel_id=1, source_target_pairs={{2,0},{3,1},{4,2},{5,3},{6,4},{7,5},{8,6},{9,7},{10,8},{11,9},{12,... | collective-permute-start | bytes 196616 | tf_op jit(solution)/shard_map/ppermute | solution.py:562
  62.5 0.1 pad_maximum_fusion.3.jac_ref
  62.6 2.1 %prepare.1 = (bf16[4,10,64,128]{3,2,1,0:T(8,128)(2,1)S(1)}, f32[4,512,256]{2,1,0:T(8,128)S(1)}) custom-call(bf16[4,6,64,128]{3,2,1,0:T(8,128)(2,1)S(1)} %copy-done.1, bf16[4,6,64,128]{3,2,1,0:T(8,128)(2,1)S(1)} %collective-permute-done.side_ref.came_ref, bf16[4,6,64,128]{3,2,1,0:T(8,128)(2,1)S(1)} %collective-permute-done.1.ring_ref, ...), custom_call_target="tpu_custom_call" | custom-call | tf_op jit(solution)/shard_map/prepare/pallas_call | solution.py:528
  64.7 0.0 collective-permute-done.5.below_ref
  64.7 5.5 %update.1 = (bf16[4,3,64,128]{3,2,1,0:T(8,128)(2,1)S(1)}, bf16[4,3,64,128]{3,2,1,0:T(8,128)(2,1)S(1)}, f32[16,16,128]{2,1,0:T(8,128)}) custom-call(s32[1]{0:T(128)S(6)} %copy.23.counts_ref, bf16[4,64,128]{2,1,0:T(8,128)(2,1)S(1)} %get-tuple-element.43.down_ref, bf16[4,64,128]{2,1,0:T(8,128)(2,1)S(1)} %get-tuple-element.44.mid_ref, ...), custom_call_target="tpu_custom_call" | custom-call | tf_op jit(solution)/shard_map/update/pallas_call | solution.py:563
  70.3 6.4 %all-to-all-start.2 = ((f32[16,16,128]{2,1,0:T(8,128)}), f32[16,16,128]{2,1,0:T(8,128)S(1)}, u32[]{:S(2)}, u32[]{:S(2)}) async-start(f32[16,16,128]{2,1,0:T(8,128)} %get-tuple-element.51), calls=%async_computation.2 | async-start | bytes 262144 | tf_op jit(solution)/shard_map/all_to_all | solution.py:595
  76.7 0.2 collective-permute-start.6
  76.9 9.0 %all-to-all-done.2.parts_ref = f32[16,16,128]{2,1,0:T(8,128)S(1)} async-done(((f32[16,16,128]{2,1,0:T(8,128)}), f32[16,16,128]{2,1,0:T(8,128)S(1)}, u32[]{:S(2)}, u32[]{:S(2)}) %all-to-all-start.2) | async-done | bytes 131104 | tf_op jit(solution)/shard_map/all_to_all | solution.py:595
  85.9 0.7 copy-done.7
  86.5 1.7 %slots.1 = (f32[8,16,128]{2,1,0:T(8,128)S(1)}, f32[16,16,128]{2,1,0:T(8,128)}) custom-call(s32[8]{0:T(128)} %get-tuple-element.38.slot_ref, f32[16,16,128]{2,1,0:T(8,128)} %copy-done.7), custom_call_target="tpu_custom_call" | custom-call | tf_op jit(solution)/shard_map/slots/pallas_call | solution.py:602
  88.3 3.5 %all-to-all-start.3 = ((f32[16,16,128]{2,1,0:T(8,128)}), f32[16,16,128]{2,1,0:T(8,128)S(1)}, u32[]{:S(2)}, u32[]{:S(2)}) async-start(f32[16,16,128]{2,1,0:T(8,128)} %get-tuple-element.53), calls=%async_computation.3 | async-start | bytes 262144 | tf_op jit(solution)/shard_map/all_to_all | solution.py:612
  91.8 1.9 %tables.1 = (bf16[144,640]{1,0:T(8,128)(2,1)}, bf16[640,144]{1,0:T(8,128)(2,1)}, bf16[24,640]{1,0:T(8,128)(2,1)}) custom-call(s32[8]{0:T(128)} %source_ref.4, s32[8]{0:T(128)} %bitcast.30, s32[8]{0:T(128)} %target_ref.3, s32[16,1,128]{2,1,0:T(1,128)} %copy-done.10), custom_call_target="tpu_custom_call" | custom-call | tf_op jit(solution)/shard_map/tables/pallas_call | solution.py:505
  93.7 0.8 maximum_select_fusion
  94.5 4.5 %all-to-all-done.3.came_ref = f32[16,16,128]{2,1,0:T(8,128)S(1)} async-done(((f32[16,16,128]{2,1,0:T(8,128)}), f32[16,16,128]{2,1,0:T(8,128)S(1)}, u32[]{:S(2)}, u32[]{:S(2)}) %all-to-all-start.3) | async-done | bytes 131104 | tf_op jit(solution)/shard_map/all_to_all | solution.py:612
  98.9 0.6 copy-done.8
  99.6 2.7 %place.1 = (f32[144,144]{1,0:T(8,128)}, f32[24,36]{1,0:T(8,128)}) custom-call(f32[8,16,128]{2,1,0:T(8,128)} %copy-done.2, f32[16,16,128]{2,1,0:T(8,128)} %copy-done.8, bf16[144,640]{1,0:T(8,128)(2,1)} %get-tuple-element.54.rows_ref, bf16[640,144]{1,0:T(8,128)(2,1)} %get-tuple-element.55.cols_ref, bf16[24,640]{1,0:T(8,128)(2,1)} %get-tuple-element.56.frames_ref, ...), custom_call_target="tpu_custom_call" | custom-call | tf_op jit(solution)/shard_map/place/pallas_call | solution.py:613
  (31 shorter events, 0.2 us)
Async XLA Ops:
  0.6 22.1 %copy-start = (bf16[49,128]{1,0:T(8,128)(2,1)S(1)}, bf16[49,128]{1,0:T(8,128)(2,1)}, u32[]{:S(2)}) copy-start(bf16[49,128]{1,0:T(8,128)(2,1)} %param.20) | copy-start | bytes 37636
  0.6 15.6 %copy-start.4 = (bf16[24,3,64,128]{3,2,1,0:T(8,128)(2,1)S(1)}, bf16[24,3,64,128]{3,2,1,0:T(8,128)(2,1)}, u32[]{:S(2)}) copy-start(bf16[24,3,64,128]{3,2,1,0:T(8,128)(2,1)} %features_ref.1) | copy-start | bytes 3538948
  2.1 13.9 %all-to-all-start = ((s32[16,1,128]{2,1,0:T(1,128)}), s32[16,1,128]{2,1,0:T(1,128)S(1)}, u32[]{:S(2)}, u32[]{:S(2)}) async-start(s32[16,1,128]{2,1,0:T(1,128)} %get-tuple-element.32), calls=%async_computation | async-start | bytes 16384 | tf_op jit(solution)/shard_map/all_to_all | solution.py:457
  16.1 2.0 %copy-start.10 = (s32[16,1,128]{2,1,0:T(1,128)}, s32[16,1,128]{2,1,0:T(1,128)S(1)}, u32[]{:S(2)}) copy-start(s32[16,1,128]{2,1,0:T(1,128)S(1)} %all-to-all-done.got_ref) | copy-start | bytes 24580
  18.1 4.6 %copy-start.11 = (bf16[128,24]{0,1:T(8,128)(2,1)S(1)}, bf16[128,24]{0,1:T(8,128)(2,1)}, u32[]{:S(2)}) copy-start(bf16[128,24]{0,1:T(8,128)(2,1)} %param.23) | copy-start | bytes 18436
  18.1 4.6 %copy-start.6 = (bf16[3,3,256,128]{3,2,1,0:T(8,128)(2,1)S(1)}, bf16[3,3,256,128]{3,2,1,0:T(8,128)(2,1)}, u32[]{:S(2)}) copy-start(bf16[3,3,256,128]{3,2,1,0:T(8,128)(2,1)} %param.22) | copy-start | bytes 1769476
  18.1 4.7 %copy-start.9 = (bf16[256,10,49]{0,2,1:T(8,128)(2,1)S(1)}, bf16[256,10,49]{0,2,1:T(8,128)(2,1)}, u32[]{:S(2)}) copy-start(bf16[256,10,49]{0,2,1:T(8,128)(2,1)} %constant.27.clone) | copy-start | bytes 752644
  18.1 25.0 %all-to-all-start.1 = ((bf16[16,2,3,64,128]{4,3,2,1,0:T(8,128)(2,1)}), bf16[16,2,3,64,128]{4,3,2,1,0:T(8,128)(2,1)}, u32[]{:S(2)}, u32[]{:S(2)}) async-start(bf16[16,2,3,64,128]{4,3,2,1,0:T(8,128)(2,1)} %bitcast.1), calls=%async_computation.1 | async-start | bytes 3145728 | tf_op jit(solution)/shard_map/all_to_all | solution.py:473
  22.7 1.3 %copy-start.5 = (bf16[3,3,256,256]{3,2,1,0:T(8,128)(2,1)S(1)}, bf16[3,3,256,256]{3,2,1,0:T(8,128)(2,1)}, u32[]{:S(2)}) copy-start(bf16[3,3,256,256]{3,2,1,0:T(8,128)(2,1)} %param.21) | copy-start | bytes 3538948
  22.8 6.0 %copy-start.1 = (bf16[4,6,64,128]{3,2,1,0:T(8,128)(2,1)S(1)}, bf16[4,6,64,128]{3,2,1,0:T(8,128)(2,1)}, u32[]{:S(2)}) copy-start(bf16[4,6,64,128]{3,2,1,0:T(8,128)(2,1)} %get-tuple-element.46.keep_ref) | copy-start | bytes 1179652
  22.8 7.6 %copy-start.12 = (bf16[128,2]{0,1:T(2,128)(2,1)S(1)}, bf16[128,2]{0,1:T(2,128)(2,1)}, u32[]{:S(2)}) copy-start(bf16[128,2]{0,1:T(2,128)(2,1)} %param.24) | copy-start | bytes 1540
  25.1 29.6 %collective-permute-start = (bf16[4,6,64,128]{3,2,1,0:T(8,128)(2,1)}, bf16[4,6,64,128]{3,2,1,0:T(8,128)(2,1)S(1)}, u32[]{:S(2)}, u32[]{:S(2)}) collective-permute-start(bf16[4,6,64,128]{3,2,1,0:T(8,128)(2,1)} %get-tuple-element.37), channel_id=1, source_target_pairs={{0,1},{1,0},{2,3},{3,2},{4,5},{5,4},{6,7},{7,6},{8,9},{9,8},{10,11... | collective-permute-start | bytes 1179656 | tf_op jit(solution)/shard_map/ppermute | solution.py:468
  27.2 27.5 %collective-permute-start.2 = (bf16[4,6,64,128]{3,2,1,0:T(8,128)(2,1)}, bf16[4,6,64,128]{3,2,1,0:T(8,128)(2,1)S(1)}, u32[]{:S(2)}, u32[]{:S(2)}) collective-permute-start(bf16[4,6,64,128]{3,2,1,0:T(8,128)(2,1)} %get-tuple-element.37), channel_id=1, source_target_pairs={{0,15},{1,2},{2,1},{3,4},{4,3},{5,6},{6,5},{7,8},{8,7},{9,10},{10,... | collective-permute-start | bytes 1179656 | tf_op jit(solution)/shard_map/ppermute | solution.py:470
  28.8 26.0 %collective-permute-start.1 = (bf16[4,6,64,128]{3,2,1,0:T(8,128)(2,1)S(1)}, bf16[4,6,64,128]{3,2,1,0:T(8,128)(2,1)S(1)}, u32[]{:S(2)}, u32[]{:S(2)}) collective-permute-start(bf16[4,6,64,128]{3,2,1,0:T(8,128)(2,1)S(1)} %copy-done.1), channel_id=1, source_target_pairs={{0,14},{1,3},{2,0},{3,5},{4,2},{5,7},{6,4},{7,9},{8,6},{9,11},{10,... | collective-permute-start | bytes 1179656 | tf_op jit(solution)/shard_map/ppermute | solution.py:469
  44.8 9.9 %collective-permute-start.3 = (bf16[4,3,64,128]{3,2,1,0:T(8,128)(2,1)S(1)}, bf16[4,3,64,128]{3,2,1,0:T(8,128)(2,1)S(1)}, u32[]{:S(2)}, u32[]{:S(2)}) collective-permute-start(bf16[4,3,64,128]{3,2,1,0:T(8,128)(2,1)S(1)} %get-tuple-element.42), channel_id=1, source_target_pairs={{0,1},{1,0},{2,3},{3,2},{4,5},{5,4},{6,7},{7,6},{8,9},{9,8},{10,11... | collective-permute-start | bytes 589832 | tf_op jit(solution)/shard_map/ppermute | solution.py:545
  51.1 3.7 %copy-start.3 = (bf16[128,128]{1,0:T(8,128)(2,1)S(1)}, bf16[128,128]{1,0:T(8,128)(2,1)}, u32[]{:S(2)}) copy-start(bf16[128,128]{1,0:T(8,128)(2,1)} %constant.29.clone.turn_ref) | copy-start | bytes 98308
  56.6 8.1 %collective-permute-start.4 = (bf16[4,64,128]{2,1,0:T(8,128)(2,1)S(1)}, bf16[4,64,128]{2,1,0:T(8,128)(2,1)S(1)}, u32[]{:S(2)}, u32[]{:S(2)}) collective-permute-start(bf16[4,64,128]{2,1,0:T(8,128)(2,1)S(1)} %get-tuple-element.45.up_ref), channel_id=1, source_target_pairs={{0,2},{1,3},{2,4},{3,5},{4,6},{5,7},{6,8},{7,9},{8,10},{9,11},{10,... | collective-permute-start | bytes 196616 | tf_op jit(solution)/shard_map/ppermute | solution.py:561
  58.3 6.4 %collective-permute-start.5 = (bf16[4,64,128]{2,1,0:T(8,128)(2,1)S(1)}, bf16[4,64,128]{2,1,0:T(8,128)(2,1)S(1)}, u32[]{:S(2)}, u32[]{:S(2)}) collective-permute-start(bf16[4,64,128]{2,1,0:T(8,128)(2,1)S(1)} %get-tuple-element.43.down_ref), channel_id=1, source_target_pairs={{2,0},{3,1},{4,2},{5,3},{6,4},{7,5},{8,6},{9,7},{10,8},{11,9},{12,... | collective-permute-start | bytes 196616 | tf_op jit(solution)/shard_map/ppermute | solution.py:562
  70.3 15.6 %all-to-all-start.2 = ((f32[16,16,128]{2,1,0:T(8,128)}), f32[16,16,128]{2,1,0:T(8,128)S(1)}, u32[]{:S(2)}, u32[]{:S(2)}) async-start(f32[16,16,128]{2,1,0:T(8,128)} %get-tuple-element.51), calls=%async_computation.2 | async-start | bytes 262144 | tf_op jit(solution)/shard_map/all_to_all | solution.py:595
  76.7 17.0 %collective-permute-start.6 = (bf16[4,3,64,128]{3,2,1,0:T(8,128)(2,1)S(1)}, bf16[4,3,64,128]{3,2,1,0:T(8,128)(2,1)S(1)}, u32[]{:S(2)}, u32[]{:S(2)}) collective-permute-start(bf16[4,3,64,128]{3,2,1,0:T(8,128)(2,1)S(1)} %get-tuple-element.50), channel_id=1, source_target_pairs={{0,1},{1,0},{2,3},{3,2},{4,5},{5,4},{6,7},{7,6},{8,9},{9,8},{10,11... | collective-permute-start | bytes 589832 | tf_op jit(solution)/shard_map/ppermute | solution.py:596
  85.9 0.7 copy-start.7
  88.3 10.7 %copy-start.2 = (f32[8,16,128]{2,1,0:T(8,128)}, f32[8,16,128]{2,1,0:T(8,128)S(1)}, u32[]{:S(2)}) copy-start(f32[8,16,128]{2,1,0:T(8,128)S(1)} %get-tuple-element.52.own_ref) | copy-start | bytes 196612
  88.3 10.7 %all-to-all-start.3 = ((f32[16,16,128]{2,1,0:T(8,128)}), f32[16,16,128]{2,1,0:T(8,128)S(1)}, u32[]{:S(2)}, u32[]{:S(2)}) async-start(f32[16,16,128]{2,1,0:T(8,128)} %get-tuple-element.53), calls=%async_computation.3 | async-start | bytes 262144 | tf_op jit(solution)/shard_map/all_to_all | solution.py:612
  98.9 0.7 copy-start.8
